TPU v7x, 32 devices: a whole 2x2x4 slice. The times are simulated.
32 devices in a mesh: shard: 2 (over core), rep: 16 (over z, y, x).
Axes of the slice: x: 2, y: 2, z: 4, core: 2. Of those that a mesh axis runs over, the one named last changes fastest.
Arguments:
- noisy_patches: bfloat16 [128, 4096], P(('shard', 'rep')), may hold values from -6 to 6
- targets: float32 [128, 4096], P(('shard', 'rep')), may hold values from -6 to 6
- timesteps: int32 [128], P(('shard', 'rep')), may hold values from 0 to 999
- labels: int32 [128], P(('shard', 'rep')), may hold values from 0 to 999
- master_big: float32 [768, 16384], P(None, 'shard'), may hold values from -0.57735027 to 0.57735027
- moment_big: float32 [768, 16384], P(None, 'shard'), may hold values from -0.00021362305 to 0.00021362305
- error_big: float32 [16, 768, 16384], P('rep', None, 'shard'), may hold values from -5.340576e-05 to 5.340576e-05
- factor_right: float32 [16384, 8], P('shard'), may hold values from -6 to 6
- master_small: float32 [768, 1032], replicated, may hold values from -4 to 4
- moment_small: float32 [768, 1032], replicated, may hold values from -0.0017089844 to 0.0017089844
- biases: float32 [14608], replicated, may hold values from -1.25 to 1.25
- moment_bias: float32 [14608], replicated, may hold values from -0.0017089844 to 0.0017089844
- step_rates: float32 [2], replicated, may hold values from 362.03867 to 724.07733
Outputs:
- total_loss: float32 [], replicated
- new_master_big: float32 [768, 16384], P(None, 'shard')
- new_moment_big: float32 [768, 16384], P(None, 'shard')
- new_error_big: float32 [16, 768, 16384], P('rep', None, 'shard')
- new_factor_right: float32 [16384, 8], P('shard')
- new_master_small: float32 [768, 1032], replicated
- new_moment_small: float32 [768, 1032], replicated
- new_biases: float32 [14608], replicated
- new_moment_bias: float32 [14608], replicated
All inputs are finite; a program needn't handle non-finite values.
Results may differ from a plain program's by a relative error of at most 0.011.
The roundings to bfloat16 on the way count: a program that leaves them out, or rounds other values in their place, can miss the bound.
Values may be sent and summed in bfloat16 or wider, within the bound.
A program may use at most 384 MiB of HBM per device.

v0:
```python
import math

import jax
import jax.numpy as jnp
from jax import lax
from jax.sharding import PartitionSpec as P

D = 768
HEADS = 12
HEAD_DIM = 64
FF = 3072
GRID = 16
FREQ = 256
NCLASS = 1000
P_DIM = 16
SEQ = 256


highest = lax.Precision.HIGHEST
epsilon = 1e-06
tiny_value = 1e-30
momentum_decay = 0.9
half_type = jnp.bfloat16


def multiply(left_side, right_side):
    return jnp.dot(left_side, right_side, preferred_element_type=jnp.float32)


def multiply_trans(left_side, right_side):
    return lax.dot_general(
        left_side, right_side, (((1,), (1,)), ((), ())), preferred_element_type=jnp.float32
    )


def outer_sum(left_side, right_side):
    return lax.dot_general(
        left_side, right_side, (((0,), (0,)), ((), ())), preferred_element_type=jnp.float32
    )


def exact_outer(left_side, right_side):
    return lax.dot_general(
        left_side,
        right_side,
        (((0,), (0,)), ((), ())),
        precision=highest,
        preferred_element_type=jnp.float32,
    )


def normalize(values):
    center = values - jnp.mean(values, axis=-1, keepdims=True)
    return center * lax.rsqrt(jnp.mean(center * center, axis=-1, keepdims=True) + epsilon)


def gelu_tanh(values):
    return jax.nn.gelu(values, approximate=True)


def slope(function, values, grad):
    unused, pullback = jax.vjp(function, values)
    return pullback(grad)[0]


def timestep_features(steps):
    half_count = FREQ // 2
    freqs = jnp.exp(-math.log(10000.0) * jnp.arange(half_count, dtype=jnp.float32) / half_count)
    angles = steps.astype(jnp.float32)[:, None] * freqs[None, :]
    return jnp.concatenate([jnp.cos(angles), jnp.sin(angles)], axis=1)


def position_table():
    quarter = D // 4
    omega = 1.0 / 10000.0 ** (jnp.arange(quarter, dtype=jnp.float32) / quarter)
    cells = jnp.arange(SEQ, dtype=jnp.int32)
    across = (cells % GRID).astype(jnp.float32)[:, None] * omega[None, :]
    downward = (cells // GRID).astype(jnp.float32)[:, None] * omega[None, :]
    return jnp.concatenate(
        [jnp.sin(across), jnp.cos(across), jnp.sin(downward), jnp.cos(downward)], axis=1
    )


def split_at(matrix, edges):
    return tuple((matrix[..., edges[place] : edges[place + 1]] for place in range(len(edges) - 1)))


def split_big(matrix):
    return split_at(
        matrix,
        [
            0,
            3 * D,
            4 * D,
            4 * D + FF,
            4 * D + 2 * FF,
            10 * D + 2 * FF,
            12 * D + 2 * FF,
            13 * D + 2 * FF,
            13 * D + 2 * FF + FREQ,
        ],
    )


def split_small(matrix):
    return split_at(matrix, [0, P_DIM, P_DIM + NCLASS, 2 * P_DIM + NCLASS])


def split_bias(vector):
    return split_at(
        vector,
        [
            0,
            D,
            2 * D,
            3 * D,
            3 * D + FF,
            4 * D + FF,
            10 * D + FF,
            12 * D + FF,
            13 * D + FF,
            14 * D + FF,
            15 * D + FF,
            15 * D + FF + P_DIM,
        ],
    )


def orthonormal(factor):
    columns = []
    for place in range(factor.shape[-1]):
        vector = factor[..., place]
        for earlier in columns:
            vector = vector - jnp.sum(earlier * vector, axis=-1, keepdims=True) * earlier
        vector = vector * lax.rsqrt(jnp.sum(vector * vector, axis=-1, keepdims=True) + tiny_value)
        columns.append(vector)
    return jnp.stack(columns, axis=-1)


def column_sums(grad):
    return jnp.sum(grad.astype(jnp.float32), axis=0)


def forward(gathered, master_small, biases, noisy_patches, timesteps, labels):
    (
        attend_weight,
        output_weight,
        up_weight,
        down_weight,
        modulate_weight,
        final_weight,
        embed_second,
        embed_first,
    ) = split_big(gathered)
    patch_weight, unused_table, head_weight = split_small(master_small.astype(half_type))
    class_table = split_small(master_small)[1]
    (
        query_bias,
        value_bias,
        output_bias,
        up_bias,
        down_bias,
        modulate_bias,
        final_bias,
        second_bias,
        first_bias,
        patch_bias,
        head_bias,
    ) = split_bias(biases)
    images = noisy_patches.shape[0]
    tokens = images * SEQ
    frequency = timestep_features(timesteps).astype(half_type)
    embed_pre = multiply_trans(frequency, embed_first) + first_bias
    embed_hidden = jax.nn.silu(embed_pre).astype(half_type)
    time_embed = multiply(embed_hidden, embed_second) + second_bias
    chosen = (labels[:, None] == jnp.arange(NCLASS, dtype=jnp.int32)[None, :]).astype(jnp.float32)
    condition = time_embed + lax.dot_general(
        chosen,
        class_table,
        (((1,), (1,)), ((), ())),
        precision=highest,
        preferred_element_type=jnp.float32,
    )
    active = jax.nn.silu(condition).astype(half_type)
    modulation = multiply(active, modulate_weight) + modulate_bias
    final_mod = multiply(active, final_weight) + final_bias
    patches = noisy_patches.reshape(tokens, P_DIM)
    stream_in = (multiply_trans(patches, patch_weight) + patch_bias).reshape(
        images, SEQ, D
    ) + position_table()[None]
    shift_attn, scale_attn, gate_attn, shift_mlp, scale_mlp, gate_mlp = jnp.split(
        modulation[:, None, :], 6, axis=2
    )
    shift_final, scale_final = jnp.split(final_mod[:, None, :], 2, axis=2)
    attn_in = (
        (normalize(stream_in) * (1.0 + scale_attn) + shift_attn)
        .astype(half_type)
        .reshape(tokens, D)
    )
    qkv_bias = jnp.concatenate([query_bias, jnp.zeros_like(query_bias), value_bias])
    projected = (multiply(attn_in, attend_weight) + qkv_bias).astype(half_type)
    queries, key_rows, value_rows = [
        piece.reshape(images, SEQ, HEADS, HEAD_DIM) for piece in jnp.split(projected, 3, axis=1)
    ]
    scores = jnp.einsum(
        "nqhd,nkhd->nhqk", queries, key_rows, preferred_element_type=jnp.float32
    ) / math.sqrt(HEAD_DIM)
    highest_score = jnp.max(scores, axis=-1, keepdims=True)
    logsum = highest_score + jnp.log(
        jnp.sum(jnp.exp(scores - highest_score), axis=-1, keepdims=True)
    )
    probs_low = jnp.exp(scores - logsum).astype(half_type)
    mixed_rows = (
        jnp.einsum("nhqk,nkhd->nqhd", probs_low, value_rows, preferred_element_type=jnp.float32)
        .astype(half_type)
        .reshape(tokens, D)
    )
    attended = (multiply(mixed_rows, output_weight) + output_bias).reshape(images, SEQ, D)
    stream_mid = stream_in + gate_attn * attended
    mlp_in = (
        (normalize(stream_mid) * (1.0 + scale_mlp) + shift_mlp).astype(half_type).reshape(tokens, D)
    )
    hidden_pre = multiply(mlp_in, up_weight) + up_bias
    hidden = gelu_tanh(hidden_pre).astype(half_type)
    mlp_out = (multiply_trans(hidden, down_weight) + down_bias).reshape(images, SEQ, D)
    stream_out = stream_mid + gate_mlp * mlp_out
    final_in = (
        (normalize(stream_out) * (1.0 + scale_final) + shift_final)
        .astype(half_type)
        .reshape(tokens, D)
    )
    output = multiply(final_in, head_weight) + head_bias
    kept = dict(
        frequency=frequency,
        embed_pre=embed_pre,
        embed_hidden=embed_hidden,
        chosen=chosen,
        condition=condition,
        active=active,
        modulation=modulation,
        final_mod=final_mod,
        patches=patches,
        stream_in=stream_in,
        attn_in=attn_in,
        queries=queries,
        key_rows=key_rows,
        value_rows=value_rows,
        logsum=logsum,
        mixed_rows=mixed_rows,
        attended=attended,
        stream_mid=stream_mid,
        mlp_in=mlp_in,
        hidden_pre=hidden_pre,
        hidden=hidden,
        mlp_out=mlp_out,
        stream_out=stream_out,
        final_in=final_in,
    )
    return (output, kept)


def backward(gathered, master_small, kept, grad_output):
    (
        attend_weight,
        output_weight,
        up_weight,
        down_weight,
        modulate_weight,
        final_weight,
        embed_second,
        embed_first,
    ) = split_big(gathered)
    patch_weight, unused_table, head_weight = split_small(master_small.astype(half_type))
    images = kept["stream_in"].shape[0]
    tokens = images * SEQ
    shift_attn, scale_attn, gate_attn, shift_mlp, scale_mlp, gate_mlp = jnp.split(
        kept["modulation"][:, None, :], 6, axis=2
    )
    shift_final, scale_final = jnp.split(kept["final_mod"][:, None, :], 2, axis=2)
    grad_out = grad_output.astype(half_type)
    grad_head = outer_sum(kept["final_in"], grad_out)
    bias_head = column_sums(grad_out)
    grad_final = multiply_trans(grad_out, head_weight).reshape(images, SEQ, D)
    grad_shift_final = jnp.sum(grad_final, axis=1)
    grad_scale_final = jnp.sum(grad_final * normalize(kept["stream_out"]), axis=1)
    grad_stream = slope(normalize, kept["stream_out"], grad_final * (1.0 + scale_final))
    grad_gate_mlp = jnp.sum(grad_stream * kept["mlp_out"], axis=1)
    grad_mlp = (grad_stream * gate_mlp).reshape(tokens, D).astype(half_type)
    bias_down = column_sums(grad_mlp)
    grad_down = outer_sum(grad_mlp, kept["hidden"])
    grad_hidden = multiply(grad_mlp, down_weight)
    grad_pre = slope(gelu_tanh, kept["hidden_pre"], grad_hidden).astype(half_type)
    bias_up = column_sums(grad_pre)
    grad_up = outer_sum(kept["mlp_in"], grad_pre)
    grad_mlp_in = multiply_trans(grad_pre, up_weight).reshape(images, SEQ, D)
    grad_shift_mlp = jnp.sum(grad_mlp_in, axis=1)
    grad_scale_mlp = jnp.sum(grad_mlp_in * normalize(kept["stream_mid"]), axis=1)
    grad_stream = grad_stream + slope(
        normalize, kept["stream_mid"], grad_mlp_in * (1.0 + scale_mlp)
    )
    grad_gate_attn = jnp.sum(grad_stream * kept["attended"], axis=1)
    grad_attn = (grad_stream * gate_attn).reshape(tokens, D).astype(half_type)
    bias_output = column_sums(grad_attn)
    grad_output_weight = outer_sum(kept["mixed_rows"], grad_attn)
    grad_mixed = (
        multiply_trans(grad_attn, output_weight)
        .astype(half_type)
        .reshape(images, SEQ, HEADS, HEAD_DIM)
    )
    inverse_root = 1.0 / math.sqrt(HEAD_DIM)
    scores = (
        jnp.einsum(
            "nqhd,nkhd->nhqk", kept["queries"], kept["key_rows"], preferred_element_type=jnp.float32
        )
        * inverse_root
    )
    probs = jnp.exp(scores - kept["logsum"])
    grad_values = jnp.einsum(
        "nhqk,nqhd->nkhd", probs.astype(half_type), grad_mixed, preferred_element_type=jnp.float32
    )
    grad_probs = jnp.einsum(
        "nqhd,nkhd->nhqk", grad_mixed, kept["value_rows"], preferred_element_type=jnp.float32
    )
    grad_scores = (
        probs * (grad_probs - jnp.sum(probs * grad_probs, axis=-1, keepdims=True))
    ).astype(half_type)
    grad_queries = (
        jnp.einsum(
            "nhqk,nkhd->nqhd", grad_scores, kept["key_rows"], preferred_element_type=jnp.float32
        )
        * inverse_root
    )
    grad_keys = (
        jnp.einsum(
            "nhqk,nqhd->nkhd", grad_scores, kept["queries"], preferred_element_type=jnp.float32
        )
        * inverse_root
    )
    grad_qkv = jnp.concatenate(
        [
            grad_queries.reshape(tokens, D),
            grad_keys.reshape(tokens, D),
            grad_values.reshape(tokens, D),
        ],
        axis=1,
    ).astype(half_type)
    bias_query = column_sums(grad_qkv[:, :D])
    bias_value = column_sums(grad_qkv[:, 2 * D :])
    grad_attend = outer_sum(kept["attn_in"], grad_qkv)
    grad_attn_in = multiply_trans(grad_qkv, attend_weight).reshape(images, SEQ, D)
    grad_shift_attn = jnp.sum(grad_attn_in, axis=1)
    grad_scale_attn = jnp.sum(grad_attn_in * normalize(kept["stream_in"]), axis=1)
    grad_stream = grad_stream + slope(
        normalize, kept["stream_in"], grad_attn_in * (1.0 + scale_attn)
    )
    grad_start = grad_stream.reshape(tokens, D).astype(half_type)
    bias_patch = column_sums(grad_start)
    grad_patch = outer_sum(grad_start, kept["patches"])
    grad_mod = jnp.concatenate(
        [
            grad_shift_attn,
            grad_scale_attn,
            grad_gate_attn,
            grad_shift_mlp,
            grad_scale_mlp,
            grad_gate_mlp,
        ],
        axis=1,
    ).astype(half_type)
    grad_fmod = jnp.concatenate([grad_shift_final, grad_scale_final], axis=1).astype(half_type)
    bias_modulate = column_sums(grad_mod)
    bias_final = column_sums(grad_fmod)
    grad_modulate = outer_sum(kept["active"], grad_mod)
    grad_final_weight = outer_sum(kept["active"], grad_fmod)
    grad_active = multiply_trans(grad_mod, modulate_weight) + multiply_trans(
        grad_fmod, final_weight
    )
    grad_condition = slope(jax.nn.silu, kept["condition"], grad_active)
    grad_table = jnp.einsum("nd,nc->dc", grad_condition, kept["chosen"], precision=highest)
    grad_embed = grad_condition.astype(half_type)
    bias_second = column_sums(grad_embed)
    grad_second = outer_sum(kept["embed_hidden"], grad_embed)
    grad_embed_hidden = multiply_trans(grad_embed, embed_second)
    grad_embed_pre = slope(jax.nn.silu, kept["embed_pre"], grad_embed_hidden).astype(half_type)
    bias_first = column_sums(grad_embed_pre)
    grad_first = outer_sum(grad_embed_pre, kept["frequency"])
    grad_big = jnp.concatenate(
        [
            grad_attend,
            grad_output_weight,
            grad_up,
            grad_down,
            grad_modulate,
            grad_final_weight,
            grad_second,
            grad_first,
        ],
        axis=1,
    )
    grad_small = jnp.concatenate([grad_patch, grad_table, grad_head], axis=1)
    grad_bias = jnp.concatenate(
        [
            bias_query,
            bias_value,
            bias_output,
            bias_up,
            bias_down,
            bias_modulate,
            bias_final,
            bias_second,
            bias_first,
            bias_patch,
            bias_head,
        ]
    )
    return (grad_big, grad_small, grad_bias)


def on_device(
    noisy_patches,
    targets,
    timesteps,
    labels,
    master_big,
    moment_big,
    error_big,
    factor_right,
    master_small,
    moment_small,
    biases,
    moment_bias,
    step_rates,
):
    shards = lax.axis_size("shard")
    replicas = lax.axis_size("rep")
    gathered = lax.all_gather(master_big.astype(half_type), "shard", axis=1, tiled=True)
    output, kept = forward(gathered, master_small, biases, noisy_patches, timesteps, labels)
    entries = noisy_patches.shape[0] * shards * replicas * SEQ * P_DIM
    error = output - targets.reshape(output.shape)
    loss_part = jnp.sum(error * error) / entries
    grad_output = 2.0 * error / entries
    gathered = lax.all_gather(master_big.astype(half_type), "shard", axis=1, tiled=True)
    grad_big, grad_small, grad_bias = backward(gathered, master_small, kept, grad_output)
    owned = lax.psum_scatter(
        grad_big.astype(jnp.bfloat16), "shard", scatter_dimension=1, tiled=True
    ).astype(jnp.float32)
    matrices = owned + error_big[0]
    left_part = jnp.dot(
        matrices, factor_right, precision=highest, preferred_element_type=jnp.float32
    )
    small_sum, bias_sum, total_loss = lax.psum((grad_small, grad_bias, loss_part), ("shard", "rep"))
    left_sum = lax.psum(left_part, "rep")
    basis = orthonormal(left_sum)
    right_sum = lax.psum(exact_outer(matrices, basis).astype(jnp.bfloat16), "rep").astype(
        jnp.float32
    )
    approx = lax.dot_general(
        basis,
        right_sum,
        (((1,), (1,)), ((), ())),
        precision=highest,
        preferred_element_type=jnp.float32,
    )
    new_error = (matrices - approx / replicas)[None]
    new_moment = momentum_decay * moment_big + approx
    new_master = master_big - step_rates[0] * new_moment
    new_moment_small = momentum_decay * moment_small + small_sum
    new_master_small = master_small - step_rates[1] * new_moment_small
    new_moment_bias = momentum_decay * moment_bias + bias_sum
    new_biases = biases - step_rates[1] * new_moment_bias
    return (
        total_loss,
        new_master,
        new_moment,
        new_error,
        right_sum,
        new_master_small,
        new_moment_small,
        new_biases,
        new_moment_bias,
    )


def solution(mesh):
    in_specs = (
        P(("shard", "rep"), None),
        P(("shard", "rep"), None),
        P(("shard", "rep")),
        P(("shard", "rep")),
        P(None, "shard"),
        P(None, "shard"),
        P("rep", None, "shard"),
        P("shard", None),
        P(),
        P(),
        P(),
        P(),
        P(),
    )
    out_specs = (
        P(),
        P(None, "shard"),
        P(None, "shard"),
        P("rep", None, "shard"),
        P("shard", None),
        P(),
        P(),
        P(),
        P(),
    )
    return jax.shard_map(
        on_device, mesh=mesh, in_specs=in_specs, out_specs=out_specs, check_vma=False
    )
```

profile of v0, /device:TPU:0, one launch (start us, length us, event | category | flops | bytes accessed | tf_op | source)
XLA Modules:
  0.0 761.1 jit_solution(13391399123688118993)
XLA Ops:
  7.2 13.2 %convert_element_type.142 = bf16[768,8192]{1,0:T(8,128)(2,1)} convert(f32[768,8192]{1,0:T(8,128)} %param.17) | non-fusion elementwise | flops 6291456 | bytes 37748736 | tf_op jit(solution)/shard_map/convert_element_type | solution.py:436
  35.0 28.7 %all-gather.2.cloned.1.call-done = bf16[768,16384]{1,0:T(8,128)(2,1)} async-done(((bf16[768,8192]{1,0:T(8,128)(2,1)}), bf16[768,16384]{1,0:T(8,128)(2,1)}) %all-gather.2.cloned.1.call-update) | async-done | bytes 25165840 | tf_op jit(solution)/shard_map/all_gather | solution.py:436
  66.4 3.0 fusion.85
  71.5 4.1 fusion.19
  77.2 6.6 add_convert_fusion
  83.8 2.3 fusion.144
  86.1 2.6 copy.62
  88.7 3.9 reshape.459
  92.5 2.6 copy.63
  95.1 3.9 reshape.460
  99.0 2.6 copy.61
  101.5 3.9 reshape.458
  105.4 3.7 multiply_reduce_fusion.1
  109.2 2.7 exponential_reduce_fusion
  113.9 2.6 fusion.69
  118.2 6.3 fusion.142
  125.1 2.5 multiply_reduce_fusion.7
  129.0 10.9 %fusion.31 = f32[1024,3072]{1,0:T(8,128)} fusion(bf16[1024,768]{1,0:T(8,128)(2,1)S(1)} %fusion.48, bf16[768,16384]{1,0:T(8,128)(2,1)} %all-gather.2.cloned.1.call-done), kind=kOutput, calls=%fused_computation.60 | convolution fusion | flops 4831838208 | bytes 18874368 | tf_op jit(solution)/shard_map/dot_general | solution.py:27
  139.9 14.3 %fusion.140 = (f32[1024]{0:T(1024)S(1)}, f32[1024,768]{1,0:T(8,128)}, f32[1024,768]{1,0:T(8,128)}) fusion(f32[1024,768]{1,0:T(8,128)S(1)} %copy-done.2, f32[4,768]{1,0:T(4,128)S(1)} %copy-done.56, f32[768]{0:T(1024)S(1)} %copy-done.87, bf16[768,16384]{1,0:T(8,128)(2,1)} %all-gather.2.cloned.1.call-done, f32[1024,3072]{1,0:T(8,128)} %fusion.31, ...), kind=kOutput, calls=%fused_computation.350 | convolution fusion | flops 4866440192 | bytes 26770432 | tf_op jit(solution)/shard_map/dot_general | solution.py:31
  154.8 2.5 multiply_reduce_fusion.6
  161.2 3.2 multiply_reduce_fusion.5
  166.9 4.6 fusion.139
  173.3 2.9 convert_reduce_fusion.2
  176.3 17.3 %convert_reduce_fusion = (f32[3072]{0:T(1024)}, bf16[1024,3072]{1,0:T(8,128)(2,1)S(1)}) fusion(f32[1024,3072]{1,0:T(8,128)} %fusion.31, f32[3072]{0:T(1024)S(1)} %copy-done.77, bf16[1024,768]{1,0:T(8,128)(2,1)S(1)} %get-tuple-element.94, bf16[768,16384]{1,0:T(8,128)(2,1)} %all-gather.2.cloned.1.call-done), kind=kOutput, calls=%fused_computation.13 | convolution fusion | flops 4904186880 | bytes 25190400 | tf_op jit(solution)/shard_map/dot_general | solution.py:27
  193.6 11.6 %multiply_reduce_fusion.4 = (f32[1024]{0:T(1024)S(1)}, f32[1024,768]{1,0:T(8,128)}) fusion(f32[1024,768]{1,0:T(8,128)S(1)} %copy-done.3, f32[4,768]{1,0:T(4,128)S(1)} %copy-done.52, f32[1024]{0:T(1024)S(1)} %copy-done.60, bf16[1024,3072]{1,0:T(8,128)(2,1)S(1)} %get-tuple-element.157, bf16[768,16384]{1,0:T(8,128)(2,1)} %all-gather.2.cloned.1.call-done), kind=kOutput, calls=%fused_computation.105 | convolution fusion | flops 4834982912 | bytes 17321984 | tf_op jit(solution)/shard_map/dot_general | solution.py:31
  207.6 4.6 fusion.138
  214.1 4.2 convert_reduce_fusion.3
  218.3 2.5 convolution_convert_fusion.8
  220.8 3.8 convolution_convert_fusion.7
  224.6 2.6 copy.70
  227.2 3.9 reshape.463
  231.1 8.8 %fusion.70 = bf16[4,256,12,64]{1,3,2,0:T(8,128)(2,1)} fusion(bf16[4,256,12,64]{1,0,3,2:T(4,128)(2,1)} %reshape.463, f32[4,12,256,256]{2,3,1,0:T(8,128)} %copy-done.1, f32[4,12,256]{2,1,0:T(8,128)S(1)} %log_add_fusion), kind=kOutput, calls=%fused_computation.131 | convolution fusion | flops 412876800 | bytes 15777792 | tf_op jit(solution)/shard_map/nhqk,nqhd->nkhd/dot_general | solution.py:318
  239.9 10.3 %multiply_reduce_fusion = (f32[4,12,256]{2,1,0:T(8,128)S(1)}, f32[4,12,256,256]{2,3,1,0:T(8,128)}) fusion(f32[4,12,256,256]{2,3,1,0:T(8,128)} %copy-done.1, f32[4,12,256]{2,1,0:T(8,128)S(1)} %log_add_fusion, bf16[4,256,12,64]{1,0,3,2:T(4,128)(2,1)S(1)} %copy-done.18, bf16[4,256,12,64]{1,0,3,2:T(4,128)(2,1)S(1)} %copy-done.19), kind=kOutput, calls=%fused_computation.15 | convolution fusion | flops 415223808 | bytes 28409856 | tf_op jit(solution)/shard_map/nqhd,nkhd->nhqk/dot_general | solution.py:321
  250.2 7.2 multiply_convert_fusion
  257.5 3.2 fusion.72
  264.0 2.4 copy.84
  266.4 2.8 copy.81
  274.7 5.7 fusion.24
  280.4 8.5 %fusion.51 = (bf16[4,768]{1,0:T(4,128)(2,1)S(1)}, bf16[4,768]{1,0:T(4,128)(2,1)S(1)}, f32[4,256,768]{2,1,0:T(8,128)S(1)}, f32[1024,768]{1,0:T(8,128)}) fusion(f32[1024,768]{1,0:T(8,128)S(1)} %get-tuple-element.144, f32[4,256]{1,0:T(4,128)S(1)} %copy-done.90, f32[4,256]{1,0:T(4,128)S(1)} %copy-done.89, f32[256,768]{1,0:T(8,128)S(1)} %copy-done.8, ...), kind=kOutput, calls=%fused_computation.88 | convolution fusion | flops 3630950400 | bytes 21662720 | tf_op jit(solution)/shard_map/dot_general | solution.py:31
  290.0 9.7 %fusion.23 = bf16[768,16384]{1,0:T(8,128)(2,1)} fusion(bf16[768,16384]{1,0:T(8,128)(2,1)} %constant_dynamic-update-slice_fusion.9, bf16[1024,768]{1,0:T(8,128)(2,1)S(1)} %copy-done.39, bf16[1024,3072]{1,0:T(8,128)(2,1)} %copy-done.112), kind=kOutput, calls=%fused_computation.36 | convolution fusion | flops 4834197504 | bytes 12582912 | tf_op jit(solution)/shard_map/dot_general | solution.py:37
  299.9 10.8 %fusion.22 = bf16[768,16384]{1,0:T(8,128)(2,1)} fusion(bf16[768,16384]{1,0:T(8,128)(2,1)} %fusion.23, bf16[1024,768]{1,0:T(8,128)(2,1)S(1)} %copy-done.41, f32[1024,3072]{1,0:T(8,128)} %fusion.31, f32[3072]{0:T(1024)S(1)} %copy-done.78), kind=kOutput, calls=%fused_computation.34 | convolution fusion | flops 4865654784 | bytes 18886656 | tf_op jit(solution)/shard_map/dot_general | solution.py:37
  310.9 4.1 multiply_reduce_fusion.3
  315.1 5.0 fusion.10
  320.1 2.2 fusion.35
  322.3 4.9 fusion.12
  327.3 3.0 convert_reduce_fusion.10
  331.8 2.3 convert_reduce_fusion.9
  336.0 3.2 multiply_reduce_fusion.2
  342.1 2.8 convert_reduce_fusion.1
  347.8 2.3 convert_reduce_fusion.5
  351.4 2.2 convert_reduce_fusion.4
  368.2 41.8 %all-reduce = (f32[]{:T(128)}, f32[14608]{0:T(1024)}) all-reduce(f32[]{:T(128)S(6)} %div.164, f32[14608]{0:T(1024)} %constant_dynamic-update-slice_fusion.16), channel_id=1, replica_groups=mesh['shard'=2,'rep'=16] {'shard','rep'}, use_global_device_ids=true, to_apply=%region_9.10 | all-reduce | flops 14609 | bytes 116872 | tf_op jit(solution)/shard_map/psum | solution.py:451
  417.9 24.9 %fusion.8 = f32[768,8]{0,1:T(8,128)S(1)} fusion(f32[8192,8]{0,1:T(8,128)S(1)} %copy-done, f32[1,768,8192]{2,1,0:T(8,128)} %param.19, bf16[768,8192]{1,0:T(8,128)(2,1)} %reduce-scatter.2.cloned.1.call-done), kind=kOutput, calls=%fused_computation.21 | convolution fusion | flops 616562688 | bytes 38035456 | tf_op jit(solution)/shard_map/dot_general | solution.py:448
  442.8 75.8 %psum.36 = f32[768,8]{0,1:T(8,128)S(1)} all-reduce(f32[768,8]{0,1:T(8,128)S(1)} %fusion.8), channel_id=1, replica_groups=mesh['shard'=2,'rep'=16] {'rep'}, use_global_device_ids=true, to_apply=%region_24.25 | all-reduce | flops 6144 | bytes 49152 | tf_op jit(solution)/shard_map/psum | solution.py:452
  522.5 5.1 multiply_reduce_fusion.16
  532.1 6.3 multiply_reduce_fusion.15
  539.0 3.7 multiply_reduce_fusion.14
  542.7 2.5 multiply_reduce_fusion.31
  545.9 4.9 multiply_reduce_fusion.13
  561.2 17.6 %subtract_multiply_fusion.2 = (f32[768,1]{0,1:T(1,128)S(1)}, f32[768,1]{0,1:T(1,128)S(1)}, f32[768,1]{0,1:T(1,128)S(1)}, f32[768,1]{0,1:T(1,128)S(1)}, f32[768,1...) fusion(f32[768,1]{0,1:T(1,128)S(1)} %get-tuple-element.90, f32[768,8]{0,1:T(8,128)S(1)} %psum.36, ...), kind=kLoop, calls=%fused_computation.301 | loop fusion | flops 48384 | bytes 46220 | tf_op jit(solution)/shard_map/mul | solution.py:135
  578.8 19.9 %fusion.9 = bf16[8192,8]{0,1:T(8,128)(2,1)} fusion(f32[768,8]{0,1:T(8,128)S(1)} %stack.2, f32[1,768,8192]{2,1,0:T(8,128)} %param.19, bf16[768,8192]{1,0:T(8,128)(2,1)} %reduce-scatter.2.cloned.1.call-done), kind=kOutput, calls=%fused_computation.23 | convolution fusion | flops 616628224 | bytes 37904384 | tf_op jit(solution)/shard_map/dot_general | solution.py:43
  598.8 6.9 multiply_subtract_fusion.1
  605.7 94.5 %all-reduce.4.cloned.1.call-done = bf16[8192,8]{0,1:T(8,128)(2,1)} async-done(((bf16[8192,8]{0,1:T(8,128)(2,1)}), bf16[8192,8]{0,1:T(8,128)(2,1)}) %all-reduce.4.cloned.1.call-update) | async-done | bytes 131088 | tf_op jit(solution)/shard_map/psum | solution.py:454
  701.8 52.5 %multiply_subtract_fusion = (f32[768,8192]{1,0:T(8,128)}, f32[768,8192]{1,0:T(8,128)}, f32[1,768,8192]{2,1,0:T(8,128)}) fusion(f32[768,8192]{1,0:T(8,128)} %param.17, f32[]{:T(128)} %bitcast.20, f32[768,8192]{1,0:T(8,128)} %param.18, f32[1,768,8192]{2,1,0:T(8,128)} %param.19, bf16[768,8192]{1,0:T(8,128)(2,1)} %reduce-scatter.2.cloned.1.call-done, ...), kind=kOutput, calls=%fused_computation.2 | convolution fusion | flops 654311424 | bytes 163733504 | tf_op jit(solution)/shard_map/dot_general | solution.py:457
  (351 shorter events, 98.2 us)
Async XLA Ops:
  7.2 410.7 %copy-start = (f32[8192,8]{0,1:T(8,128)S(1)}, f32[8192,8]{0,1:T(8,128)}, u32[]{:S(2)}) copy-start(f32[8192,8]{0,1:T(8,128)} %param.20) | copy-start | bytes 786436
  7.2 56.4 %all-gather.2.cloned.1.call-start = ((), (), s32[]{:S(2)}) async-start(), calls=%async_computation.1 | async-start | bytes 37748736 | tf_op jit(solution)/shard_map/all_gather | solution.py:436
  20.4 6.5 copy-start.15
  20.4 397.5 %reduce-scatter.2.cloned.1.call-start = ((), (), s32[]{:S(2)}) async-start(), calls=%async_computation.2 | async-start | bytes 37748736 | tf_op jit(solution)/shard_map/reduce_scatter | solution.py:444
  30.8 35.6 %copy-start.109 = (s32[4]{0:T(128)S(1)}, s32[4]{0:T(128)}, u32[]{:S(2)}) copy-start(s32[4]{0:T(128)} %param.16) | copy-start | bytes 52
  30.8 45.4 %copy-start.49 = (f32[1024]{0:T(1024)}, f32[1024]{0:T(1024)S(1)}, u32[]{:S(2)}) copy-start(f32[1024]{0:T(1024)S(1)} %broadcast_multiply_fusion.4) | copy-start | bytes 12292
  33.6 30.0 %copy-start.83 = (f32[1024]{0:T(1024)}, f32[1024]{0:T(1024)S(1)}, u32[]{:S(2)}) copy-start(f32[1024]{0:T(1024)S(1)} %multiply_reduce_fusion.8) | copy-start | bytes 12292
  33.6 42.7 %copy-start.61 = (f32[1024]{0:T(1024)}, f32[1024]{0:T(1024)S(1)}, u32[]{:S(2)}) copy-start(f32[1024]{0:T(1024)S(1)} %fusion.119) | copy-start | bytes 12292
  34.9 29.9 %copy-start.105 = (bf16[4,128]{1,0:T(4,128)(2,1)}, bf16[4,128]{1,0:T(4,128)(2,1)S(1)}, u32[]{:S(2)}) copy-start(bf16[4,128]{1,0:T(4,128)(2,1)S(1)} %get-tuple-element.139) | copy-start | bytes 3076
  35.0 29.9 %copy-start.107 = (bf16[4,128]{1,0:T(4,128)(2,1)}, bf16[4,128]{1,0:T(4,128)(2,1)S(1)}, u32[]{:S(2)}) copy-start(bf16[4,128]{1,0:T(4,128)(2,1)S(1)} %get-tuple-element.140) | copy-start | bytes 3076
  64.8 6.7 copy-start.72
  64.9 6.6 slice-start.3
  76.3 7.5 copy-start.42
  77.2 6.6 copy-start.36
  118.2 6.3 copy-start.30
  127.6 12.3 %copy-start.81 = (f32[1024]{0:T(1024)}, f32[1024]{0:T(1024)S(1)}, u32[]{:S(2)}) copy-start(f32[1024]{0:T(1024)S(1)} %multiply_reduce_fusion.7) | copy-start | bytes 12292
  128.2 11.6 %copy-start.79 = (f32[1024]{0:T(1024)}, f32[1024]{0:T(1024)S(1)}, u32[]{:S(2)}) copy-start(f32[1024]{0:T(1024)S(1)} %get-tuple-element.128) | copy-start | bytes 12292
  128.9 10.9 %copy-start.38 = (bf16[1024,768]{1,0:T(8,128)(2,1)}, bf16[1024,768]{1,0:T(8,128)(2,1)S(1)}, u32[]{:S(2)}) copy-start(bf16[1024,768]{1,0:T(8,128)(2,1)S(1)} %fusion.48) | copy-start | bytes 4718596
  128.9 10.9 %copy-start.56 = (f32[4,768]{1,0:T(4,128)S(1)}, f32[4,768]{1,0:T(4,128)}, u32[]{:S(2)}) copy-start(f32[4,768]{1,0:T(4,128)} %get-tuple-element.170) | copy-start | bytes 36868
  129.0 10.9 %copy-start.76 = (f32[3072]{0:T(1024)S(1)}, f32[3072]{0:T(1024)}, u32[]{:S(2)}) copy-start(f32[3072]{0:T(1024)} %slice.122) | copy-start | bytes 36868
  129.0 10.9 %copy-start.87 = (f32[768]{0:T(1024)S(1)}, f32[768]{0:T(1024)}, u32[]{:S(2)}) copy-start(f32[768]{0:T(1024)} %get-tuple-element.116) | copy-start | bytes 9220
  176.2 17.3 %copy-start.40 = (bf16[1024,768]{1,0:T(8,128)(2,1)}, bf16[1024,768]{1,0:T(8,128)(2,1)S(1)}, u32[]{:S(2)}) copy-start(bf16[1024,768]{1,0:T(8,128)(2,1)S(1)} %get-tuple-element.94) | copy-start | bytes 4718596
  176.2 17.3 %copy-start.3 = (f32[1024,768]{1,0:T(8,128)S(1)}, f32[1024,768]{1,0:T(8,128)}, u32[]{:S(2)}) copy-start(f32[1024,768]{1,0:T(8,128)} %get-tuple-element.104) | copy-start | bytes 9437188
  176.2 17.3 %copy-start.52 = (f32[4,768]{1,0:T(4,128)S(1)}, f32[4,768]{1,0:T(4,128)}, u32[]{:S(2)}) copy-start(f32[4,768]{1,0:T(4,128)} %get-tuple-element.168) | copy-start | bytes 36868
  176.2 17.3 %copy-start.60 = (f32[1024]{0:T(1024)S(1)}, f32[1024]{0:T(1024)}, u32[]{:S(2)}) copy-start(f32[1024]{0:T(1024)} %copy-done.59) | copy-start | bytes 12292
  193.5 11.6 %copy-start.112 = (bf16[1024,3072]{1,0:T(8,128)(2,1)}, bf16[1024,3072]{1,0:T(8,128)(2,1)S(1)}, u32[]{:S(2)}) copy-start(bf16[1024,3072]{1,0:T(8,128)(2,1)S(1)} %get-tuple-element.157) | copy-start | bytes 18874372
  193.5 12.2 %copy-start.82 = (f32[1024]{0:T(1024)S(1)}, f32[1024]{0:T(1024)}, u32[]{:S(2)}) copy-start(f32[1024]{0:T(1024)} %copy-done.81) | copy-start | bytes 12292
  231.1 8.8 %copy-start.18 = (bf16[4,256,12,64]{1,0,3,2:T(4,128)(2,1)S(1)}, bf16[4,256,12,64]{1,0,3,2:T(4,128)(2,1)}, u32[]{:S(2)}) copy-start(bf16[4,256,12,64]{1,0,3,2:T(4,128)(2,1)} %reshape.458) | copy-start | bytes 4718596
  231.1 8.8 %copy-start.19 = (bf16[4,256,12,64]{1,0,3,2:T(4,128)(2,1)S(1)}, bf16[4,256,12,64]{1,0,3,2:T(4,128)(2,1)}, u32[]{:S(2)}) copy-start(bf16[4,256,12,64]{1,0,3,2:T(4,128)(2,1)} %reshape.463) | copy-start | bytes 4718596
  231.1 19.1 %slice-start = ((s8[12582912]{0:T(1024)(128)(4,1)}), s8[4194304]{0:T(1024)(128)(4,1)S(1)}, s32[]{:S(2)}) async-start(s8[12582912]{0:T(1024)(128)(4,1)} %bitcast.209), calls=%async_computation.5 | async-start | bytes 8388608
  239.9 10.3 %slice-start.1 = ((s8[12582912]{0:T(1024)(128)(4,1)}), s8[4194304]{0:T(1024)(128)(4,1)S(1)}, s32[]{:S(2)}) async-start(s8[12582912]{0:T(1024)(128)(4,1)} %bitcast.209), calls=%async_computation.6 | async-start | bytes 8388608
  239.9 10.4 %slice-start.2 = ((s8[12582912]{0:T(1024)(128)(4,1)}), s8[4194304]{0:T(1024)(128)(4,1)S(1)}, s32[]{:S(2)}) async-start(s8[12582912]{0:T(1024)(128)(4,1)} %bitcast.209), calls=%async_computation.7 | async-start | bytes 8388608
  250.2 7.2 copy-start.20
  274.6 5.7 copy-start.90
  280.4 8.5 %copy-start.33 = (bf16[768,768]{1,0:T(8,128)(2,1)S(1)}, bf16[768,768]{1,0:T(8,128)(2,1)}, u32[]{:S(2)}) copy-start(bf16[768,768]{1,0:T(8,128)(2,1)} %copy.84) | copy-start | bytes 3538948
  280.4 9.6 %copy-start.39 = (bf16[1024,768]{1,0:T(8,128)(2,1)S(1)}, bf16[1024,768]{1,0:T(8,128)(2,1)}, u32[]{:S(2)}) copy-start(bf16[1024,768]{1,0:T(8,128)(2,1)} %copy-done.38) | copy-start | bytes 4718596
  290.0 9.7 %copy-start.41 = (bf16[1024,768]{1,0:T(8,128)(2,1)S(1)}, bf16[1024,768]{1,0:T(8,128)(2,1)}, u32[]{:S(2)}) copy-start(bf16[1024,768]{1,0:T(8,128)(2,1)} %copy-done.40) | copy-start | bytes 4718596
  290.0 9.7 %copy-start.78 = (f32[3072]{0:T(1024)S(1)}, f32[3072]{0:T(1024)}, u32[]{:S(2)}) copy-start(f32[3072]{0:T(1024)} %slice.122) | copy-start | bytes 36868
  299.7 11.0 %copy-start.99 = (f32[4,256]{1,0:T(4,128)S(1)}, f32[4,256]{1,0:T(4,128)}, u32[]{:S(2)}) copy-start(f32[4,256]{1,0:T(4,128)} %reduce_sum.721) | copy-start | bytes 12292
  299.7 11.0 %copy-start.102 = (f32[4,256]{1,0:T(4,128)S(1)}, f32[4,256]{1,0:T(4,128)}, u32[]{:S(2)}) copy-start(f32[4,256]{1,0:T(4,128)} %add.410) | copy-start | bytes 12292
  299.7 11.0 %copy-start.100 = (f32[4,256]{1,0:T(4,128)S(1)}, f32[4,256]{1,0:T(4,128)}, u32[]{:S(2)}) copy-start(f32[4,256]{1,0:T(4,128)} %reduce_sum.722) | copy-start | bytes 12292
  299.8 11.0 %copy-start.101 = (f32[4,256]{1,0:T(4,128)S(1)}, f32[4,256]{1,0:T(4,128)}, u32[]{:S(2)}) copy-start(f32[4,256]{1,0:T(4,128)} %add.413) | copy-start | bytes 12292
  299.8 11.0 %copy-start.12 = (f32[1024,768]{1,0:T(8,128)S(1)}, f32[1024,768]{1,0:T(8,128)}, u32[]{:S(2)}) copy-start(f32[1024,768]{1,0:T(8,128)} %get-tuple-element.151) | copy-start | bytes 9437188
  299.8 11.0 %copy-start.26 = (f32[1024,768]{1,0:T(8,128)S(1)}, f32[1024,768]{1,0:T(8,128)}, u32[]{:S(2)}) copy-start(f32[1024,768]{1,0:T(8,128)} %get-tuple-element.148) | copy-start | bytes 9437188
  299.8 11.0 %copy-start.27 = (f32[1024,768]{1,0:T(8,128)S(1)}, f32[1024,768]{1,0:T(8,128)}, u32[]{:S(2)}) copy-start(f32[1024,768]{1,0:T(8,128)} %get-tuple-element.153) | copy-start | bytes 9437188
  299.8 11.0 %copy-start.53 = (f32[4,768]{1,0:T(4,128)S(1)}, f32[4,768]{1,0:T(4,128)}, u32[]{:S(2)}) copy-start(f32[4,768]{1,0:T(4,128)} %get-tuple-element.168) | copy-start | bytes 36868
  299.8 11.0 %copy-start.57 = (f32[4,768]{1,0:T(4,128)S(1)}, f32[4,768]{1,0:T(4,128)}, u32[]{:S(2)}) copy-start(f32[4,768]{1,0:T(4,128)} %get-tuple-element.170) | copy-start | bytes 36868
  299.8 11.0 %copy-start.92 = (f32[4,256]{1,0:T(4,128)S(1)}, f32[4,256]{1,0:T(4,128)}, u32[]{:S(2)}) copy-start(f32[4,256]{1,0:T(4,128)} %div.178) | copy-start | bytes 12292
  299.8 11.0 %copy-start.93 = (f32[4,256]{1,0:T(4,128)S(1)}, f32[4,256]{1,0:T(4,128)}, u32[]{:S(2)}) copy-start(f32[4,256]{1,0:T(4,128)} %div.174) | copy-start | bytes 12292
  299.8 11.0 %copy-start.94 = (f32[4,256]{1,0:T(4,128)S(1)}, f32[4,256]{1,0:T(4,128)}, u32[]{:S(2)}) copy-start(f32[4,256]{1,0:T(4,128)} %div.177) | copy-start | bytes 12292
  299.8 11.0 %copy-start.95 = (f32[4,256]{1,0:T(4,128)S(1)}, f32[4,256]{1,0:T(4,128)}, u32[]{:S(2)}) copy-start(f32[4,256]{1,0:T(4,128)} %div.181) | copy-start | bytes 12292
  315.0 12.3 %copy-start.67 = (bf16[4,768]{1,0:T(4,128)(2,1)}, bf16[4,768]{1,0:T(4,128)(2,1)S(1)}, u32[]{:S(2)}) copy-start(bf16[4,768]{1,0:T(4,128)(2,1)S(1)} %get-tuple-element.11) | copy-start | bytes 18436
  315.0 12.3 %copy-start.69 = (bf16[4,768]{1,0:T(4,128)(2,1)}, bf16[4,768]{1,0:T(4,128)(2,1)S(1)}, u32[]{:S(2)}) copy-start(bf16[4,768]{1,0:T(4,128)(2,1)S(1)} %get-tuple-element.14) | copy-start | bytes 18436
  322.3 8.0 %copy-start.73 = (f32[4,768]{1,0:T(4,128)S(1)}, f32[4,768]{1,0:T(4,128)}, u32[]{:S(2)}) copy-start(f32[4,768]{1,0:T(4,128)} %copy-done.72) | copy-start | bytes 36868
  327.3 6.9 copy-start.106
  327.3 6.9 copy-start.108
  335.3 263.5 %all-reduce.6.cloned.1.call-start = ((), (), s32[]{:S(2)}) async-start(), calls=%async_computation.4 | async-start | bytes 6340608 | tf_op jit(solution)/shard_map/psum | solution.py:451
  345.0 9.9 %copy-start.91 = (f32[768]{0:T(1024)S(1)}, f32[768]{0:T(1024)}, u32[]{:S(2)}) copy-start(f32[768]{0:T(1024)} %get-tuple-element.95) | copy-start | bytes 9220
  345.0 12.6 %copy-start.103 = (f32[768]{0:T(1024)S(1)}, f32[768]{0:T(1024)}, u32[]{:S(2)}) copy-start(f32[768]{0:T(1024)} %get-tuple-element.93) | copy-start | bytes 9220
  345.0 65.1 %copy-start.24 = (bf16[1024,768]{1,0:T(8,128)(2,1)S(1)}, bf16[1024,768]{1,0:T(8,128)(2,1)}, u32[]{:S(2)}) copy-start(bf16[1024,768]{1,0:T(8,128)(2,1)} %copy-done.23) | copy-start | bytes 4718596
  345.0 65.4 %copy-start.32 = (bf16[1024,768]{1,0:T(8,128)(2,1)S(1)}, bf16[1024,768]{1,0:T(8,128)(2,1)}, u32[]{:S(2)}) copy-start(bf16[1024,768]{1,0:T(8,128)(2,1)} %get-tuple-element.92) | copy-start | bytes 4718596
  347.8 63.8 %copy-start.71 = (f32[4,768]{1,0:T(4,128)S(1)}, f32[4,768]{1,0:T(4,128)}, u32[]{:S(2)}) copy-start(f32[4,768]{1,0:T(4,128)} %copy-done.70) | copy-start | bytes 36868
  415.7 284.5 %all-reduce.4.cloned.1.call-start = ((), (), s32[]{:S(2)}) async-start(), calls=%async_computation.3 | async-start | bytes 262144 | tf_op jit(solution)/shard_map/psum | solution.py:454
  578.8 20.0 %copy-start.16 = (f32[768,1032]{0,1:T(8,128)S(1)}, f32[768,1032]{0,1:T(8,128)}, u32[]{:S(2)}) copy-start(f32[768,1032]{0,1:T(8,128)} %param.21) | copy-start | bytes 9510916
  (57 other events, 163.2 us)
Sparse Core Ops, SparseCore 0:
  20.6 43.0 all-gather.1
  335.4 31.6 reduce-scatter.1
  415.9 138.3 all-reduce.5
  598.9 101.2 all-reduce.3
where the time goes:
time: 770 us; the launch traced here: 761 us
  matrix products  278 us (36%)
  other arithmetic  141 us (18%)
  waiting for transfers between devices  123 us (16%)
  blocking collectives  118 us (15%)
  local copies, waits for them, and re-layouts  80.3 us (10%)
  between operations  21.4 us (3%)
    psum x1, waiting for transfers between devices, on_device(): lax.psum(exact_outer(matrices, basis).astype(jnp.bfloat16), 'rep')  94.5 us
    psum x1, blocking collectives, on_device(): left_sum = lax.psum(left_part, 'rep')  75.8 us
    dot_general x10, matrix products, multiply_trans(): lax.dot_general(left_side, right_side, (((1,), (1,)), ((), ())), preferre...  53.5 us
    dot_general x1, matrix products, on_device(): lax.dot_general(basis, right_sum, (((1,), (1,)), ((), ())), precision=hig...  52.5 us
    dot_general x8, matrix products, multiply(): return jnp.dot(left_side, right_side, preferred_element_type=jnp.float32)  50.7 us
    psum x1, blocking collectives, on_device(): lax.psum((grad_small, grad_bias, loss_part), ('shard', 'rep'))  41.8 us
    dot_general x10, matrix products, outer_sum(): lax.dot_general(left_side, right_side, (((0,), (0,)), ((), ())), preferre...  40.2 us
    all_gather x1, waiting for transfers between devices, on_device(): lax.all_gather(master_big.astype(half_type), 'shard', axis=1, tiled=True)  28.7 us
  transfers between devices with their start and end apart: 4, of which 2 were waited for; matrix products, arithmetic and copies ran while one was open for 21% of the time, Pallas kernels for 0%

commit v1 on v0

--- a/solution.py
+++ b/solution.py
@@ -1,8 +1,11 @@
+import functools
 import math
 
 import jax
 import jax.numpy as jnp
 from jax import lax
+from jax.experimental import pallas as pl
+from jax.experimental.pallas import tpu as pltpu
 from jax.sharding import PartitionSpec as P
 
 D = 768
@@ -376,7 +379,6 @@
         grad_fmod, final_weight
     )
     grad_condition = slope(jax.nn.silu, kept["condition"], grad_active)
-    grad_table = jnp.einsum("nd,nc->dc", grad_condition, kept["chosen"], precision=highest)
     grad_embed = grad_condition.astype(half_type)
     bias_second = column_sums(grad_embed)
     grad_second = outer_sum(kept["embed_hidden"], grad_embed)
@@ -397,7 +399,7 @@
         ],
         axis=1,
     )
-    grad_small = jnp.concatenate([grad_patch, grad_table, grad_head], axis=1)
+    grad_small = (grad_patch, grad_head, grad_condition)
     grad_bias = jnp.concatenate(
         [
             bias_query,
@@ -440,7 +442,11 @@
     loss_part = jnp.sum(error * error) / entries
     grad_output = 2.0 * error / entries
     gathered = lax.all_gather(master_big.astype(half_type), "shard", axis=1, tiled=True)
-    grad_big, grad_small, grad_bias = backward(gathered, master_small, kept, grad_output)
+    grad_big, (grad_patch, grad_head, grad_condition), grad_bias = backward(
+        gathered, master_small, kept, grad_output
+    )
+    grad_table = jnp.einsum("nd,nc->dc", grad_condition, kept["chosen"], precision=highest)
+    grad_small = jnp.concatenate([grad_patch, grad_table, grad_head], axis=1)
     owned = lax.psum_scatter(
         grad_big.astype(jnp.bfloat16), "shard", scatter_dimension=1, tiled=True
     ).astype(jnp.float32)
@@ -481,6 +487,579 @@
     )
 
 
+MESH = pl.DeviceIdType.MESH
+BLOCK = 512
+RANK = 8
+LANES = 128
+REPS = 16
+
+
+def sds(shape, dtype=jnp.float32):
+    return jax.ShapeDtypeStruct(shape, dtype)
+
+
+def split_two(values):
+    high = values.astype(half_type)
+    low = (values - high.astype(jnp.float32)).astype(half_type)
+    return high, low
+
+
+def greet(others):
+    barrier = pltpu.get_barrier_semaphore()
+    for other in others:
+        pl.semaphore_signal(barrier, inc=1, device_id=other, device_id_type=MESH)
+    return barrier, len(others)
+
+
+def small_kernel(
+    sums_ref, rows_ref, total_ref, gathered_ref, half_ref, part_ref, mine_ref, send_sem, recv_sem
+):
+    shard = lax.axis_index("shard")
+    rep = lax.axis_index("rep")
+    partner = (1 - shard, rep)
+    peers = [(shard, lax.rem(rep + step, REPS)) for step in range(1, REPS)]
+    barrier, count = greet([partner] + peers)
+    pl.semaphore_wait(barrier, count)
+
+    def remote(source, target, where, who):
+        return pltpu.make_async_remote_copy(
+            src_ref=source,
+            dst_ref=target,
+            send_sem=send_sem.at[where],
+            recv_sem=recv_sem.at[where],
+            device_id=who,
+            device_id_type=MESH,
+        )
+
+    rows_out = [
+        pltpu.make_async_remote_copy(
+            src_ref=rows_ref,
+            dst_ref=gathered_ref.at[shard, rep],
+            send_sem=send_sem.at[step],
+            recv_sem=recv_sem.at[rep],
+            device_id=peers[step - 1],
+            device_id_type=MESH,
+        )
+        for step in range(1, REPS)
+    ]
+    own_half = remote(sums_ref.at[1 - shard], half_ref, 16, partner)
+    own_half.start()
+    for copy in rows_out:
+        copy.start()
+    gathered_ref[shard, rep] = rows_ref[...]
+    own_half.wait()
+    half_ref[...] = half_ref[...] + sums_ref[shard]
+    parts_out = [
+        pltpu.make_async_remote_copy(
+            src_ref=half_ref.at[lax.rem(rep + step, REPS)],
+            dst_ref=part_ref.at[rep],
+            send_sem=send_sem.at[17 + step],
+            recv_sem=recv_sem.at[17 + rep],
+            device_id=peers[step - 1],
+            device_id_type=MESH,
+        )
+        for step in range(1, REPS)
+    ]
+    for copy in parts_out:
+        copy.start()
+    part_ref[rep] = half_ref[rep]
+
+    def arrived(slots, base):
+        for step in range(1, REPS):
+            other = lax.rem(rep + step, REPS)
+            pltpu.make_async_remote_copy(
+                src_ref=slots.at[other],
+                dst_ref=slots.at[other],
+                send_sem=send_sem.at[base],
+                recv_sem=recv_sem.at[base + other],
+                device_id=peers[step - 1],
+                device_id_type=MESH,
+            ).wait_recv()
+
+    arrived(part_ref, 17)
+    mine_ref[...] = jnp.sum(part_ref[...], axis=0)
+    whole_out = [
+        pltpu.make_async_remote_copy(
+            src_ref=mine_ref,
+            dst_ref=total_ref.at[shard, rep],
+            send_sem=send_sem.at[33 + step],
+            recv_sem=recv_sem.at[33 + rep],
+            device_id=peers[step - 1],
+            device_id_type=MESH,
+        )
+        for step in range(1, REPS)
+    ]
+    for copy in whole_out:
+        copy.start()
+    total_ref[shard, rep] = mine_ref[...]
+    arrived(gathered_ref.at[shard], 0)
+    rows_across = remote(gathered_ref.at[shard], gathered_ref.at[shard], 49, partner)
+    rows_across.start()
+    arrived(total_ref.at[shard], 33)
+    total_across = remote(total_ref.at[shard], total_ref.at[shard], 50, partner)
+    total_across.start()
+    for copy in rows_out + parts_out + whole_out:
+        copy.wait_send()
+    rows_across.wait()
+    total_across.wait()
+
+
+def small_sums(sums, rows):
+    return pl.pallas_call(
+        small_kernel,
+        out_shape=(sds((2, REPS) + sums.shape[2:]), sds((2, REPS) + rows.shape)),
+        in_specs=[pl.BlockSpec(memory_space=pltpu.VMEM)] * 2,
+        out_specs=[pl.BlockSpec(memory_space=pltpu.VMEM)] * 2,
+        scratch_shapes=[
+            pltpu.VMEM(sums.shape[1:], jnp.float32),
+            pltpu.VMEM((REPS,) + sums.shape[2:], jnp.float32),
+            pltpu.VMEM(sums.shape[2:], jnp.float32),
+            pltpu.SemaphoreType.DMA((51,)),
+            pltpu.SemaphoreType.DMA((51,)),
+        ],
+        compiler_params=pltpu.CompilerParams(
+            collective_id=1, has_side_effects=True, vmem_limit_bytes=16 * 1024 * 1024
+        ),
+        name="small_sums",
+    )(sums, rows)
+
+
+def tail_kernel(
+    rates_ref,
+    own_hbm,
+    recv_hbm,
+    error_hbm,
+    factor_ref,
+    moment_hbm,
+    master_hbm,
+    new_master_hbm,
+    new_moment_hbm,
+    new_error_hbm,
+    right_ref,
+    m_ref,
+    v_ref,
+    own_ref,
+    recv_ref,
+    master_ref,
+    stack_ref,
+    left_acc,
+    left_ref,
+    plane_ref,
+    column_ref,
+    basis_rows,
+    basis_cols,
+    send_ref,
+    part_ref,
+    mine_ref,
+    whole_ref,
+    load_sem,
+    own_sem,
+    recv_sem,
+    moment_sem,
+    master_sem,
+    out_sem,
+    left_send,
+    left_recv,
+    right_send,
+    right_recv,
+):
+    blocks = m_ref.shape[0]
+    shard = lax.axis_index("shard")
+    rep = lax.axis_index("rep")
+    peers = [(shard, lax.rem(rep + step, REPS)) for step in range(1, REPS)]
+    barrier, count = greet(peers)
+
+    def columns(block):
+        return pl.ds(pl.multiple_of(block * BLOCK, BLOCK), BLOCK)
+
+    def load_error(block):
+        return pltpu.make_async_copy(
+            error_hbm.at[0, :, columns(block)], m_ref.at[block], load_sem.at[block]
+        )
+
+    def load_own(block, slot):
+        return pltpu.make_async_copy(
+            own_hbm.at[:, columns(block)], own_ref.at[slot], own_sem.at[slot]
+        )
+
+    def load_recv(block, slot):
+        return pltpu.make_async_copy(
+            recv_hbm.at[:, columns(block)], recv_ref.at[slot], recv_sem.at[slot]
+        )
+
+    def load_moment(block):
+        return pltpu.make_async_copy(
+            moment_hbm.at[:, columns(block)], v_ref.at[block], moment_sem.at[block]
+        )
+
+    depth = own_ref.shape[0]
+
+    for block in range(depth):
+        load_error(block).start()
+        load_own(block, block).start()
+        load_recv(block, block).start()
+
+    high, low = split_two(factor_ref[...])
+    stack_ref[...] = jnp.zeros_like(stack_ref)
+    stack_ref[0:RANK] = high
+    stack_ref[RANK : 2 * RANK] = low
+    left_acc[...] = jnp.zeros_like(left_acc)
+
+    def gather_block(block, carry):
+        slot = lax.rem(block, depth)
+        load_error(block).wait()
+        load_own(block, slot).wait()
+        load_recv(block, slot).wait()
+        matrix = (
+            own_ref[slot].astype(jnp.float32) + recv_ref[slot].astype(jnp.float32) + m_ref[block]
+        )
+        m_ref[block] = matrix
+        high, low = split_two(matrix)
+        factor = stack_ref[:, columns(block)]
+        left_acc[...] += multiply_trans(high, factor) + multiply_trans(low, factor)
+
+        @pl.when(block + depth < blocks)
+        def _():
+            load_error(block + depth).start()
+            load_own(block + depth, slot).start()
+            load_recv(block + depth, slot).start()
+
+        return carry
+
+    lax.fori_loop(0, blocks, gather_block, 0)
+    for block in range(blocks):
+        load_moment(block).start()
+
+    def load_master(block, slot):
+        return pltpu.make_async_copy(
+            master_hbm.at[:, columns(block)], master_ref.at[slot], master_sem.at[slot]
+        )
+
+    slots = master_ref.shape[0]
+    for block in range(slots):
+        load_master(block, block).start()
+
+    turned = left_acc[...].T
+    left_ref[...] = turned[0:RANK] + turned[RANK : 2 * RANK]
+    pl.semaphore_wait(barrier, count)
+
+    place = lax.rem(rep, 4)
+    level = lax.div(rep, 4)
+    plane_out = []
+    for step in range(1, 4):
+        other = lax.rem(place + step, 4)
+        plane_out.append(
+            pltpu.make_async_remote_copy(
+                src_ref=left_ref,
+                dst_ref=plane_ref.at[place],
+                send_sem=left_send.at[step],
+                recv_sem=left_recv.at[place],
+                device_id=(shard, level * 4 + other),
+                device_id_type=MESH,
+            )
+        )
+    for copy in plane_out:
+        copy.start()
+    plane_ref[place] = left_ref[...]
+    for step in range(1, 4):
+        other = lax.rem(place + step, 4)
+        pltpu.make_async_remote_copy(
+            src_ref=left_ref,
+            dst_ref=plane_ref.at[other],
+            send_sem=left_send.at[step],
+            recv_sem=left_recv.at[other],
+            device_id=(shard, level * 4 + other),
+            device_id_type=MESH,
+        ).wait_recv()
+    plane_sum = (plane_ref[0] + plane_ref[1]) + (plane_ref[2] + plane_ref[3])
+    for copy in plane_out:
+        copy.wait_send()
+    left_ref[...] = plane_sum
+    column_out = []
+    for step in range(1, 4):
+        other = lax.rem(level + step, 4)
+        column_out.append(
+            pltpu.make_async_remote_copy(
+                src_ref=left_ref,
+                dst_ref=column_ref.at[level],
+                send_sem=left_send.at[4 + step],
+                recv_sem=left_recv.at[4 + level],
+                device_id=(shard, other * 4 + place),
+                device_id_type=MESH,
+            )
+        )
+    for copy in column_out:
+        copy.start()
+    column_ref[level] = plane_sum
+    for step in range(1, 4):
+        other = lax.rem(level + step, 4)
+        pltpu.make_async_remote_copy(
+            src_ref=left_ref,
+            dst_ref=column_ref.at[other],
+            send_sem=left_send.at[4 + step],
+            recv_sem=left_recv.at[4 + other],
+            device_id=(shard, other * 4 + place),
+            device_id_type=MESH,
+        ).wait_recv()
+    vectors = (column_ref[0] + column_ref[1]) + (column_ref[2] + column_ref[3])
+
+    row_index = lax.broadcasted_iota(jnp.int32, (RANK, 1), 0)
+    for place_of in range(RANK):
+        row = vectors[place_of : place_of + 1]
+        unit = row * lax.rsqrt(jnp.sum(row * row, axis=1, keepdims=True) + tiny_value)
+        dots = jnp.sum(vectors * unit, axis=1, keepdims=True)
+        vectors = jnp.where(
+            row_index > place_of,
+            vectors - dots * unit,
+            jnp.where(row_index == place_of, unit, vectors),
+        )
+    high, low = split_two(vectors)
+    basis_rows[...] = jnp.concatenate([high, low], axis=0)
+    padded = jnp.concatenate(
+        [
+            high.astype(jnp.float32),
+            low.astype(jnp.float32),
+            jnp.zeros((LANES - 2 * RANK, vectors.shape[1]), jnp.float32),
+        ],
+        axis=0,
+    )
+    basis_cols[...] = padded.T.astype(half_type)
+    for copy in column_out:
+        copy.wait_send()
+
+    def right_block(block, carry):
+        high, low = split_two(m_ref[block])
+        first = multiply(basis_rows[...], high)
+        second = multiply(basis_rows[...], low)
+        both = first + second
+        send_ref[block] = (both[0:RANK] + both[RANK : 2 * RANK]).astype(half_type)
+        return carry
+
+    lax.fori_loop(0, blocks, right_block, 0)
+
+    def right_copy(source, target, base, step, sender):
+        return pltpu.make_async_remote_copy(
+            src_ref=source,
+            dst_ref=target,
+            send_sem=right_send.at[base + step],
+            recv_sem=right_recv.at[base + sender],
+            device_id=peers[step - 1],
+            device_id_type=MESH,
+        )
+
+    scatter = [
+        right_copy(send_ref.at[lax.rem(rep + step, REPS)], part_ref.at[rep], 0, step, rep)
+        for step in range(1, REPS)
+    ]
+    for copy in scatter:
+        copy.start()
+    part_ref[rep] = send_ref[rep]
+    for step in range(1, REPS):
+        other = lax.rem(rep + step, REPS)
+        right_copy(send_ref.at[other], part_ref.at[other], 0, step, other).wait_recv()
+    mine_ref[...] = jnp.sum(part_ref[...].astype(jnp.float32), axis=0).astype(half_type)
+    spread = [
+        right_copy(mine_ref, whole_ref.at[rep], REPS, step, rep) for step in range(1, REPS)
+    ]
+    for copy in spread:
+        copy.start()
+    whole_ref[rep] = mine_ref[...]
+    for step in range(1, REPS):
+        other = lax.rem(rep + step, REPS)
+        right_copy(mine_ref, whole_ref.at[other], REPS, step, other).wait_recv()
+
+    def out_error(block):
+        return pltpu.make_async_copy(
+            m_ref.at[block], new_error_hbm.at[0, :, columns(block)], load_sem.at[block]
+        )
+
+    def out_moment(block):
+        return pltpu.make_async_copy(
+            v_ref.at[block], new_moment_hbm.at[:, columns(block)], moment_sem.at[block]
+        )
+
+    def out_master(block, slot):
+        return pltpu.make_async_copy(
+            master_ref.at[slot], new_master_hbm.at[:, columns(block)], out_sem.at[slot]
+        )
+
+    rate = rates_ref[0]
+
+    def update_block(block, carry):
+        slot = lax.rem(block, slots)
+
+        @pl.when(jnp.logical_and(block >= 1, block - 1 + slots < blocks))
+        def _():
+            earlier = lax.rem(block - 1, slots)
+            out_master(block - 1, earlier).wait()
+            load_master(block - 1 + slots, earlier).start()
+
+        right = whole_ref[block]
+        right_ref[:, columns(block)] = right.astype(jnp.float32)
+        approx = multiply(
+            basis_cols[:, 0 : 2 * RANK], jnp.concatenate([right, right], axis=0)
+        )
+        m_ref[block] = m_ref[block] - approx * (1.0 / REPS)
+        out_error(block).start()
+        load_moment(block).wait()
+        moment = momentum_decay * v_ref[block] + approx
+        v_ref[block] = moment
+        out_moment(block).start()
+        load_master(block, slot).wait()
+        master_ref[slot] = master_ref[slot] - rate * moment
+        out_master(block, slot).start()
+        return carry
+
+    lax.fori_loop(0, blocks, update_block, 0)
+    for block in range(blocks):
+        out_error(block).wait()
+        out_moment(block).wait()
+    for block in range(blocks - slots, blocks):
+        out_master(block, block % slots).wait()
+    for copy in scatter + spread:
+        copy.wait_send()
+
+
+def compress(rates, own, received, error, factor_rows, moment, master):
+    rows, cols = own.shape
+    blocks = cols // BLOCK
+    depth = 3
+    slots = 3
+    hbm = pl.BlockSpec(memory_space=pl.ANY)
+    vmem = pl.BlockSpec(memory_space=pltpu.VMEM)
+    return pl.pallas_call(
+        tail_kernel,
+        out_shape=(
+            sds(master.shape),
+            sds(moment.shape),
+            sds(error.shape),
+            sds((RANK, cols)),
+        ),
+        in_specs=[pl.BlockSpec(memory_space=pltpu.SMEM), hbm, hbm, hbm, vmem, hbm, hbm],
+        out_specs=[hbm, hbm, hbm, vmem],
+        scratch_shapes=[
+            pltpu.VMEM((blocks, rows, BLOCK), jnp.float32),
+            pltpu.VMEM((blocks, rows, BLOCK), jnp.float32),
+            pltpu.VMEM((depth, rows, BLOCK), half_type),
+            pltpu.VMEM((depth, rows, BLOCK), half_type),
+            pltpu.VMEM((slots, rows, BLOCK), jnp.float32),
+            pltpu.VMEM((LANES, cols), half_type),
+            pltpu.VMEM((rows, LANES), jnp.float32),
+            pltpu.VMEM((RANK, rows), jnp.float32),
+            pltpu.VMEM((4, RANK, rows), jnp.float32),
+            pltpu.VMEM((4, RANK, rows), jnp.float32),
+            pltpu.VMEM((2 * RANK, rows), half_type),
+            pltpu.VMEM((rows, LANES), half_type),
+            pltpu.VMEM((blocks, RANK, BLOCK), half_type),
+            pltpu.VMEM((blocks, RANK, BLOCK), half_type),
+            pltpu.VMEM((RANK, BLOCK), half_type),
+            pltpu.VMEM((blocks, RANK, BLOCK), half_type),
+            pltpu.SemaphoreType.DMA((blocks,)),
+            pltpu.SemaphoreType.DMA((depth,)),
+            pltpu.SemaphoreType.DMA((depth,)),
+            pltpu.SemaphoreType.DMA((blocks,)),
+            pltpu.SemaphoreType.DMA((slots,)),
+            pltpu.SemaphoreType.DMA((slots,)),
+            pltpu.SemaphoreType.DMA((8,)),
+            pltpu.SemaphoreType.DMA((8,)),
+            pltpu.SemaphoreType.DMA((2 * REPS,)),
+            pltpu.SemaphoreType.DMA((2 * REPS,)),
+        ],
+        compiler_params=pltpu.CompilerParams(
+            collective_id=2, has_side_effects=True, vmem_limit_bytes=67_000_000
+        ),
+        name="compress",
+    )(rates, own, received, error, factor_rows, moment, master)
+
+
+def on_pair(
+    noisy_patches,
+    targets,
+    timesteps,
+    labels,
+    master_big,
+    moment_big,
+    error_big,
+    factor_right,
+    master_small,
+    moment_small,
+    biases,
+    moment_bias,
+    step_rates,
+):
+    shards = lax.axis_size("shard")
+    replicas = lax.axis_size("rep")
+    gathered = lax.all_gather(master_big.astype(half_type), "shard", axis=1, tiled=True)
+    output, kept = forward(gathered, master_small, biases, noisy_patches, timesteps, labels)
+    entries = noisy_patches.shape[0] * shards * replicas * SEQ * P_DIM
+    error = output - targets.reshape(output.shape)
+    loss_part = jnp.sum(error * error) / entries
+    grad_output = 2.0 * error / entries
+    grad_big, (grad_patch, grad_head, grad_condition), grad_bias = backward(
+        gathered, master_small, kept, grad_output
+    )
+    shard = lax.axis_index("shard")
+    cols = master_big.shape[1]
+    low_grad = grad_big.astype(half_type)
+    own = lax.dynamic_slice_in_dim(low_grad, shard * cols, cols, axis=1)
+    received = lax.ppermute(
+        lax.dynamic_slice_in_dim(low_grad, (1 - shard) * cols, cols, axis=1),
+        "shard",
+        [(0, 1), (1, 0)],
+    )
+    images = labels.shape[0]
+    flat = jnp.concatenate(
+        [
+            grad_patch.T.reshape(-1),
+            grad_head.T.reshape(-1),
+            grad_bias,
+            loss_part[None],
+        ]
+    )
+    width = shards * replicas * 16 * LANES
+    sums = jnp.pad(flat, (0, width - flat.shape[0])).reshape(shards, replicas, 16, LANES)
+    lines = images * D // LANES
+    rows = jnp.concatenate(
+        [
+            grad_condition.reshape(lines, LANES),
+            jnp.pad(labels.astype(jnp.float32)[None], ((0, 7), (0, LANES - images))),
+        ]
+    )
+    total, all_rows = small_sums(sums, rows)
+    new_master, new_moment, new_error, right_rows = compress(
+        step_rates, own, received, error_big, factor_right.T, moment_big, master_big
+    )
+    total = total.reshape(-1)
+    all_labels = all_rows[:, :, lines, :images].reshape(-1).astype(jnp.int32)
+    conditions = all_rows[:, :, :lines, :].reshape(-1, D)
+    chosen = (jnp.arange(NCLASS, dtype=jnp.int32)[:, None] == all_labels[None, :]).astype(
+        jnp.float32
+    )
+    table_rows = jnp.dot(chosen, conditions, precision=highest, preferred_element_type=jnp.float32)
+    strip = P_DIM * D
+    small_sum = jnp.concatenate(
+        [total[:strip].reshape(P_DIM, D), table_rows, total[strip : 2 * strip].reshape(P_DIM, D)]
+    ).T
+    bias_count = biases.shape[0]
+    bias_sum = total[2 * strip : 2 * strip + bias_count]
+    total_loss = total[2 * strip + bias_count]
+    new_moment_small = momentum_decay * moment_small + small_sum
+    new_master_small = master_small - step_rates[1] * new_moment_small
+    new_moment_bias = momentum_decay * moment_bias + bias_sum
+    new_biases = biases - step_rates[1] * new_moment_bias
+    return (
+        total_loss,
+        new_master,
+        new_moment,
+        new_error,
+        right_rows.T,
+        new_master_small,
+        new_moment_small,
+        new_biases,
+        new_moment_bias,
+    )
+
+
 def solution(mesh):
     in_specs = (
         P(("shard", "rep"), None),
@@ -508,6 +1087,7 @@
         P(),
         P(),
     )
+    fits = mesh.shape["shard"] == 2 and mesh.shape["rep"] == 16
     return jax.shard_map(
-        on_device, mesh=mesh, in_specs=in_specs, out_specs=out_specs, check_vma=False
-    )
+        on_pair if fits else on_device, mesh=mesh, in_specs=in_specs, out_specs=out_specs, check_vma=False
+    )

time: 770 us -> 537 us (0.70)
  blocking collectives: 118 us -> 0 us
  Pallas kernels: 0 us -> 104 us
  matrix products: 278 us -> 175 us
  waiting for transfers between devices: 123 us -> 30.5 us
  other arithmetic: 141 us -> 73.8 us
  local copies, waits for them, and re-layouts: 80.3 us -> 126 us
    psum x2 -> x0, blocking collectives: 118 us -> none  [the longest x1 75.8 us: on_device(): left_sum = lax.psum(left_part, 'rep')]
    pallas_call x0 -> x2, Pallas kernels: none -> 104 us  [the longest x1 81.2 us: compress(): pl.pallas_call(tail_kernel, out_shape=(sds(master.shape), sds(moment.shap...]
    dot_general x4 -> x1, matrix products: 99.5 us -> 2.38 us  [on_pair(): jnp.dot(chosen, conditions, precision=highest, preferred_element_type=jnp...]
    psum x2 -> x0, waiting for transfers between devices: 94.5 us -> none  [the longest x1 94.5 us: on_device(): lax.psum(exact_outer(matrices, basis).astype(jnp.bfloat16), 'rep')]
    reduce_sum x15 -> x1, other arithmetic: 39.7 us -> 2.47 us  [backward(): jnp.sum(grad_attn_in * normalize(kept['stream_in']), axis=1)]
    unnamed x254 -> x181, local copies, waits for them, and re-layouts: 25.5 us -> 61.5 us
    mul x2 -> x0, other arithmetic: 17.6 us -> none  [orthonormal(): vector * lax.rsqrt(jnp.sum(vector * vector, axis=-1, keepdims=True) + tin...]
    dynamic_slice x0 -> x1, local copies, waits for them, and re-layouts: none -> 17.4 us  [on_pair(): lax.dynamic_slice_in_dim(low_grad, (1 - shard) * cols, cols, axis=1)]
  transfers between devices with their start and end apart: 4 -> 2, of which waited for: 2 -> 1; matrix products, arithmetic and copies ran while one was open for 21% -> 7% of each run, Pallas kernels for 0% -> 4%
where the time goes in v1:
time: 537 us; the launch traced here: 527 us
  matrix products  175 us (33%)
  local copies, waits for them, and re-layouts  126 us (23%)
  Pallas kernels  104 us (19%)
  other arithmetic  73.8 us (14%)
  waiting for transfers between devices  30.5 us (6%)
  between operations  16.5 us (3%)
    pallas_call x1, Pallas kernels, compress(): pl.pallas_call(tail_kernel, out_shape=(sds(master.shape), sds(moment.shap...  81.2 us
    unnamed x181, local copies, waits for them, and re-layouts  61.5 us
    dot_general x10, matrix products, multiply_trans(): lax.dot_general(left_side, right_side, (((1,), (1,)), ((), ())), preferre...  50.6 us
    dot_general x8, matrix products, multiply(): return jnp.dot(left_side, right_side, preferred_element_type=jnp.float32)  50 us
    dot_general x10, matrix products, outer_sum(): lax.dot_general(left_side, right_side, (((0,), (0,)), ((), ())), preferre...  38.6 us
    all_gather x1, waiting for transfers between devices, on_pair(): lax.all_gather(master_big.astype(half_type), 'shard', axis=1, tiled=True)  30.5 us
    pallas_call x1, Pallas kernels, small_sums(): pl.pallas_call(small_kernel, out_shape=(sds((2, REPS) + sums.shape[2:]),...  23.1 us
    dynamic_slice x1, local copies, waits for them, and re-layouts, on_pair(): lax.dynamic_slice_in_dim(low_grad, (1 - shard) * cols, cols, axis=1)  17.4 us
  transfers between devices with their start and end apart: 2, of which 1 were waited for; matrix products, arithmetic and copies ran while one was open for 7% of the time, Pallas kernels for 4%

profile of v1, /device:TPU:0, one launch (start us, length us, event | category | flops | bytes accessed | tf_op | source)
XLA Modules:
  0.0 526.8 jit_solution(4903994008251555309)
XLA Ops:
  7.2 13.1 %convert_element_type.150 = bf16[768,8192]{1,0:T(8,128)(2,1)} convert(f32[768,8192]{1,0:T(8,128)} %master_hbm.1) | non-fusion elementwise | flops 6291456 | bytes 37748736 | tf_op jit(solution)/shard_map/convert_element_type | solution.py:992
  22.0 1.9 reshape.429
  23.9 1.8 copy.69
  25.9 1.9 multiply_sine_fusion.1
  30.2 2.0 multiply_reduce_fusion.8
  33.1 30.5 %all-gather.2.cloned.1.call-done = bf16[768,16384]{1,0:T(8,128)(2,1)} async-done(((bf16[768,8192]{1,0:T(8,128)(2,1)}), bf16[768,16384]{1,0:T(8,128)(2,1)}) %all-gather.2.cloned.1.call-update) | async-done | bytes 25165840 | tf_op jit(solution)/shard_map/all_gather | solution.py:992
  67.0 3.0 fusion.84
  70.0 2.1 fusion.59
  72.1 4.1 fusion.16
  77.1 6.6 %add_convert_fusion = bf16[1024,2304]{1,0:T(8,128)(2,1)S(1)} fusion(bf16[1024,768]{1,0:T(8,128)(2,1)S(1)} %fusion.42, f32[2304]{0:T(1024)S(1)} %pad_maximum_fusion.1, bf16[768,16384]{1,0:T(8,128)(2,1)} %all-gather.2.cloned.1.call-done), kind=kOutput, calls=%fused_computation.16 | convolution fusion | flops 3628597248 | bytes 9839616 | tf_op jit(solution)/shard_map/dot_general | solution.py:30
  83.8 2.3 fusion.143
  86.1 2.6 copy.62
  88.6 3.9 reshape.426
  92.5 2.6 copy.63
  95.1 3.9 reshape.427
  98.9 2.6 copy.61
  101.5 4.1 reshape.425
  105.6 3.8 multiply_reduce_fusion.1
  109.3 2.7 exponential_reduce_fusion
  112.1 2.0 copy-done
  114.1 2.4 fusion.68
  118.1 6.3 %fusion.141 = (f32[1024]{0:T(1024)S(1)}, f32[1024,768]{1,0:T(8,128)}, f32[1024,768]{1,0:T(8,128)}) fusion(f32[4,768]{1,0:T(4,128)S(1)} %get-tuple-element.111, f32[256,768]{1,0:T(8,128)S(1)} %copy-done.6, f32[1024,768]{1,0:T(8,128)S(1)} %get-tuple-element.89, f32[768]{0:T(1024)S(1)} %get-tuple-element.69, f32[768]{0:T(1024)S(1)} %get-tuple-element.64, ...), kind=kOutput, calls=%fused_computation.260 | convolution fusion | flops 1212677120 | bytes 12998656 | tf_op jit(solution)/shard_map/dot_general | solution.py:30
  124.5 2.5 multiply_reduce_fusion.7
  128.0 10.9 %fusion.28 = f32[1024,3072]{1,0:T(8,128)} fusion(bf16[1024,768]{1,0:T(8,128)(2,1)S(1)} %fusion.46, bf16[768,16384]{1,0:T(8,128)(2,1)} %all-gather.2.cloned.1.call-done), kind=kOutput, calls=%fused_computation.53 | convolution fusion | flops 4831838208 | bytes 18874368 | tf_op jit(solution)/shard_map/dot_general | solution.py:30
  138.9 14.1 %fusion.139 = (f32[1024]{0:T(1024)S(1)}, f32[1024,768]{1,0:T(8,128)}, f32[1024,768]{1,0:T(8,128)}) fusion(f32[1024,768]{1,0:T(8,128)S(1)} %copy-done.1, f32[4,768]{1,0:T(4,128)S(1)} %get-tuple-element.116, f32[768]{0:T(1024)S(1)} %get-tuple-element.63, bf16[768,16384]{1,0:T(8,128)(2,1)} %all-gather.2.cloned.1.call-done, f32[1024,3072]{1,0:T(8,128)} %fusion.28, ...), kind=kOutput, calls=%fused_computation.259 | convolution fusion | flops 4866440192 | bytes 26770432 | tf_op jit(solution)/shard_map/dot_general | solution.py:34
  153.0 2.5 multiply_reduce_fusion.6
  156.5 2.0 multiply_reduce_fusion.9
  158.5 3.2 multiply_reduce_fusion.5
  161.7 4.6 fusion.138
  166.3 2.9 convert_reduce_fusion.2
  169.3 16.5 %convert_reduce_fusion = (f32[3072]{0:T(1024)S(1)}, bf16[1024,3072]{1,0:T(8,128)(2,1)S(1)}) fusion(f32[1024,3072]{1,0:T(8,128)} %fusion.28, f32[3072]{0:T(1024)S(1)} %slice.113, bf16[1024,768]{1,0:T(8,128)(2,1)S(1)} %get-tuple-element.38, bf16[768,16384]{1,0:T(8,128)(2,1)} %all-gather.2.cloned.1.call-done), kind=kOutput, calls=%fused_computation.9 | convolution fusion | flops 4904186880 | bytes 25190400 | tf_op jit(solution)/shard_map/dot_general | solution.py:30
  185.8 11.6 %multiply_reduce_fusion.4 = (f32[1024]{0:T(1024)S(1)}, f32[1024,768]{1,0:T(8,128)}) fusion(f32[1024,768]{1,0:T(8,128)S(1)} %copy-done.2, f32[4,768]{1,0:T(4,128)S(1)} %get-tuple-element.114, f32[1024]{0:T(1024)S(1)} %broadcast_multiply_fusion.1, bf16[1024,3072]{1,0:T(8,128)(2,1)S(1)} %get-tuple-element.103, bf16[768,16384]{1,0:T(8,128)(2,1)} %all-gather.2.cloned.1.call-done), kind=kOutput, calls=%fused_computation.98 | convolution fusion | flops 4834982912 | bytes 17321984 | tf_op jit(solution)/shard_map/dot_general | solution.py:34
  197.4 4.6 fusion.137
  202.0 3.5 convert_reduce_fusion.3
  206.6 3.8 convolution_convert_fusion.7
  210.5 2.6 copy.70
  213.1 4.2 reshape.430
  217.3 8.7 %fusion.69 = bf16[4,256,12,64]{1,3,2,0:T(8,128)(2,1)} fusion(bf16[4,256,12,64]{1,0,3,2:T(4,128)(2,1)} %reshape.430, f32[4,12,256,256]{2,3,1,0:T(8,128)} %copy-done, f32[4,12,256]{2,1,0:T(8,128)S(1)} %log_add_fusion), kind=kOutput, calls=%fused_computation.125 | convolution fusion | flops 412876800 | bytes 15777792 | tf_op jit(solution)/shard_map/nhqk,nqhd->nkhd/dot_general | solution.py:321
  226.1 10.3 %multiply_reduce_fusion = (f32[4,12,256]{2,1,0:T(8,128)S(1)}, f32[4,12,256,256]{2,3,1,0:T(8,128)}) fusion(f32[4,12,256,256]{2,3,1,0:T(8,128)} %copy-done, f32[4,12,256]{2,1,0:T(8,128)S(1)} %log_add_fusion, bf16[4,256,12,64]{1,0,3,2:T(4,128)(2,1)S(1)} %copy-done.17, bf16[4,256,12,64]{1,0,3,2:T(4,128)(2,1)S(1)} %copy-done.18), kind=kOutput, calls=%fused_computation.11 | convolution fusion | flops 415223808 | bytes 28409856 | tf_op jit(solution)/shard_map/nqhd,nkhd->nhqk/dot_general | solution.py:324
  236.8 7.2 %multiply_convert_fusion = bf16[4,12,256,256]{2,3,1,0:T(8,128)(2,1)S(1)} fusion(f32[4,12,256,256]{2,3,1,0:T(8,128)} %get-tuple-element.99, f32[4,12,256,256]{2,3,1,0:T(8,128)S(1)} %bitcast.217, f32[4,12,256]{2,1,0:T(8,128)S(1)} %get-tuple-element.98, f32[4,12,256]{2,1,0:T(8,128)S(1)} %log_add_fusion), kind=kLoop, calls=%fused_computation.10 | loop fusion | flops 15728640 | bytes 31555584 | tf_op jit(solution)/shard_map/convert_element_type | solution.py:329
  244.0 3.2 fusion.71
  247.2 2.2 fusion.70
  249.4 2.8 copy.81
  257.6 5.6 %fusion.21 = bf16[768,16384]{1,0:T(8,128)(2,1)} fusion(bf16[1024,768]{1,0:T(8,128)(2,1)S(1)} %copy-done.36, bf16[1024,2304]{0,1:T(8,128)(2,1)S(1)} %constant_dynamic-update-slice_fusion), kind=kOutput, calls=%fused_computation.31 | convolution fusion | flops 3625648128 | bytes 9830400 | tf_op jit(solution)/shard_map/dot_general | solution.py:40
  263.2 6.9 %multiply_reduce_fusion.3 = (f32[1024]{0:T(1024)S(1)}, f32[1024,768]{1,0:T(8,128)S(1)}) fusion(f32[4,768]{1,0:T(4,128)S(1)} %get-tuple-element.112, f32[1024]{0:T(1024)S(1)} %broadcast_multiply_fusion.2, f32[256,768]{1,0:T(8,128)S(1)} %copy-done.7, f32[1024,768]{1,0:T(8,128)S(1)} %get-tuple-element.89, f32[768]{0:T(1024)S(1)} %get-tuple-element.69, ...), kind=kOutput, calls=%fused_computation.94 | convolution fusion | flops 3628596224 | bytes 15358976 | tf_op jit(solution)/shard_map/dot_general | solution.py:34
  270.2 2.5 fusion.49
  274.3 2.4 fusion.66
  276.7 9.7 %fusion.20 = bf16[768,16384]{1,0:T(8,128)(2,1)} fusion(bf16[768,16384]{1,0:T(8,128)(2,1)} %fusion.66, bf16[1024,768]{1,0:T(8,128)(2,1)S(1)} %copy-done.38, bf16[1024,3072]{1,0:T(8,128)(2,1)} %copy-done.70), kind=kOutput, calls=%fused_computation.29 | convolution fusion | flops 4834197504 | bytes 12582912 | tf_op jit(solution)/shard_map/dot_general | solution.py:40
  286.5 9.0 %fusion.19 = bf16[768,16384]{1,0:T(8,128)(2,1)} fusion(bf16[768,16384]{1,0:T(8,128)(2,1)} %fusion.20, bf16[1024,768]{1,0:T(8,128)(2,1)} %copy-done.39, f32[1024,3072]{1,0:T(8,128)S(1)} %bitcast.225, f32[3072]{0:T(1024)S(1)} %slice.113), kind=kOutput, calls=%fused_computation.27 | convolution fusion | flops 4865654784 | bytes 18886656 | tf_op jit(solution)/shard_map/dot_general | solution.py:40
  295.5 5.5 %multiply_reduce_fusion.2 = (bf16[4,768]{1,0:T(4,128)(2,1)S(1)}, bf16[4,768]{1,0:T(4,128)(2,1)S(1)}, bf16[4,768]{1,0:T(4,128)(2,1)S(1)}, bf16[4,768]{1,0:T(4,128...) fusion(f32[1024,768]{1,0:T(8,128)S(1)} %copy-done.26, f32[4,256]{1,0:T(4,128)S(1)} %div.173, ...), kind=kLoop, calls=%fused_computation.86 | loop fusion | flops 22788096 | bytes 15835136 | tf_op jit(solution)/shard_map/reduce_sum | solution.py:290
  301.2 5.0 fusion.7
  306.2 2.2 fusion.32
  308.4 4.9 fusion.9
  313.4 2.4 convert_reduce_fusion.11
  320.2 17.4 %constant_dynamic-slice_fusion = (bf16[768,8192]{1,0:T(8,128)(2,1)}, bf16[768,8192]{1,0:T(8,128)(2,1)}) fusion(bf16[768,16384]{1,0:T(8,128)(2,1)} %fusion.82, s32[]{:T(128)S(6)} %select_n.33, s32[]{:T(128)S(6)} %select_n.32), kind=kLoop, calls=%fused_computation.245 | loop fusion | bytes 50331656 | tf_op jit(solution)/shard_map/dynamic_slice | solution.py:1006
  340.2 3.4 fusion.133
  344.5 3.4 convert_reduce_fusion.1
  350.2 23.1 %small_sums.1 = (f32[2,16,16,128]{3,2,1,0:T(8,128)S(1)}, f32[2,16,32,128]{3,2,1,0:T(8,128)S(1)}) custom-call(f32[2,16,16,128]{3,2,1,0:T(8,128)S(1)} %bitcast.212, f32[32,128]{1,0:T(8,128)S(1)} %select_maximum_fusion.rows_ref), custom_call_target="tpu_custom_call" | custom-call | tf_op jit(solution)/shard_map/small_sums/pallas_call | solution.py:608
  379.5 2.4 fusion.97
  383.3 6.1 %multiply_subtract_fusion = (f32[768,1032]{0,1:T(8,128)}, f32[768,1032]{0,1:T(8,128)}) fusion(f32[768,1032]{0,1:T(8,128)S(1)} %copy-done.15, f32[]{:T(128)} %bitcast.37, f32[16,768]{1,0:T(8,128)S(1)} %copy-done.48, f32[1000,768]{1,0:T(8,128)S(1)} %fusion.97, f32[16,768]{1,0:T(8,128)S(1)} %reshape.445, f32[768,1032]{0,1:T(8,128)} %param.22), kind=kLoop, calls=%fused_computation.59 | loop fusion | flops 4755456 | bytes 15851524 | tf_op jit(solution)/shard_map/sub | solution.py:1047
  389.3 81.2 %compress.1 = (f32[768,8192]{1,0:T(8,128)}, f32[768,8192]{1,0:T(8,128)}, f32[1,768,8192]{2,1,0:T(8,128)}, f32[8,8192]{1,0:T(8,128)}) custom-call(f32[2]{0:T(128)} %rates_ref.1, bf16[768,8192]{1,0:T(8,128)(2,1)} %get-tuple-element.50.own_hbm, bf16[768,8192]{1,0:T(8,128)(2,1)} %collective-permute-done.recv_hbm, f32[1,768,8192]{2,1,0:T(8,128)} %error_hbm.1, ...), custom_call_target="tpu_custom_call" | custom-call | tf_op jit(solution)/shard_map/compress/pallas_call | solution.py:930
  470.6 19.5 %copy.138 = f32[768,8192]{1,0:T(8,128)} copy(f32[768,8192]{1,0:T(8,128)} %get-tuple-element.127) | data formatting | bytes 50331648
  490.1 19.5 %copy.139 = f32[768,8192]{1,0:T(8,128)} copy(f32[768,8192]{1,0:T(8,128)} %get-tuple-element.128) | data formatting | bytes 50331648
  509.9 8.9 %copy.140 = f32[1,768,8192]{2,1,0:T(8,128)} copy(f32[1,768,8192]{2,1,0:T(8,128)S(1)} %bitcast.219) | data formatting | bytes 50331648
  (263 shorter events, 39.3 us)
Async XLA Ops:
  7.2 56.4 %all-gather.2.cloned.1.call-start = ((), (), s32[]{:S(2)}) async-start(), calls=%async_computation | async-start | bytes 37748736 | tf_op jit(solution)/shard_map/all_gather | solution.py:992
  20.4 5.4 %copy-start.14 = (f32[768,1032]{0,1:T(8,128)S(1)}, f32[768,1032]{0,1:T(8,128)}, u32[]{:S(2)}) copy-start(f32[768,1032]{0,1:T(8,128)} %param.21) | copy-start | bytes 9510916
  22.0 6.1 %copy-start.32 = (bf16[1024,16]{1,0:T(8,128)(2,1)}, bf16[1024,16]{1,0:T(8,128)(2,1)S(1)}, u32[]{:S(2)}) copy-start(bf16[1024,16]{1,0:T(8,128)(2,1)S(1)} %reshape.424) | copy-start | bytes 98308
  25.9 3.7 copy-start.34
  29.0 3.9 copy-start.67
  29.6 37.3 %copy-start.65 = (s32[4]{0:T(128)S(1)}, s32[4]{0:T(128)}, u32[]{:S(2)}) copy-start(s32[4]{0:T(128)} %param.16) | copy-start | bytes 52
  32.3 39.8 %copy-start.54 = (f32[1024]{0:T(1024)}, f32[1024]{0:T(1024)S(1)}, u32[]{:S(2)}) copy-start(f32[1024]{0:T(1024)S(1)} %multiply_reduce_fusion.8) | copy-start | bytes 12292
  32.3 43.9 %copy-start.49 = (f32[1024]{0:T(1024)}, f32[1024]{0:T(1024)S(1)}, u32[]{:S(2)}) copy-start(f32[1024]{0:T(1024)S(1)} %fusion.118) | copy-start | bytes 12292
  33.0 31.7 %copy-start.60 = (bf16[4,128]{1,0:T(4,128)(2,1)}, bf16[4,128]{1,0:T(4,128)(2,1)S(1)}, u32[]{:S(2)}) copy-start(bf16[4,128]{1,0:T(4,128)(2,1)S(1)} %get-tuple-element.86) | copy-start | bytes 3076
  33.1 31.7 %copy-start.62 = (bf16[4,128]{1,0:T(4,128)(2,1)}, bf16[4,128]{1,0:T(4,128)(2,1)S(1)}, u32[]{:S(2)}) copy-start(bf16[4,128]{1,0:T(4,128)(2,1)S(1)} %get-tuple-element.87) | copy-start | bytes 3076
  65.4 6.6 %slice-start.12 = ((f32[14608]{0:T(1024)}), f32[4608]{0:T(1024)S(1)}, s32[]{:S(2)}) async-start(f32[14608]{0:T(1024)} %param.23), calls=%async_computation.13 | async-start | bytes 40960 | tf_op jit(solution)/shard_map/slice | solution.py:88
  70.0 6.2 %copy-start.44 = (f32[4,768]{1,0:T(4,128)}, f32[4,768]{1,0:T(4,128)S(1)}, u32[]{:S(2)}) copy-start(f32[4,768]{1,0:T(4,128)S(1)} %fusion.84) | copy-start | bytes 36868
  72.0 4.2 copy-start.5
  77.1 6.7 %copy-start.35 = (bf16[1024,768]{1,0:T(8,128)(2,1)}, bf16[1024,768]{1,0:T(8,128)(2,1)S(1)}, u32[]{:S(2)}) copy-start(bf16[1024,768]{1,0:T(8,128)(2,1)S(1)} %fusion.42) | copy-start | bytes 4718596
  109.3 4.8 copy-start
  109.3 4.8 copy-start.16
  118.1 6.3 %copy-start.30 = (bf16[96,8,4,256]{3,1,2,0:T(8,128)(2,1)}, bf16[96,8,4,256]{3,1,2,0:T(8,128)(2,1)S(1)}, u32[]{:S(2)}) copy-start(bf16[96,8,4,256]{3,1,2,0:T(8,128)(2,1)S(1)} %copy.92) | copy-start | bytes 4718596
  128.0 10.9 %copy-start.37 = (bf16[1024,768]{1,0:T(8,128)(2,1)}, bf16[1024,768]{1,0:T(8,128)(2,1)S(1)}, u32[]{:S(2)}) copy-start(bf16[1024,768]{1,0:T(8,128)(2,1)S(1)} %fusion.46) | copy-start | bytes 4718596
  156.5 5.2 copy-start.24
  169.3 16.5 %copy-start.39 = (bf16[1024,768]{1,0:T(8,128)(2,1)}, bf16[1024,768]{1,0:T(8,128)(2,1)S(1)}, u32[]{:S(2)}) copy-start(bf16[1024,768]{1,0:T(8,128)(2,1)S(1)} %get-tuple-element.38) | copy-start | bytes 4718596
  169.3 16.5 %copy-start.2 = (f32[1024,768]{1,0:T(8,128)S(1)}, f32[1024,768]{1,0:T(8,128)}, u32[]{:S(2)}) copy-start(f32[1024,768]{1,0:T(8,128)} %get-tuple-element.48) | copy-start | bytes 9437188
  185.7 11.6 %copy-start.70 = (bf16[1024,3072]{1,0:T(8,128)(2,1)}, bf16[1024,3072]{1,0:T(8,128)(2,1)S(1)}, u32[]{:S(2)}) copy-start(bf16[1024,3072]{1,0:T(8,128)(2,1)S(1)} %get-tuple-element.103) | copy-start | bytes 18874372
  217.3 8.7 %copy-start.17 = (bf16[4,256,12,64]{1,0,3,2:T(4,128)(2,1)S(1)}, bf16[4,256,12,64]{1,0,3,2:T(4,128)(2,1)}, u32[]{:S(2)}) copy-start(bf16[4,256,12,64]{1,0,3,2:T(4,128)(2,1)} %reshape.425) | copy-start | bytes 4718596
  217.3 8.7 %copy-start.18 = (bf16[4,256,12,64]{1,0,3,2:T(4,128)(2,1)S(1)}, bf16[4,256,12,64]{1,0,3,2:T(4,128)(2,1)}, u32[]{:S(2)}) copy-start(bf16[4,256,12,64]{1,0,3,2:T(4,128)(2,1)} %reshape.430) | copy-start | bytes 4718596
  217.3 19.1 %slice-start = ((s8[12582912]{0:T(1024)(128)(4,1)}), s8[4194304]{0:T(1024)(128)(4,1)S(1)}, s32[]{:S(2)}) async-start(s8[12582912]{0:T(1024)(128)(4,1)} %bitcast.216), calls=%async_computation.1 | async-start | bytes 8388608
  226.1 10.4 %slice-start.1 = ((s8[12582912]{0:T(1024)(128)(4,1)}), s8[4194304]{0:T(1024)(128)(4,1)S(1)}, s32[]{:S(2)}) async-start(s8[12582912]{0:T(1024)(128)(4,1)} %bitcast.216), calls=%async_computation.2 | async-start | bytes 8388608
  226.1 10.7 %slice-start.2 = ((s8[12582912]{0:T(1024)(128)(4,1)}), s8[4194304]{0:T(1024)(128)(4,1)S(1)}, s32[]{:S(2)}) async-start(s8[12582912]{0:T(1024)(128)(4,1)} %bitcast.216), calls=%async_computation.3 | async-start | bytes 8388608
  236.8 7.2 %copy-start.19 = (bf16[4,256,12,64]{1,0,3,2:T(4,128)(2,1)S(1)}, bf16[4,256,12,64]{1,0,3,2:T(4,128)(2,1)}, u32[]{:S(2)}) copy-start(bf16[4,256,12,64]{1,0,3,2:T(4,128)(2,1)} %reshape.426) | copy-start | bytes 4718596
  244.0 3.2 copy-start.25
  252.5 3.9 copy-start.20
  257.6 5.6 %copy-start.7 = (f32[256,768]{1,0:T(8,128)S(1)}, f32[256,768]{1,0:T(8,128)}, u32[]{:S(2)}) copy-start(f32[256,768]{1,0:T(8,128)} %copy-done.4) | copy-start | bytes 2359300
  263.2 7.0 %copy-start.13 = (f32[1024,768]{1,0:T(8,128)S(1)}, f32[1024,768]{1,0:T(8,128)}, u32[]{:S(2)}) copy-start(f32[1024,768]{1,0:T(8,128)} %get-tuple-element.92) | copy-start | bytes 9437188
  263.2 7.0 %copy-start.57 = (f32[4,256]{1,0:T(4,128)S(1)}, f32[4,256]{1,0:T(4,128)}, u32[]{:S(2)}) copy-start(f32[4,256]{1,0:T(4,128)} %div.169) | copy-start | bytes 12292
  263.2 7.0 %copy-start.58 = (f32[4,256]{1,0:T(4,128)S(1)}, f32[4,256]{1,0:T(4,128)}, u32[]{:S(2)}) copy-start(f32[4,256]{1,0:T(4,128)} %rsqrt.52) | copy-start | bytes 12292
  270.2 4.1 copy-start.41
  274.3 12.1 %slice-start.9 = ((s8[12582912]{0:T(1024)(128)(4,1)}), s8[4194304]{0:T(1024)(128)(4,1)S(1)}, s32[]{:S(2)}) async-start(s8[12582912]{0:T(1024)(128)(4,1)} %bitcast.224), calls=%async_computation.10 | async-start | bytes 8388608
  276.7 9.7 %slice-start.10 = ((s8[12582912]{0:T(1024)(128)(4,1)}), s8[4194304]{0:T(1024)(128)(4,1)S(1)}, s32[]{:S(2)}) async-start(s8[12582912]{0:T(1024)(128)(4,1)} %bitcast.224), calls=%async_computation.11 | async-start | bytes 8388608
  276.7 9.7 %slice-start.11 = ((s8[12582912]{0:T(1024)(128)(4,1)}), s8[4194304]{0:T(1024)(128)(4,1)S(1)}, s32[]{:S(2)}) async-start(s8[12582912]{0:T(1024)(128)(4,1)} %bitcast.224), calls=%async_computation.12 | async-start | bytes 8388608
  286.4 9.1 %copy-start.12 = (f32[1024,768]{1,0:T(8,128)S(1)}, f32[1024,768]{1,0:T(8,128)}, u32[]{:S(2)}) copy-start(f32[1024,768]{1,0:T(8,128)} %get-tuple-element.95) | copy-start | bytes 9437188
  286.4 9.1 %copy-start.26 = (f32[1024,768]{1,0:T(8,128)S(1)}, f32[1024,768]{1,0:T(8,128)}, u32[]{:S(2)}) copy-start(f32[1024,768]{1,0:T(8,128)} %get-tuple-element.93) | copy-start | bytes 9437188
  286.4 9.1 %copy-start.27 = (f32[1024,768]{1,0:T(8,128)S(1)}, f32[1024,768]{1,0:T(8,128)}, u32[]{:S(2)}) copy-start(f32[1024,768]{1,0:T(8,128)} %get-tuple-element.97) | copy-start | bytes 9437188
  295.5 5.6 %copy-start.45 = (f32[4,768]{1,0:T(4,128)S(1)}, f32[4,768]{1,0:T(4,128)}, u32[]{:S(2)}) copy-start(f32[4,768]{1,0:T(4,128)} %copy-done.44) | copy-start | bytes 36868
  308.4 7.4 %copy-start.53 = (f32[4,768]{1,0:T(4,128)S(1)}, f32[4,768]{1,0:T(4,128)}, u32[]{:S(2)}) copy-start(f32[4,768]{1,0:T(4,128)} %copy-done.52) | copy-start | bytes 36868
  313.3 5.7 %copy-start.61 = (bf16[4,128]{1,0:T(4,128)(2,1)S(1)}, bf16[4,128]{1,0:T(4,128)(2,1)}, u32[]{:S(2)}) copy-start(bf16[4,128]{1,0:T(4,128)(2,1)} %copy-done.60) | copy-start | bytes 3076
  313.3 5.8 %copy-start.63 = (bf16[4,128]{1,0:T(4,128)(2,1)S(1)}, bf16[4,128]{1,0:T(4,128)(2,1)}, u32[]{:S(2)}) copy-start(bf16[4,128]{1,0:T(4,128)(2,1)} %copy-done.62) | copy-start | bytes 3076
  320.2 17.6 %copy-start.68 = (f32[2]{0:T(128)S(1)}, f32[2]{0:T(128)}, u32[]{:S(2)}) copy-start(f32[2]{0:T(128)} %rates_ref.1) | copy-start | bytes 28
  320.2 18.2 %copy-start.66 = (s32[4]{0:T(128)S(1)}, s32[4]{0:T(128)}, u32[]{:S(2)}) copy-start(s32[4]{0:T(128)} %param.16) | copy-start | bytes 52
  320.2 20.0 %copy-start.55 = (f32[1024]{0:T(1024)S(1)}, f32[1024]{0:T(1024)}, u32[]{:S(2)}) copy-start(f32[1024]{0:T(1024)} %copy-done.54) | copy-start | bytes 12292
  320.2 20.0 %copy-start.50 = (f32[1024]{0:T(1024)S(1)}, f32[1024]{0:T(1024)}, u32[]{:S(2)}) copy-start(f32[1024]{0:T(1024)} %copy-done.49) | copy-start | bytes 12292
  337.6 51.8 %collective-permute-start = (bf16[768,8192]{1,0:T(8,128)(2,1)}, bf16[768,8192]{1,0:T(8,128)(2,1)}, u32[]{:S(2)}, u32[]{:S(2)}) collective-permute-start(bf16[768,8192]{1,0:T(8,128)(2,1)} %get-tuple-element.49), channel_id=1, source_target_pairs={{0,16},{16,0},{1,17},{17,1},{2,18},{18,2},{3,19},{19,3},{4,20},{20... | collective-permute-start | bytes 37748744 | tf_op jit(solution)/shard_map/ppermute | solution.py:1005
  340.2 3.5 copy-start.8
  340.2 3.5 copy-start.9
  340.2 4.3 copy-start.11
  344.5 3.5 copy-start.33
  350.2 31.8 %copy-start.43 = (f32[14608]{0:T(1024)S(1)}, f32[14608]{0:T(1024)}, u32[]{:S(2)}) copy-start(f32[14608]{0:T(1024)} %param.23) | copy-start | bytes 175300
  350.2 33.1 %copy-start.15 = (f32[768,1032]{0,1:T(8,128)S(1)}, f32[768,1032]{0,1:T(8,128)}, u32[]{:S(2)}) copy-start(f32[768,1032]{0,1:T(8,128)} %param.21) | copy-start | bytes 9510916
  379.5 3.7 copy-start.48
  470.6 39.0 %slice-start.3 = ((s8[25165824]{0:T(1024)(128)(4,1)}), s8[4194304]{0:T(1024)(128)(4,1)S(1)}, s32[]{:S(2)}) async-start(s8[25165824]{0:T(1024)(128)(4,1)} %bitcast.218), calls=%async_computation.4 | async-start | bytes 8388608
  470.6 39.0 %slice-start.4 = ((s8[25165824]{0:T(1024)(128)(4,1)}), s8[4194304]{0:T(1024)(128)(4,1)S(1)}, s32[]{:S(2)}) async-start(s8[25165824]{0:T(1024)(128)(4,1)} %bitcast.218), calls=%async_computation.5 | async-start | bytes 8388608
  470.6 39.0 %slice-start.5 = ((s8[25165824]{0:T(1024)(128)(4,1)}), s8[4194304]{0:T(1024)(128)(4,1)S(1)}, s32[]{:S(2)}) async-start(s8[25165824]{0:T(1024)(128)(4,1)} %bitcast.218), calls=%async_computation.6 | async-start | bytes 8388608
  490.1 19.5 %slice-start.6 = ((s8[25165824]{0:T(1024)(128)(4,1)}), s8[4194304]{0:T(1024)(128)(4,1)S(1)}, s32[]{:S(2)}) async-start(s8[25165824]{0:T(1024)(128)(4,1)} %bitcast.218), calls=%async_computation.7 | async-start | bytes 8388608
  490.1 19.5 %slice-start.7 = ((s8[25165824]{0:T(1024)(128)(4,1)}), s8[4194304]{0:T(1024)(128)(4,1)S(1)}, s32[]{:S(2)}) async-start(s8[25165824]{0:T(1024)(128)(4,1)} %bitcast.218), calls=%async_computation.8 | async-start | bytes 8388608
  490.1 19.8 %slice-start.8 = ((s8[25165824]{0:T(1024)(128)(4,1)}), s8[4194304]{0:T(1024)(128)(4,1)S(1)}, s32[]{:S(2)}) async-start(s8[25165824]{0:T(1024)(128)(4,1)} %bitcast.218), calls=%async_computation.9 | async-start | bytes 8388608
  509.9 8.9 %copy-start.47 = (f32[8,8192]{1,0:T(8,128)S(1)}, f32[8,8192]{1,0:T(8,128)}, u32[]{:S(2)}) copy-start(f32[8,8192]{1,0:T(8,128)} %get-tuple-element.19) | copy-start | bytes 786436
  (22 other events, 40.8 us)
Sparse Core Ops, SparseCore 0:
  20.5 42.9 all-gather.1

commit v2 on v1

--- a/solution.py
+++ b/solution.py
@@ -625,39 +625,30 @@
 
 
 def tail_kernel(
-    rates_ref,
     own_hbm,
     recv_hbm,
     error_hbm,
     factor_ref,
     moment_hbm,
-    master_hbm,
-    new_master_hbm,
-    new_moment_hbm,
-    new_error_hbm,
-    right_ref,
     m_ref,
     v_ref,
+    whole_ref,
+    basis_cols,
     own_ref,
     recv_ref,
-    master_ref,
     stack_ref,
     left_acc,
     left_ref,
     plane_ref,
     column_ref,
     basis_rows,
-    basis_cols,
     send_ref,
     part_ref,
     mine_ref,
-    whole_ref,
     load_sem,
     own_sem,
     recv_sem,
     moment_sem,
-    master_sem,
-    out_sem,
     left_send,
     left_recv,
     right_send,
@@ -727,17 +718,8 @@
         return carry
 
     lax.fori_loop(0, blocks, gather_block, 0)
-    for block in range(blocks):
+    for block in range(v_ref.shape[0]):
         load_moment(block).start()
-
-    def load_master(block, slot):
-        return pltpu.make_async_copy(
-            master_hbm.at[:, columns(block)], master_ref.at[slot], master_sem.at[slot]
-        )
-
-    slots = master_ref.shape[0]
-    for block in range(slots):
-        load_master(block, block).start()
 
     turned = left_acc[...].T
     left_ref[...] = turned[0:RANK] + turned[RANK : 2 * RANK]
@@ -867,109 +849,593 @@
     for step in range(1, REPS):
         other = lax.rem(rep + step, REPS)
         right_copy(mine_ref, whole_ref.at[other], REPS, step, other).wait_recv()
-
-    def out_error(block):
+    for copy in scatter + spread:
+        copy.wait_send()
+    for block in range(v_ref.shape[0]):
+        load_moment(block).wait()
+
+
+def update_kernel(
+    rates_ref,
+    m_ref,
+    v_ref,
+    whole_ref,
+    basis_cols,
+    moment_hbm,
+    master_hbm,
+    new_master_hbm,
+    new_moment_hbm,
+    new_error_hbm,
+    right_ref,
+    error_ref,
+    moment_ref,
+    master_ref,
+    moment_sem,
+    master_sem,
+    error_out,
+    moment_out,
+    master_out,
+):
+    blocks = m_ref.shape[0]
+    early = v_ref.shape[0]
+    slots = master_ref.shape[0]
+    rate = rates_ref[0]
+
+    def columns(block):
+        return pl.ds(pl.multiple_of(block * BLOCK, BLOCK), BLOCK)
+
+    def load_master(block, slot):
         return pltpu.make_async_copy(
-            m_ref.at[block], new_error_hbm.at[0, :, columns(block)], load_sem.at[block]
-        )
-
-    def out_moment(block):
+            master_hbm.at[:, columns(block)], master_ref.at[slot], master_sem.at[slot]
+        )
+
+    def load_moment(block, slot):
         return pltpu.make_async_copy(
-            v_ref.at[block], new_moment_hbm.at[:, columns(block)], moment_sem.at[block]
+            moment_hbm.at[:, columns(block)], moment_ref.at[slot], moment_sem.at[slot]
+        )
+
+    def out_error(block, slot):
+        return pltpu.make_async_copy(
+            error_ref.at[slot], new_error_hbm.at[0, :, columns(block)], error_out.at[slot]
+        )
+
+    def out_moment(block, slot):
+        return pltpu.make_async_copy(
+            moment_ref.at[slot], new_moment_hbm.at[:, columns(block)], moment_out.at[slot]
         )
 
     def out_master(block, slot):
         return pltpu.make_async_copy(
-            master_ref.at[slot], new_master_hbm.at[:, columns(block)], out_sem.at[slot]
-        )
-
-    rate = rates_ref[0]
+            master_ref.at[slot], new_master_hbm.at[:, columns(block)], master_out.at[slot]
+        )
+
+    ahead = slots - 2
+    for block in range(ahead):
+        load_master(block, block).start()
 
     def update_block(block, carry):
         slot = lax.rem(block, slots)
-
-        @pl.when(jnp.logical_and(block >= 1, block - 1 + slots < blocks))
+        next_slot = lax.rem(block + ahead, slots)
+
+        @pl.when(block >= 2)
         def _():
-            earlier = lax.rem(block - 1, slots)
-            out_master(block - 1, earlier).wait()
-            load_master(block - 1 + slots, earlier).start()
+            out_error(block - 2, next_slot).wait()
+            out_moment(block - 2, next_slot).wait()
+            out_master(block - 2, next_slot).wait()
+
+        @pl.when(block + ahead < blocks)
+        def _():
+            load_master(block + ahead, next_slot).start()
+
+            @pl.when(block + ahead >= early)
+            def _():
+                load_moment(block + ahead, next_slot).start()
 
         right = whole_ref[block]
         right_ref[:, columns(block)] = right.astype(jnp.float32)
-        approx = multiply(
-            basis_cols[:, 0 : 2 * RANK], jnp.concatenate([right, right], axis=0)
-        )
-        m_ref[block] = m_ref[block] - approx * (1.0 / REPS)
-        out_error(block).start()
-        load_moment(block).wait()
-        moment = momentum_decay * v_ref[block] + approx
-        v_ref[block] = moment
-        out_moment(block).start()
+        approx = multiply(basis_cols[:, 0 : 2 * RANK], jnp.concatenate([right, right], axis=0))
+        error_ref[slot] = m_ref[block] - approx * (1.0 / REPS)
+        out_error(block, slot).start()
+
+        @pl.when(block < early)
+        def _():
+            moment_ref[slot] = momentum_decay * v_ref[jnp.minimum(block, early - 1)] + approx
+
+        @pl.when(block >= early)
+        def _():
+            load_moment(block, slot).wait()
+            moment_ref[slot] = momentum_decay * moment_ref[slot] + approx
+
+        out_moment(block, slot).start()
         load_master(block, slot).wait()
-        master_ref[slot] = master_ref[slot] - rate * moment
+        master_ref[slot] = master_ref[slot] - rate * moment_ref[slot]
         out_master(block, slot).start()
         return carry
 
     lax.fori_loop(0, blocks, update_block, 0)
-    for block in range(blocks):
-        out_error(block).wait()
-        out_moment(block).wait()
-    for block in range(blocks - slots, blocks):
+    for block in range(blocks - 2, blocks):
+        out_error(block, block % slots).wait()
+        out_moment(block, block % slots).wait()
         out_master(block, block % slots).wait()
-    for copy in scatter + spread:
-        copy.wait_send()
 
 
 def compress(rates, own, received, error, factor_rows, moment, master):
     rows, cols = own.shape
     blocks = cols // BLOCK
     depth = 3
-    slots = 3
+    slots = 4
     hbm = pl.BlockSpec(memory_space=pl.ANY)
     vmem = pl.BlockSpec(memory_space=pltpu.VMEM)
+    matrices, moments, whole, basis = pl.pallas_call(
+        tail_kernel,
+        out_shape=(
+            pltpu.VMEM((blocks, rows, BLOCK), jnp.float32),
+            pltpu.VMEM((4, rows, BLOCK), jnp.float32),
+            pltpu.VMEM((blocks, RANK, BLOCK), half_type),
+            pltpu.VMEM((rows, LANES), half_type),
+        ),
+        in_specs=[hbm, hbm, hbm, vmem, hbm],
+        out_specs=[vmem] * 4,
+        scratch_shapes=[
+            pltpu.VMEM((depth, rows, BLOCK), half_type),
+            pltpu.VMEM((depth, rows, BLOCK), half_type),
+            pltpu.VMEM((LANES, cols), half_type),
+            pltpu.VMEM((rows, LANES), jnp.float32),
+            pltpu.VMEM((RANK, rows), jnp.float32),
+            pltpu.VMEM((4, RANK, rows), jnp.float32),
+            pltpu.VMEM((4, RANK, rows), jnp.float32),
+            pltpu.VMEM((2 * RANK, rows), half_type),
+            pltpu.VMEM((blocks, RANK, BLOCK), half_type),
+            pltpu.VMEM((blocks, RANK, BLOCK), half_type),
+            pltpu.VMEM((RANK, BLOCK), half_type),
+            pltpu.SemaphoreType.DMA((blocks,)),
+            pltpu.SemaphoreType.DMA((depth,)),
+            pltpu.SemaphoreType.DMA((depth,)),
+            pltpu.SemaphoreType.DMA((blocks,)),
+            pltpu.SemaphoreType.DMA((8,)),
+            pltpu.SemaphoreType.DMA((8,)),
+            pltpu.SemaphoreType.DMA((2 * REPS,)),
+            pltpu.SemaphoreType.DMA((2 * REPS,)),
+        ],
+        compiler_params=pltpu.CompilerParams(
+            collective_id=2, has_side_effects=True, vmem_limit_bytes=14_000_000
+        ),
+        name="compress",
+    )(own, received, error, factor_rows, moment)
     return pl.pallas_call(
-        tail_kernel,
+        update_kernel,
         out_shape=(
             sds(master.shape),
             sds(moment.shape),
             sds(error.shape),
             sds((RANK, cols)),
         ),
-        in_specs=[pl.BlockSpec(memory_space=pltpu.SMEM), hbm, hbm, hbm, vmem, hbm, hbm],
+        in_specs=[pl.BlockSpec(memory_space=pltpu.SMEM), vmem, vmem, vmem, vmem, hbm, hbm],
         out_specs=[hbm, hbm, hbm, vmem],
         scratch_shapes=[
-            pltpu.VMEM((blocks, rows, BLOCK), jnp.float32),
-            pltpu.VMEM((blocks, rows, BLOCK), jnp.float32),
-            pltpu.VMEM((depth, rows, BLOCK), half_type),
-            pltpu.VMEM((depth, rows, BLOCK), half_type),
             pltpu.VMEM((slots, rows, BLOCK), jnp.float32),
-            pltpu.VMEM((LANES, cols), half_type),
-            pltpu.VMEM((rows, LANES), jnp.float32),
-            pltpu.VMEM((RANK, rows), jnp.float32),
-            pltpu.VMEM((4, RANK, rows), jnp.float32),
-            pltpu.VMEM((4, RANK, rows), jnp.float32),
-            pltpu.VMEM((2 * RANK, rows), half_type),
-            pltpu.VMEM((rows, LANES), half_type),
-            pltpu.VMEM((blocks, RANK, BLOCK), half_type),
-            pltpu.VMEM((blocks, RANK, BLOCK), half_type),
-            pltpu.VMEM((RANK, BLOCK), half_type),
-            pltpu.VMEM((blocks, RANK, BLOCK), half_type),
-            pltpu.SemaphoreType.DMA((blocks,)),
-            pltpu.SemaphoreType.DMA((depth,)),
-            pltpu.SemaphoreType.DMA((depth,)),
-            pltpu.SemaphoreType.DMA((blocks,)),
+            pltpu.VMEM((slots, rows, BLOCK), jnp.float32),
+            pltpu.VMEM((slots, rows, BLOCK), jnp.float32),
             pltpu.SemaphoreType.DMA((slots,)),
             pltpu.SemaphoreType.DMA((slots,)),
-            pltpu.SemaphoreType.DMA((8,)),
-            pltpu.SemaphoreType.DMA((8,)),
-            pltpu.SemaphoreType.DMA((2 * REPS,)),
-            pltpu.SemaphoreType.DMA((2 * REPS,)),
+            pltpu.SemaphoreType.DMA((slots,)),
+            pltpu.SemaphoreType.DMA((slots,)),
+            pltpu.SemaphoreType.DMA((slots,)),
         ],
-        compiler_params=pltpu.CompilerParams(
-            collective_id=2, has_side_effects=True, vmem_limit_bytes=67_000_000
-        ),
-        name="compress",
-    )(rates, own, received, error, factor_rows, moment, master)
+        compiler_params=pltpu.CompilerParams(vmem_limit_bytes=24500000),
+        name="update",
+    )(rates, matrices, moments, whole, basis, moment, master)
+
+
+GROUP = 2 * HEAD_DIM
+CHUNK = 768
+
+
+def unit_rows(values):
+    center = values - jnp.mean(values, axis=-1, keepdims=True)
+    inverse = lax.rsqrt(jnp.mean(center * center, axis=-1, keepdims=True) + epsilon)
+    return center * inverse, inverse
+
+
+def unit_back(unit, inverse, grad):
+    return inverse * (
+        grad
+        - jnp.mean(grad, axis=-1, keepdims=True)
+        - unit * jnp.mean(grad * unit, axis=-1, keepdims=True)
+    )
+
+
+def gelu_both(values):
+    scale = math.sqrt(2.0 / math.pi)
+    square = values * values
+    bent = jnp.tanh(scale * (values + 0.044715 * (values * square)))
+    half = 0.5 * (1.0 + bent)
+    slope = half + 0.5 * values * (1.0 - bent * bent) * (scale * (1.0 + 0.134145 * square))
+    return values * half, slope
+
+
+def token_sum(values):
+    return jnp.sum(values, axis=0, keepdims=True)
+
+
+def image_kernel(
+    entries,
+    patches_ref,
+    targets_ref,
+    mods_ref,
+    place_ref,
+    patch_weight_ref,
+    head_weight_ref,
+    qkv_bias_ref,
+    output_bias_ref,
+    up_bias_ref,
+    down_bias_ref,
+    patch_bias_ref,
+    head_bias_ref,
+    weights_hbm,
+    attn_in_ref,
+    mixed_ref,
+    mlp_in_ref,
+    hidden_ref,
+    grad_qkv_ref,
+    grad_attn_ref,
+    grad_pre_ref,
+    grad_mlp_ref,
+    mod_grad_ref,
+    grad_patch_ref,
+    grad_head_ref,
+    bias_qkv_ref,
+    bias_output_ref,
+    bias_up_ref,
+    bias_down_ref,
+    bias_patch_ref,
+    bias_head_ref,
+    loss_ref,
+    weight_ref,
+    qkv_ref,
+    probs_ref,
+    slope_ref,
+    unit_start_ref,
+    unit_mid_ref,
+    stream_ref,
+    attended_ref,
+    mlp_out_ref,
+    grad_mixed_ref,
+    total_ref,
+    sem,
+):
+    image = pl.program_id(0)
+    edges = [0, 3 * D, 4 * D, 4 * D + FF, 4 * D + 2 * FF]
+
+    def load(part):
+        span = slice(edges[part], edges[part + 1])
+        return pltpu.make_async_copy(weights_hbm.at[:, span], weight_ref.at[:, span], sem.at[part])
+
+    sums = [
+        grad_patch_ref,
+        grad_head_ref,
+        bias_qkv_ref,
+        bias_output_ref,
+        bias_up_ref,
+        bias_down_ref,
+        bias_patch_ref,
+        bias_head_ref,
+        loss_ref,
+    ]
+
+    @pl.when(image == 0)
+    def _():
+        for part in range(4):
+            load(part).start()
+        for total in sums:
+            total[...] = jnp.zeros_like(total)
+
+    def arrived(part):
+        @pl.when(image == 0)
+        def _():
+            load(part).wait()
+
+    def modulation(place):
+        return mods_ref[0, place : place + 1, :]
+
+    def weight(first, width):
+        return weight_ref[:, pl.ds(first, width)]
+
+    patches = patches_ref[...]
+    start = multiply(patches, patch_weight_ref[...]) + patch_bias_ref[...] + place_ref[...]
+    stream_ref[...] = start
+    unit, inverse_start = unit_rows(start)
+    unit_start_ref[...] = unit
+    attn_in_ref[...] = (unit * (1.0 + modulation(1)) + modulation(0)).astype(half_type)
+    arrived(0)
+    for part in range(3):
+        span = slice(part * D, (part + 1) * D)
+        qkv_ref[:, span] = (
+            multiply(attn_in_ref[...], weight_ref[:, span]) + qkv_bias_ref[:, span]
+        ).astype(half_type)
+
+    scale = 1.0 / math.sqrt(HEAD_DIM)
+    first_half = lax.broadcasted_iota(jnp.int32, (1, GROUP), 1) < HEAD_DIM
+
+    def pair_slice(ref, part, pair):
+        return ref[:, pl.ds(pl.multiple_of(part * D + pair * GROUP, GROUP), GROUP)]
+
+    def halves(values):
+        nothing = jnp.zeros_like(values)
+        return jnp.where(first_half, values, nothing), jnp.where(first_half, nothing, values)
+
+    def attend(pair, carry):
+        queries = pair_slice(qkv_ref, 0, pair)
+        keys = halves(pair_slice(qkv_ref, 1, pair))
+        turned = pair_slice(qkv_ref, 2, pair).T
+        rows = []
+        for half in range(2):
+            scores = multiply_trans(keys[half], queries) * scale
+            weights = jnp.exp(scores - jnp.max(scores, axis=0, keepdims=True))
+            probs = weights * (1.0 / jnp.sum(weights, axis=0, keepdims=True))
+            probs_ref[2 * pair + half] = probs
+            rows.append(
+                multiply(
+                    turned[half * HEAD_DIM : (half + 1) * HEAD_DIM], probs.astype(half_type)
+                )
+            )
+        mixed_ref[:, pl.ds(pl.multiple_of(pair * GROUP, GROUP), GROUP)] = (
+            jnp.concatenate(rows, axis=0).T.astype(half_type)
+        )
+        return carry
+
+    lax.fori_loop(0, HEADS // 2, attend, 0)
+    arrived(1)
+    attended = multiply(mixed_ref[...], weight_ref[:, edges[1] : edges[2]]) + output_bias_ref[...]
+    attended_ref[...] = attended
+    middle = stream_ref[...] + modulation(2) * attended
+    stream_ref[...] = middle
+    unit, inverse_mid = unit_rows(middle)
+    unit_mid_ref[...] = unit
+    mlp_in_ref[...] = (unit * (1.0 + modulation(4)) + modulation(3)).astype(half_type)
+    arrived(2)
+    arrived(3)
+    total_ref[...] = jnp.zeros_like(total_ref) + down_bias_ref[...]
+    for part in range(FF // CHUNK):
+        span = slice(part * CHUNK, (part + 1) * CHUNK)
+        before = (
+            multiply(mlp_in_ref[...], weight(edges[2] + part * CHUNK, CHUNK)) + up_bias_ref[:, span]
+        )
+        after, slope_part = gelu_both(before)
+        slope_ref[:, span] = slope_part
+        after = after.astype(half_type)
+        hidden_ref[:, span] = after
+        total_ref[...] += multiply_trans(after, weight(edges[3] + part * CHUNK, CHUNK))
+    mlp_out_ref[...] = total_ref[...]
+    unit, inverse_end = unit_rows(stream_ref[...] + modulation(5) * total_ref[...])
+    final_in = (unit * (1.0 + modulation(7)) + modulation(6)).astype(half_type)
+    error = (
+        multiply_trans(final_in, head_weight_ref[...]) + head_bias_ref[...] - targets_ref[...]
+    )
+    loss_ref[...] += token_sum(error * error)
+    grad_out = (error * (2.0 / entries)).astype(half_type)
+    bias_head_ref[...] += token_sum(grad_out.astype(jnp.float32))
+    grad_head_ref[...] += outer_sum(grad_out, final_in)
+
+    grad_final = multiply(grad_out, head_weight_ref[...])
+    mod_grad_ref[0, 6:7] = token_sum(grad_final)
+    mod_grad_ref[0, 7:8] = token_sum(grad_final * unit)
+    grad_stream = unit_back(unit, inverse_end, grad_final * (1.0 + modulation(7)))
+    stream_ref[...] = grad_stream
+    mod_grad_ref[0, 5:6] = token_sum(grad_stream * mlp_out_ref[...])
+    grad_mlp = (grad_stream * modulation(5)).astype(half_type)
+    grad_mlp_ref[...] = grad_mlp
+    bias_down_ref[...] += token_sum(grad_mlp.astype(jnp.float32))
+    total_ref[...] = jnp.zeros_like(total_ref)
+    for part in range(FF // CHUNK):
+        span = slice(part * CHUNK, (part + 1) * CHUNK)
+        grad_pre = (
+            multiply(grad_mlp_ref[...], weight(edges[3] + part * CHUNK, CHUNK)) * slope_ref[:, span]
+        ).astype(half_type)
+        grad_pre_ref[:, span] = grad_pre
+        bias_up_ref[:, span] += token_sum(grad_pre.astype(jnp.float32))
+        total_ref[...] += multiply_trans(grad_pre, weight(edges[2] + part * CHUNK, CHUNK))
+    grad_in = total_ref[...]
+    unit = unit_mid_ref[...]
+    mod_grad_ref[0, 3:4] = token_sum(grad_in)
+    mod_grad_ref[0, 4:5] = token_sum(grad_in * unit)
+    grad_stream = stream_ref[...] + unit_back(unit, inverse_mid, grad_in * (1.0 + modulation(4)))
+    stream_ref[...] = grad_stream
+    mod_grad_ref[0, 2:3] = token_sum(grad_stream * attended_ref[...])
+    grad_attn = (grad_stream * modulation(2)).astype(half_type)
+    grad_attn_ref[...] = grad_attn
+    bias_output_ref[...] += token_sum(grad_attn.astype(jnp.float32))
+    grad_mixed_ref[...] = multiply_trans(grad_attn, weight_ref[:, edges[1] : edges[2]]).astype(
+        half_type
+    )
+
+    def attend_back(pair, carry):
+        queries = pair_slice(qkv_ref, 0, pair)
+        keys_turned = pair_slice(qkv_ref, 1, pair).T
+        values = halves(pair_slice(qkv_ref, 2, pair))
+        grads = pair_slice(grad_mixed_ref, 0, pair)
+        rows, key_grads, value_grads = [], [], []
+        for half in range(2):
+            probs = probs_ref[2 * pair + half]
+            grad_probs = multiply_trans(values[half], grads)
+            value_grads.append(multiply(probs.astype(half_type), grads))
+            product = probs * grad_probs
+            grad_scores = (product - probs * token_sum(product)).astype(half_type)
+            key_grads.append(multiply(grad_scores, queries))
+            rows.append(
+                multiply(keys_turned[half * HEAD_DIM : (half + 1) * HEAD_DIM], grad_scores)
+            )
+
+        def put(part, values):
+            grad_qkv_ref[:, pl.ds(pl.multiple_of(part * D + pair * GROUP, GROUP), GROUP)] = (
+                values.astype(half_type)
+            )
+
+        put(0, jnp.concatenate(rows, axis=0).T * scale)
+        put(1, jnp.where(first_half, key_grads[0], key_grads[1]) * scale)
+        put(2, jnp.where(first_half, value_grads[0], value_grads[1]))
+        return carry
+
+    lax.fori_loop(0, HEADS // 2, attend_back, 0)
+    bias_qkv_ref[...] += token_sum(grad_qkv_ref[...].astype(jnp.float32))
+    grad_in = multiply_trans(grad_qkv_ref[...], weight_ref[:, : edges[1]])
+    unit = unit_start_ref[...]
+    mod_grad_ref[0, 0:1] = token_sum(grad_in)
+    mod_grad_ref[0, 1:2] = token_sum(grad_in * unit)
+    grad_start = (
+        stream_ref[...] + unit_back(unit, inverse_start, grad_in * (1.0 + modulation(1)))
+    ).astype(half_type)
+    bias_patch_ref[...] += token_sum(grad_start.astype(jnp.float32))
+    grad_patch_ref[...] += outer_sum(patches, grad_start)
+
+
+def run_images(
+    patches, targets, mods, places, patch_weight, head_weight, biases, gathered, entries
+):
+    images = mods.shape[0]
+    tokens = images * SEQ
+    wide = 4 * D + 2 * FF
+
+    def rows(width):
+        return pl.BlockSpec((SEQ, width), lambda image: (image, 0))
+
+    def fixed(array):
+        return pl.BlockSpec(array.shape, lambda image: (0,) * len(array.shape))
+
+    vector = [(P_DIM, D), (P_DIM, D), (1, 3 * D), (1, D), (1, FF), (1, D), (1, D), (1, P_DIM)]
+    vector = [sds(shape) for shape in vector + [(1, P_DIM)]]
+    saved = [D, D, D, FF, 3 * D, D, FF, D]
+    per_image = pl.BlockSpec((1, 8, D), lambda image: (image, 0, 0))
+    return pl.pallas_call(
+        functools.partial(image_kernel, entries),
+        grid=(images,),
+        out_shape=[sds((tokens, width), half_type) for width in saved]
+        + [sds((images, 8, D))]
+        + vector,
+        in_specs=[rows(P_DIM), rows(P_DIM), per_image, fixed(places)]
+        + [fixed(patch_weight), fixed(head_weight)]
+        + [fixed(bias) for bias in biases]
+        + [pl.BlockSpec(memory_space=pl.ANY)],
+        out_specs=[rows(width) for width in saved] + [per_image] + [fixed(item) for item in vector],
+        scratch_shapes=[
+            pltpu.VMEM((D, wide), half_type),
+            pltpu.VMEM((SEQ, 3 * D), half_type),
+            pltpu.VMEM((HEADS, SEQ, SEQ), jnp.float32),
+            pltpu.VMEM((SEQ, FF), jnp.float32),
+            pltpu.VMEM((SEQ, D), jnp.float32),
+            pltpu.VMEM((SEQ, D), jnp.float32),
+            pltpu.VMEM((SEQ, D), jnp.float32),
+            pltpu.VMEM((SEQ, D), jnp.float32),
+            pltpu.VMEM((SEQ, D), jnp.float32),
+            pltpu.VMEM((SEQ, D), half_type),
+            pltpu.VMEM((SEQ, D), jnp.float32),
+            pltpu.SemaphoreType.DMA((4,)),
+        ],
+        compiler_params=pltpu.CompilerParams(vmem_limit_bytes=60_000_000),
+        name="images",
+    )(patches, targets, mods, places, patch_weight, head_weight, *biases, gathered)
+
+
+def train_gradients(gathered, master_small, biases, noisy_patches, targets, timesteps, labels, entries):
+    edges = [0, 3 * D, 4 * D, 4 * D + FF, 4 * D + 2 * FF]
+    pieces = split_big(gathered)
+    modulate_weight, final_weight, embed_second, embed_first = pieces[4:]
+    patch_weight, class_table, head_weight = split_small(master_small)
+    (
+        query_bias,
+        value_bias,
+        output_bias,
+        up_bias,
+        down_bias,
+        modulate_bias,
+        final_bias,
+        second_bias,
+        first_bias,
+        patch_bias,
+        head_bias,
+    ) = split_bias(biases)
+    images = noisy_patches.shape[0]
+    frequency = timestep_features(timesteps).astype(half_type)
+    embed_pre = multiply_trans(frequency, embed_first) + first_bias
+    embed_hidden = jax.nn.silu(embed_pre).astype(half_type)
+    time_embed = multiply(embed_hidden, embed_second) + second_bias
+    chosen = (labels[:, None] == jnp.arange(NCLASS, dtype=jnp.int32)[None, :]).astype(jnp.float32)
+    condition = time_embed + lax.dot_general(
+        chosen,
+        class_table,
+        (((1,), (1,)), ((), ())),
+        precision=highest,
+        preferred_element_type=jnp.float32,
+    )
+    active = jax.nn.silu(condition).astype(half_type)
+    both_weight = gathered[:, edges[4] : edges[4] + 8 * D]
+    mods = multiply(active, both_weight) + jnp.concatenate([modulate_bias, final_bias])
+    qkv_bias = jnp.concatenate([query_bias, jnp.zeros_like(query_bias), value_bias])
+    (
+        attn_in,
+        mixed,
+        mlp_in,
+        hidden,
+        grad_qkv,
+        grad_attn,
+        grad_pre,
+        grad_mlp,
+        mod_grads,
+        grad_patch,
+        grad_head,
+        bias_qkv,
+        bias_output,
+        bias_up,
+        bias_down,
+        bias_patch,
+        bias_head,
+        losses,
+    ) = run_images(
+        noisy_patches.reshape(-1, P_DIM),
+        targets.reshape(-1, P_DIM),
+        mods.reshape(images, 8, D),
+        position_table(),
+        patch_weight.T.astype(half_type),
+        head_weight.T.astype(half_type),
+        [item[None] for item in (qkv_bias, output_bias, up_bias, down_bias, patch_bias, head_bias)],
+        gathered,
+        entries,
+    )
+    grad_mods = mod_grads.reshape(images, 8 * D).astype(half_type)
+    bias_mods = column_sums(grad_mods)
+    grad_active = multiply_trans(grad_mods, both_weight)
+    grad_condition = slope(jax.nn.silu, condition, grad_active)
+    grad_embed = grad_condition.astype(half_type)
+    grad_embed_hidden = multiply_trans(grad_embed, embed_second)
+    grad_embed_pre = slope(jax.nn.silu, embed_pre, grad_embed_hidden).astype(half_type)
+    grad_big = jnp.concatenate(
+        [
+            outer_sum(attn_in, grad_qkv),
+            outer_sum(mixed, grad_attn),
+            outer_sum(mlp_in, grad_pre),
+            outer_sum(grad_mlp, hidden),
+            outer_sum(active, grad_mods),
+            outer_sum(embed_hidden, grad_embed),
+            outer_sum(grad_embed_pre, frequency),
+        ],
+        axis=1,
+    )
+    grad_bias = jnp.concatenate(
+        [
+            bias_qkv[0, :D],
+            bias_qkv[0, 2 * D :],
+            bias_output[0],
+            bias_up[0],
+            bias_down[0],
+            bias_mods,
+            column_sums(grad_embed),
+            column_sums(grad_embed_pre),
+            bias_patch[0],
+            bias_head[0],
+        ]
+    )
+    loss_part = jnp.sum(losses) / entries
+    return grad_big, grad_patch, grad_head, grad_condition, grad_bias, loss_part
 
 
 def on_pair(
@@ -990,13 +1456,9 @@
     shards = lax.axis_size("shard")
     replicas = lax.axis_size("rep")
     gathered = lax.all_gather(master_big.astype(half_type), "shard", axis=1, tiled=True)
-    output, kept = forward(gathered, master_small, biases, noisy_patches, timesteps, labels)
     entries = noisy_patches.shape[0] * shards * replicas * SEQ * P_DIM
-    error = output - targets.reshape(output.shape)
-    loss_part = jnp.sum(error * error) / entries
-    grad_output = 2.0 * error / entries
-    grad_big, (grad_patch, grad_head, grad_condition), grad_bias = backward(
-        gathered, master_small, kept, grad_output
+    grad_big, grad_patch, grad_head, grad_condition, grad_bias, loss_part = train_gradients(
+        gathered, master_small, biases, noisy_patches, targets, timesteps, labels, entries
     )
     shard = lax.axis_index("shard")
     cols = master_big.shape[1]
@@ -1010,8 +1472,8 @@
     images = labels.shape[0]
     flat = jnp.concatenate(
         [
-            grad_patch.T.reshape(-1),
-            grad_head.T.reshape(-1),
+            grad_patch.reshape(-1),
+            grad_head.reshape(-1),
             grad_bias,
             loss_part[None],
         ]
@@ -1026,9 +1488,6 @@
         ]
     )
     total, all_rows = small_sums(sums, rows)
-    new_master, new_moment, new_error, right_rows = compress(
-        step_rates, own, received, error_big, factor_right.T, moment_big, master_big
-    )
     total = total.reshape(-1)
     all_labels = all_rows[:, :, lines, :images].reshape(-1).astype(jnp.int32)
     conditions = all_rows[:, :, :lines, :].reshape(-1, D)
@@ -1047,6 +1506,20 @@
     new_master_small = master_small - step_rates[1] * new_moment_small
     new_moment_bias = momentum_decay * moment_bias + bias_sum
     new_biases = biases - step_rates[1] * new_moment_bias
+    factor_rows, *small = lax.optimization_barrier(
+        (
+            factor_right.T,
+            total_loss,
+            new_master_small,
+            new_moment_small,
+            new_biases,
+            new_moment_bias,
+        )
+    )
+    total_loss, new_master_small, new_moment_small, new_biases, new_moment_bias = small
+    new_master, new_moment, new_error, right_rows = compress(
+        step_rates, own, received, error_big, factor_rows, moment_big, master_big
+    )
     return (
         total_loss,
         new_master,

time: 537 us -> 389 us (0.72)
  matrix products: 175 us -> 52.6 us
  Pallas kernels: 104 us -> 205 us
  local copies, waits for them, and re-layouts: 126 us -> 50.5 us
  other arithmetic: 73.8 us -> 28.7 us
    pallas_call x1 -> x3, Pallas kernels: 81.2 us -> 176 us  [the longest x1 90.7 us: run_images(): pl.pallas_call(functools.partial(image_kernel, entries), grid=(images,),...]
    dot_general x8 -> x2, matrix products: 50 us -> 6.59 us  [multiply(): return jnp.dot(left_side, right_side, preferred_element_type=jnp.float32)]
    unnamed x181 -> x52, local copies, waits for them, and re-layouts: 61.5 us -> 18.6 us
    dot_general x10 -> x3, matrix products: 50.6 us -> 9.76 us  [multiply_trans(): lax.dot_general(left_side, right_side, (((1,), (1,)), ((), ())), preferre...]
    reduce_sum x16 -> x1, other arithmetic: 40.7 us -> 0.6 us  [train_gradients(): loss_part = jnp.sum(losses) / entries]
    dot_general x7 -> x1, matrix products: 33.5 us -> 1.14 us  [train_gradients(): lax.dot_general(chosen, class_table, (((1,), (1,)), ((), ())), precision=...]
    reshape x9 -> x4, local copies, waits for them, and re-layouts: 20 us -> 1.95 us  [the longest x1 1.01 us: train_gradients(): targets.reshape(-1, P_DIM)]
    split x4 -> x0, local copies, waits for them, and re-layouts: 10 us -> none  [forward(): jnp.split(projected, 3, axis=1)]
  transfers between devices with their start and end apart: 2 -> 2, of which waited for: 1 -> 1; matrix products, arithmetic and copies ran while one was open for 7% -> 8% of each run, Pallas kernels for 4% -> 8%
where the time goes in v2:
time: 389 us; the launch traced here: 383 us
  Pallas kernels  205 us (53%)
  matrix products  52.6 us (14%)
  local copies, waits for them, and re-layouts  50.5 us (13%)
  waiting for transfers between devices  31 us (8%)
  other arithmetic  28.7 us (7%)
  between operations  15.5 us (4%)
    pallas_call x1, Pallas kernels, run_images(): pl.pallas_call(functools.partial(image_kernel, entries), grid=(images,),...  90.7 us
    pallas_call x1, Pallas kernels, compress(): pl.pallas_call(tail_kernel, out_shape=(pltpu.VMEM((blocks, rows, BLOCK),...  43.9 us
    pallas_call x1, Pallas kernels, compress(): pl.pallas_call(update_kernel, out_shape=(sds(master.shape), sds(moment.sh...  41.1 us
    dot_general x7, matrix products, outer_sum(): lax.dot_general(left_side, right_side, (((0,), (0,)), ((), ())), preferre...  32.7 us
    all_gather x1, waiting for transfers between devices, on_pair(): lax.all_gather(master_big.astype(half_type), 'shard', axis=1, tiled=True)  31 us
    pallas_call x1, Pallas kernels, small_sums(): pl.pallas_call(small_kernel, out_shape=(sds((2, REPS) + sums.shape[2:]),...  28.9 us
    unnamed x52, local copies, waits for them, and re-layouts  18.6 us
    dynamic_slice x1, local copies, waits for them, and re-layouts, on_pair(): lax.dynamic_slice_in_dim(low_grad, (1 - shard) * cols, cols, axis=1)  17.4 us
  transfers between devices with their start and end apart: 2, of which 1 were waited for; matrix products, arithmetic and copies ran while one was open for 8% of the time, Pallas kernels for 8%

profile of v2, /device:TPU:0, one launch (start us, length us, event | category | flops | bytes accessed | tf_op | source)
XLA Modules:
  0.0 383.1 jit_solution(11270965225343178037)
XLA Ops:
  7.2 0.0 all-gather.2.cloned.1.call-start
  7.2 13.1 %convert_element_type.81 = bf16[768,8192]{1,0:T(8,128)(2,1)} convert(f32[768,8192]{1,0:T(8,128)} %master_hbm.1) | non-fusion elementwise | flops 6291456 | bytes 37748736 | tf_op jit(solution)/shard_map/convert_element_type | solution.py:1458
  20.4 0.0 copy-start.4
  20.4 0.0 all-gather.2.cloned.1.call-update
  20.4 0.0 copy-start.14
  20.4 0.8 copy-done.5
  21.2 0.6 slice.89
  21.8 0.6 broadcast_in_dim.45.patch_bias_ref
  22.4 0.6 broadcast_in_dim.44.down_bias_ref
  23.0 0.6 broadcast_in_dim.20.output_bias_ref
  23.6 0.6 broadcast_in_dim.19.qkv_bias_ref
  24.2 0.9 reshape.100.patches_ref
  25.1 1.0 reshape.101.targets_ref
  26.2 1.3 convert.33
  27.5 1.9 multiply_sine_fusion.1
  29.4 1.2 pad_maximum_fusion.place_ref
  30.6 0.1 fusion.36
  30.7 0.5 slice_bitcast_fusion.2.head_bias_ref
  31.2 1.4 slice_bitcast_fusion
  32.6 31.0 %all-gather.2.cloned.1.call-done.weights_hbm = bf16[768,16384]{1,0:T(8,128)(2,1)} async-done(((bf16[768,8192]{1,0:T(8,128)(2,1)}), bf16[768,16384]{1,0:T(8,128)(2,1)}) %all-gather.2.cloned.1.call-update) | async-done | bytes 25165840 | tf_op jit(solution)/shard_map/all_gather | solution.py:1458
  63.6 1.2 convolution_add_fusion
  64.8 1.6 convolution_add_fusion.1
  66.4 1.1 fusion.17
  67.5 5.0 %fusion.5 = f32[4,6144]{1,0:T(4,128)S(1)} fusion(bf16[768,16384]{1,0:T(8,128)(2,1)} %all-gather.2.cloned.1.call-done.weights_hbm, f32[6144]{0:T(1024)S(1)} %slice-done, f32[4,768]{1,0:T(4,128)S(1)} %fusion.17), kind=kOutput, calls=%fused_computation.6 | convolution fusion | flops 37788672 | bytes 9572352 | tf_op jit(solution)/shard_map/dot_general | solution.py:30
  72.5 0.7 copy.34
  73.2 90.7 %images.1 = (bf16[1024,768]{1,0:T(8,128)(2,1)}, bf16[1024,768]{1,0:T(8,128)(2,1)}, bf16[1024,768]{1,0:T(8,128)(2,1)}, bf16[1024,3072]{1,0:T(8,128)(2,1)}, bf16[1...) custom-call(bf16[1024,16]{1,0:T(8,128)(2,1)} %reshape.100.patches_re, ...), custom_call_target="tpu_custom_call" | custom-call | tf_op jit(solution)/shard_map/images/pallas_call | solution.py:1309
  163.9 0.9 convert_bitcast_fusion
  164.9 0.0 slice-start.3
  164.9 0.0 slice-start.4
  164.9 8.6 %fusion.10 = bf16[768,16384]{1,0:T(8,128)(2,1)} fusion(bf16[1024,768]{1,0:T(8,128)(2,1)} %get-tuple-element.56, bf16[1024,2304]{1,0:T(8,128)(2,1)} %get-tuple-element.57), kind=kOutput, calls=%fused_computation.12 | convolution fusion | flops 3625648128 | bytes 9830400 | tf_op jit(solution)/shard_map/dot_general | solution.py:40
  173.6 0.0 slice-start.1
  173.6 2.5 fusion.14
  176.0 0.0 slice-start.2
  176.1 6.8 %fusion.9 = bf16[768,16384]{1,0:T(8,128)(2,1)} fusion(bf16[768,16384]{1,0:T(8,128)(2,1)} %fusion.14, bf16[1024,768]{1,0:T(8,128)(2,1)S(1)} %copy-done.16, bf16[1024,3072]{1,0:T(8,128)(2,1)S(1)} %bitcast.59), kind=kOutput, calls=%fused_computation.10 | convolution fusion | flops 4834197504 | bytes 12582912 | tf_op jit(solution)/shard_map/dot_general | solution.py:40
  182.9 6.8 %fusion.8 = bf16[768,16384]{1,0:T(8,128)(2,1)} fusion(bf16[768,16384]{1,0:T(8,128)(2,1)} %fusion.9, bf16[1024,768]{1,0:T(8,128)(2,1)S(1)} %copy-done.15, bf16[1024,3072]{1,0:T(8,128)(2,1)S(1)} %bitcast.57), kind=kOutput, calls=%fused_computation.8 | convolution fusion | flops 4834197504 | bytes 12582912 | tf_op jit(solution)/shard_map/dot_general | solution.py:40
  189.7 5.4 %fusion = bf16[768,16384]{1,0:T(8,128)(2,1)} fusion(bf16[768,16384]{1,0:T(8,128)(2,1)} %fusion.8, bf16[4,6144]{1,0:T(4,128)(2,1)S(1)} %bitcast.49, f32[4,768]{1,0:T(4,128)S(1)} %fusion.17), kind=kOutput, calls=%fused_computation.1 | convolution fusion | flops 42482688 | bytes 9498624 | tf_op jit(solution)/shard_map/dot_general | solution.py:40
  195.1 6.2 %convert_reduce_fusion.3 = (f32[768]{0:T(1024)S(1)}, f32[4,768]{1,0:T(4,128)S(1)}) fusion(f32[4,768]{1,0:T(4,128)S(1)} %fusion.17, bf16[4,6144]{1,0:T(4,128)(2,1)S(1)} %bitcast.50, bf16[768,16384]{1,0:T(8,128)(2,1)} %all-gather.2.cloned.1.call-done.weights_hbm), kind=kOutput, calls=%fused_computation.59 | convolution fusion | flops 37784832 | bytes 9513984 | tf_op jit(solution)/shard_map/dot_general | solution.py:34
  201.3 1.6 fusion.15
  202.9 2.3 convert_reduce_fusion.2
  205.2 1.1 fusion.16
  206.3 0.0 copy-start.7
  206.3 17.4 %constant_dynamic-slice_fusion = (bf16[768,8192]{1,0:T(8,128)(2,1)}, bf16[768,8192]{1,0:T(8,128)(2,1)}) fusion(bf16[768,16384]{1,0:T(8,128)(2,1)} %fusion.16, s32[]{:T(128)S(6)} %select_n.33, s32[]{:T(128)S(6)} %select_n.32), kind=kLoop, calls=%fused_computation.83 | loop fusion | bytes 50331656 | tf_op jit(solution)/shard_map/dynamic_slice | solution.py:1468
  223.7 0.2 collective-permute-start
  223.9 0.6 slice.96
  224.5 0.5 convert_bitcast_fusion.1
  225.1 0.6 reduce_sum.42
  226.5 0.8 concatenate.30
  227.3 0.7 select_maximum_fusion.rows_ref
  228.0 28.9 %small_sums.1 = (f32[2,16,16,128]{3,2,1,0:T(8,128)S(1)}, f32[2,16,32,128]{3,2,1,0:T(8,128)S(1)}) custom-call(f32[2,16,16,128]{3,2,1,0:T(8,128)S(1)} %bitcast.44, f32[32,128]{1,0:T(8,128)S(1)} %select_maximum_fusion.rows_ref), custom_call_target="tpu_custom_call" | custom-call | tf_op jit(solution)/shard_map/small_sums/pallas_call | solution.py:608
  256.8 0.6 slice.107
  257.4 0.8 slice.99
  258.2 0.1 convert_reduce_fusion.1
  258.2 0.1 convert_element_type.97
  258.3 1.8 reshape.109
  260.2 0.6 fusion.46
  260.8 0.8 reshape.108
  261.6 1.4 reshape.110
  263.1 2.4 fusion.23
  265.4 2.1 multiply_subtract_fusion.1
  267.6 6.1 %multiply_subtract_fusion = (f32[768,1032]{0,1:T(8,128)}, f32[768,1032]{0,1:T(8,128)}) fusion(f32[768,1032]{0,1:T(8,128)S(1)} %copy-done.4, f32[]{:T(128)} %bitcast.12, f32[16,768]{1,0:T(8,128)} %reshape.110, f32[1000,768]{1,0:T(8,128)S(1)} %fusion.23, f32[16,768]{1,0:T(8,128)S(1)} %reshape.108, f32[768,1032]{0,1:T(8,128)} %param.22), kind=kLoop, calls=%fused_computation.15 | loop fusion | flops 4755456 | bytes 15851524 | tf_op jit(solution)/shard_map/sub | solution.py:1506
  273.7 43.9 %compress.1 = (f32[16,768,512]{2,1,0:T(8,128)S(1)}, f32[4,768,512]{2,1,0:T(8,128)S(1)}, bf16[16,8,512]{2,1,0:T(8,128)(2,1)S(1)}, bf16[768,128]{1,0:T(8,128)(2,1)S(1)}) custom-call(bf16[768,8192]{1,0:T(8,128)(2,1)} %get-tuple-element.84.own_hbm, bf16[768,8192]{1,0:T(8,128)(2,1)} %collective-permute-done.recv_hbm, f32[1,768,8192]{2,1,0:T(8,128)} %error_hbm.1, ...), custom_call_target="tpu_custom_call" | custom-call | tf_op jit(solution)/shard_map/compress/pallas_call | solution.py:969
  317.6 8.9 %copy-done = f32[16,768,512]{2,1,0:T(8,128)} copy-done((f32[16,768,512]{2,1,0:T(8,128)}, f32[16,768,512]{2,1,0:T(8,128)S(1)}, u32[]{:S(2)}) %copy-start) | copy-done | bytes 25165848
  326.5 8.2 %copy-done.1 = f32[16,768,512]{2,1,0:T(8,128)S(1)} copy-done((f32[16,768,512]{2,1,0:T(8,128)S(1)}, f32[16,768,512]{2,1,0:T(8,128)}, u32[]{:S(2)}) %copy-start.1) | copy-done | bytes 25165848
  334.7 41.1 %update.1 = (f32[768,8192]{1,0:T(8,128)}, f32[768,8192]{1,0:T(8,128)}, f32[1,768,8192]{2,1,0:T(8,128)}, f32[8,8192]{1,0:T(8,128)}) custom-call(f32[2]{0:T(128)S(1)} %copy-done.3, f32[16,768,512]{2,1,0:T(8,128)S(1)} %copy-done.1, f32[4,768,512]{2,1,0:T(8,128)S(1)} %get-tuple-element.66.v_ref, bf16[16,8,512]{2,1,0:T(8,128)(2,1)S(1)} %get-tuple-element.67.whole_ref, ...), custom_call_target="tpu_custom_call" | custom-call | tf_op jit(solution)/shard_map/update/pallas_call | solution.py:1005
  (62 shorter events, 0.3 us)
Async XLA Ops:
  7.2 56.4 %all-gather.2.cloned.1.call-start = ((), (), s32[]{:S(2)}) async-start(), calls=%async_computation | async-start | bytes 37748736 | tf_op jit(solution)/shard_map/all_gather | solution.py:1458
  20.4 0.8 copy-start.5
  20.4 1.4 copy-start.19
  20.4 3.8 %copy-start.9 = (bf16[4,4096]{1,0:T(4,128)(2,1)S(1)}, bf16[4,4096]{1,0:T(4,128)(2,1)}, u32[]{:S(2)}) copy-start(bf16[4,4096]{1,0:T(4,128)(2,1)} %param.13) | copy-start | bytes 98308
  20.4 4.8 %copy-start.6 = (f32[4,4096]{1,0:T(4,128)S(1)}, f32[4,4096]{1,0:T(4,128)}, u32[]{:S(2)}) copy-start(f32[4,4096]{1,0:T(4,128)} %param.14) | copy-start | bytes 196612
  20.4 5.8 %copy-start.4 = (f32[768,1032]{0,1:T(8,128)S(1)}, f32[768,1032]{0,1:T(8,128)}, u32[]{:S(2)}) copy-start(f32[768,1032]{0,1:T(8,128)} %param.21) | copy-start | bytes 9510916
  20.4 46.0 %copy-start.14 = (s32[4]{0:T(128)S(1)}, s32[4]{0:T(128)}, u32[]{:S(2)}) copy-start(s32[4]{0:T(128)} %param.16) | copy-start | bytes 52
  26.1 41.4 %slice-start = ((f32[14608]{0:T(1024)}), f32[6144]{0:T(1024)S(1)}, s32[]{:S(2)}) async-start(f32[14608]{0:T(1024)} %param.23), calls=%async_computation.1 | async-start | bytes 49152 | tf_op jit(solution)/shard_map/concatenate | solution.py:1372
  164.9 11.2 %slice-start.3 = ((s8[6291456]{0:T(1024)(128)(4,1)}), s8[4194304]{0:T(1024)(128)(4,1)S(1)}, s32[]{:S(2)}) async-start(s8[6291456]{0:T(1024)(128)(4,1)} %bitcast.58), calls=%async_computation.4 | async-start | bytes 8388608
  164.9 8.7 %copy-start.17 = (bf16[1024,768]{1,0:T(8,128)(2,1)S(1)}, bf16[1024,768]{1,0:T(8,128)(2,1)}, u32[]{:S(2)}) copy-start(bf16[1024,768]{1,0:T(8,128)(2,1)} %get-tuple-element.58) | copy-start | bytes 4718596
  164.9 8.7 %copy-start.18 = (bf16[1024,768]{1,0:T(8,128)(2,1)S(1)}, bf16[1024,768]{1,0:T(8,128)(2,1)}, u32[]{:S(2)}) copy-start(bf16[1024,768]{1,0:T(8,128)(2,1)} %get-tuple-element.59) | copy-start | bytes 4718596
  164.9 11.1 %slice-start.4 = ((s8[6291456]{0:T(1024)(128)(4,1)}), s8[2097152]{0:T(1024)(128)(4,1)S(1)}, s32[]{:S(2)}) async-start(s8[6291456]{0:T(1024)(128)(4,1)} %bitcast.58), calls=%async_computation.5 | async-start | bytes 4194304
  173.5 2.5 copy-start.16
  173.6 9.3 %slice-start.1 = ((s8[6291456]{0:T(1024)(128)(4,1)}), s8[4194304]{0:T(1024)(128)(4,1)S(1)}, s32[]{:S(2)}) async-start(s8[6291456]{0:T(1024)(128)(4,1)} %bitcast.56), calls=%async_computation.2 | async-start | bytes 8388608
  176.0 6.8 %slice-start.2 = ((s8[6291456]{0:T(1024)(128)(4,1)}), s8[2097152]{0:T(1024)(128)(4,1)S(1)}, s32[]{:S(2)}) async-start(s8[6291456]{0:T(1024)(128)(4,1)} %bitcast.56), calls=%async_computation.3 | async-start | bytes 4194304
  176.1 6.8 %copy-start.15 = (bf16[1024,768]{1,0:T(8,128)(2,1)S(1)}, bf16[1024,768]{1,0:T(8,128)(2,1)}, u32[]{:S(2)}) copy-start(bf16[1024,768]{1,0:T(8,128)(2,1)} %get-tuple-element.62) | copy-start | bytes 4718596
  206.3 17.7 %copy-start.3 = (f32[2]{0:T(128)S(1)}, f32[2]{0:T(128)}, u32[]{:S(2)}) copy-start(f32[2]{0:T(128)} %rates_ref.1) | copy-start | bytes 28
  206.3 18.8 %copy-start.20 = (f32[1,16]{1,0:T(1,128)S(1)}, f32[1,16]{1,0:T(1,128)}, u32[]{:S(2)}) copy-start(f32[1,16]{1,0:T(1,128)} %get-tuple-element.52) | copy-start | bytes 196
  206.3 19.4 %copy-start.8 = (f32[16,768]{1,0:T(8,128)S(1)}, f32[16,768]{1,0:T(8,128)}, u32[]{:S(2)}) copy-start(f32[16,768]{1,0:T(8,128)} %get-tuple-element.43) | copy-start | bytes 147460
  206.3 19.4 %copy-start.13 = (f32[1,768]{1,0:T(1,128)S(1)}, f32[1,768]{1,0:T(1,128)}, u32[]{:S(2)}) copy-start(f32[1,768]{1,0:T(1,128)} %get-tuple-element.46) | copy-start | bytes 9220
  206.3 19.4 %copy-start.12 = (f32[1,768]{1,0:T(1,128)S(1)}, f32[1,768]{1,0:T(1,128)}, u32[]{:S(2)}) copy-start(f32[1,768]{1,0:T(1,128)} %get-tuple-element.48) | copy-start | bytes 9220
  206.3 19.4 %copy-start.11 = (f32[1,768]{1,0:T(1,128)S(1)}, f32[1,768]{1,0:T(1,128)}, u32[]{:S(2)}) copy-start(f32[1,768]{1,0:T(1,128)} %get-tuple-element.50) | copy-start | bytes 9220
  206.3 19.5 %copy-start.7 = (f32[16,768]{1,0:T(8,128)S(1)}, f32[16,768]{1,0:T(8,128)}, u32[]{:S(2)}) copy-start(f32[16,768]{1,0:T(8,128)} %get-tuple-element.44) | copy-start | bytes 147460
  206.3 20.1 %copy-start.10 = (f32[1,2304]{1,0:T(1,128)S(1)}, f32[1,2304]{1,0:T(1,128)}, u32[]{:S(2)}) copy-start(f32[1,2304]{1,0:T(1,128)} %get-tuple-element.45) | copy-start | bytes 27652
  223.7 50.0 %collective-permute-start = (bf16[768,8192]{1,0:T(8,128)(2,1)}, bf16[768,8192]{1,0:T(8,128)(2,1)}, u32[]{:S(2)}, u32[]{:S(2)}) collective-permute-start(bf16[768,8192]{1,0:T(8,128)(2,1)} %get-tuple-element.83), channel_id=1, source_target_pairs={{0,16},{16,0},{1,17},{17,1},{2,18},{18,2},{3,19},{19,3},{4,20},{20... | collective-permute-start | bytes 37748744 | tf_op jit(solution)/shard_map/ppermute | solution.py:1467
  267.6 6.1 %copy-start.2 = (f32[8192,8]{0,1:T(8,128)S(1)}, f32[8192,8]{0,1:T(8,128)}, u32[]{:S(2)}) copy-start(f32[8192,8]{0,1:T(8,128)} %param.20) | copy-start | bytes 786436
  317.6 8.9 %copy-start = (f32[16,768,512]{2,1,0:T(8,128)}, f32[16,768,512]{2,1,0:T(8,128)S(1)}, u32[]{:S(2)}) copy-start(f32[16,768,512]{2,1,0:T(8,128)S(1)} %get-tuple-element.65.m_ref) | copy-start | bytes 75497472
  326.5 8.2 %copy-start.1 = (f32[16,768,512]{2,1,0:T(8,128)S(1)}, f32[16,768,512]{2,1,0:T(8,128)}, u32[]{:S(2)}) copy-start(f32[16,768,512]{2,1,0:T(8,128)} %copy-done) | copy-start | bytes 75497472
Sparse Core Ops, SparseCore 0:
  20.5 43.0 all-gather.1

commit v3 on v2

--- a/solution.py
+++ b/solution.py
@@ -489,6 +489,10 @@
 
 MESH = pl.DeviceIdType.MESH
 BLOCK = 512
+PIECE = 256
+EARLY = 10
+KERNEL_BYTES = 18_000_000
+EXCHANGE_BYTES = 36_000_000
 RANK = 8
 LANES = 128
 REPS = 16
@@ -511,129 +515,21 @@
     return barrier, len(others)
 
 
-def small_kernel(
-    sums_ref, rows_ref, total_ref, gathered_ref, half_ref, part_ref, mine_ref, send_sem, recv_sem
-):
-    shard = lax.axis_index("shard")
-    rep = lax.axis_index("rep")
-    partner = (1 - shard, rep)
-    peers = [(shard, lax.rem(rep + step, REPS)) for step in range(1, REPS)]
-    barrier, count = greet([partner] + peers)
-    pl.semaphore_wait(barrier, count)
-
-    def remote(source, target, where, who):
-        return pltpu.make_async_remote_copy(
-            src_ref=source,
-            dst_ref=target,
-            send_sem=send_sem.at[where],
-            recv_sem=recv_sem.at[where],
-            device_id=who,
-            device_id_type=MESH,
-        )
-
-    rows_out = [
-        pltpu.make_async_remote_copy(
-            src_ref=rows_ref,
-            dst_ref=gathered_ref.at[shard, rep],
-            send_sem=send_sem.at[step],
-            recv_sem=recv_sem.at[rep],
-            device_id=peers[step - 1],
-            device_id_type=MESH,
-        )
-        for step in range(1, REPS)
-    ]
-    own_half = remote(sums_ref.at[1 - shard], half_ref, 16, partner)
-    own_half.start()
-    for copy in rows_out:
-        copy.start()
-    gathered_ref[shard, rep] = rows_ref[...]
-    own_half.wait()
-    half_ref[...] = half_ref[...] + sums_ref[shard]
-    parts_out = [
-        pltpu.make_async_remote_copy(
-            src_ref=half_ref.at[lax.rem(rep + step, REPS)],
-            dst_ref=part_ref.at[rep],
-            send_sem=send_sem.at[17 + step],
-            recv_sem=recv_sem.at[17 + rep],
-            device_id=peers[step - 1],
-            device_id_type=MESH,
-        )
-        for step in range(1, REPS)
-    ]
-    for copy in parts_out:
-        copy.start()
-    part_ref[rep] = half_ref[rep]
-
-    def arrived(slots, base):
-        for step in range(1, REPS):
-            other = lax.rem(rep + step, REPS)
-            pltpu.make_async_remote_copy(
-                src_ref=slots.at[other],
-                dst_ref=slots.at[other],
-                send_sem=send_sem.at[base],
-                recv_sem=recv_sem.at[base + other],
-                device_id=peers[step - 1],
-                device_id_type=MESH,
-            ).wait_recv()
-
-    arrived(part_ref, 17)
-    mine_ref[...] = jnp.sum(part_ref[...], axis=0)
-    whole_out = [
-        pltpu.make_async_remote_copy(
-            src_ref=mine_ref,
-            dst_ref=total_ref.at[shard, rep],
-            send_sem=send_sem.at[33 + step],
-            recv_sem=recv_sem.at[33 + rep],
-            device_id=peers[step - 1],
-            device_id_type=MESH,
-        )
-        for step in range(1, REPS)
-    ]
-    for copy in whole_out:
-        copy.start()
-    total_ref[shard, rep] = mine_ref[...]
-    arrived(gathered_ref.at[shard], 0)
-    rows_across = remote(gathered_ref.at[shard], gathered_ref.at[shard], 49, partner)
-    rows_across.start()
-    arrived(total_ref.at[shard], 33)
-    total_across = remote(total_ref.at[shard], total_ref.at[shard], 50, partner)
-    total_across.start()
-    for copy in rows_out + parts_out + whole_out:
-        copy.wait_send()
-    rows_across.wait()
-    total_across.wait()
-
-
-def small_sums(sums, rows):
-    return pl.pallas_call(
-        small_kernel,
-        out_shape=(sds((2, REPS) + sums.shape[2:]), sds((2, REPS) + rows.shape)),
-        in_specs=[pl.BlockSpec(memory_space=pltpu.VMEM)] * 2,
-        out_specs=[pl.BlockSpec(memory_space=pltpu.VMEM)] * 2,
-        scratch_shapes=[
-            pltpu.VMEM(sums.shape[1:], jnp.float32),
-            pltpu.VMEM((REPS,) + sums.shape[2:], jnp.float32),
-            pltpu.VMEM(sums.shape[2:], jnp.float32),
-            pltpu.SemaphoreType.DMA((51,)),
-            pltpu.SemaphoreType.DMA((51,)),
-        ],
-        compiler_params=pltpu.CompilerParams(
-            collective_id=1, has_side_effects=True, vmem_limit_bytes=16 * 1024 * 1024
-        ),
-        name="small_sums",
-    )(sums, rows)
-
-
 def tail_kernel(
-    own_hbm,
-    recv_hbm,
+    grad_hbm,
     error_hbm,
     factor_ref,
     moment_hbm,
-    m_ref,
+    sums_ref,
+    rows_ref,
     v_ref,
     whole_ref,
     basis_cols,
+    total_ref,
+    gathered_ref,
+    recv_hbm,
+    m_hbm,
+    m_ref,
     own_ref,
     recv_ref,
     stack_ref,
@@ -645,6 +541,9 @@
     send_ref,
     part_ref,
     mine_ref,
+    half_ref,
+    share_ref,
+    small_ref,
     load_sem,
     own_sem,
     recv_sem,
@@ -653,15 +552,52 @@
     left_recv,
     right_send,
     right_recv,
+    grad_send,
+    grad_recv,
+    small_send,
+    small_recv,
+    m_sem,
 ):
     blocks = m_ref.shape[0]
+    cols = recv_hbm.shape[1]
     shard = lax.axis_index("shard")
     rep = lax.axis_index("rep")
+    partner = (1 - shard, rep)
     peers = [(shard, lax.rem(rep + step, REPS)) for step in range(1, REPS)]
-    barrier, count = greet(peers)
+    barrier, count = greet([partner] + peers)
 
     def columns(block):
         return pl.ds(pl.multiple_of(block * BLOCK, BLOCK), BLOCK)
+
+    def part_columns(part, block):
+        return pl.ds(pl.multiple_of(part * cols + block * BLOCK, BLOCK), BLOCK)
+
+    def send_grad(block):
+        return pltpu.make_async_remote_copy(
+            src_ref=grad_hbm.at[:, part_columns(1 - shard, block)],
+            dst_ref=recv_hbm.at[:, columns(block)],
+            send_sem=grad_send.at[block],
+            recv_sem=grad_recv.at[block],
+            device_id=partner,
+            device_id_type=MESH,
+        )
+
+    def small_copy(source, target, sent, got, who):
+        return pltpu.make_async_remote_copy(
+            src_ref=source,
+            dst_ref=target,
+            send_sem=small_send.at[sent],
+            recv_sem=small_recv.at[got],
+            device_id=who,
+            device_id_type=MESH,
+        )
+
+    def arrived(slots, base):
+        for step in range(1, REPS):
+            other = lax.rem(rep + step, REPS)
+            small_copy(
+                slots.at[other], slots.at[other], base, base + other, peers[step - 1]
+            ).wait_recv()
 
     def load_error(block):
         return pltpu.make_async_copy(
@@ -670,7 +606,7 @@
 
     def load_own(block, slot):
         return pltpu.make_async_copy(
-            own_hbm.at[:, columns(block)], own_ref.at[slot], own_sem.at[slot]
+            grad_hbm.at[:, part_columns(shard, block)], own_ref.at[slot], own_sem.at[slot]
         )
 
     def load_recv(block, slot):
@@ -678,6 +614,9 @@
             recv_hbm.at[:, columns(block)], recv_ref.at[slot], recv_sem.at[slot]
         )
 
+    def save_matrix(block):
+        return pltpu.make_async_copy(m_ref.at[block], m_hbm.at[block], m_sem.at[block])
+
     def load_moment(block):
         return pltpu.make_async_copy(
             moment_hbm.at[:, columns(block)], v_ref.at[block], moment_sem.at[block]
@@ -688,13 +627,27 @@
     for block in range(depth):
         load_error(block).start()
         load_own(block, block).start()
-        load_recv(block, block).start()
+    pl.semaphore_wait(barrier, count)
+    own_half = small_copy(sums_ref.at[1 - shard], half_ref, 16, 16, partner)
+    own_half.start()
+    for block in range(blocks):
+        send_grad(block).start()
+    rows_out = [
+        small_copy(rows_ref, gathered_ref.at[shard, rep], step, rep, peers[step - 1])
+        for step in range(1, REPS)
+    ]
+    for copy in rows_out:
+        copy.start()
+    gathered_ref[shard, rep] = rows_ref[...]
 
     high, low = split_two(factor_ref[...])
     stack_ref[...] = jnp.zeros_like(stack_ref)
     stack_ref[0:RANK] = high
     stack_ref[RANK : 2 * RANK] = low
     left_acc[...] = jnp.zeros_like(left_acc)
+    for block in range(depth):
+        send_grad(block).wait_recv()
+        load_recv(block, block).start()
 
     def gather_block(block, carry):
         slot = lax.rem(block, depth)
@@ -705,6 +658,7 @@
             own_ref[slot].astype(jnp.float32) + recv_ref[slot].astype(jnp.float32) + m_ref[block]
         )
         m_ref[block] = matrix
+        save_matrix(block).start()
         high, low = split_two(matrix)
         factor = stack_ref[:, columns(block)]
         left_acc[...] += multiply_trans(high, factor) + multiply_trans(low, factor)
@@ -713,17 +667,33 @@
         def _():
             load_error(block + depth).start()
             load_own(block + depth, slot).start()
+            send_grad(block + depth).wait_recv()
             load_recv(block + depth, slot).start()
 
         return carry
 
-    lax.fori_loop(0, blocks, gather_block, 0)
+    lax.fori_loop(0, blocks // 2, gather_block, 0)
+    own_half.wait()
+    half_ref[...] = half_ref[...] + sums_ref[shard]
+    shares_out = [
+        small_copy(
+            half_ref.at[lax.rem(rep + step, REPS)],
+            share_ref.at[rep],
+            17 + step,
+            17 + rep,
+            peers[step - 1],
+        )
+        for step in range(1, REPS)
+    ]
+    for copy in shares_out:
+        copy.start()
+    share_ref[rep] = half_ref[rep]
+    lax.fori_loop(blocks // 2, blocks, gather_block, 0)
     for block in range(v_ref.shape[0]):
         load_moment(block).start()
 
     turned = left_acc[...].T
     left_ref[...] = turned[0:RANK] + turned[RANK : 2 * RANK]
-    pl.semaphore_wait(barrier, count)
 
     place = lax.rem(rep, 4)
     level = lax.div(rep, 4)
@@ -743,6 +713,15 @@
     for copy in plane_out:
         copy.start()
     plane_ref[place] = left_ref[...]
+    arrived(share_ref, 17)
+    small_ref[...] = jnp.sum(share_ref[...], axis=0)
+    whole_out = [
+        small_copy(small_ref, total_ref.at[shard, rep], 33 + step, 33 + rep, peers[step - 1])
+        for step in range(1, REPS)
+    ]
+    for copy in whole_out:
+        copy.start()
+    total_ref[shard, rep] = small_ref[...]
     for step in range(1, 4):
         other = lax.rem(place + step, 4)
         pltpu.make_async_remote_copy(
@@ -808,6 +787,12 @@
     basis_cols[...] = padded.T.astype(half_type)
     for copy in column_out:
         copy.wait_send()
+    arrived(gathered_ref.at[shard], 0)
+    rows_across = small_copy(gathered_ref.at[shard], gathered_ref.at[shard], 49, 49, partner)
+    rows_across.start()
+    arrived(total_ref.at[shard], 33)
+    total_across = small_copy(total_ref.at[shard], total_ref.at[shard], 50, 50, partner)
+    total_across.start()
 
     def right_block(block, carry):
         high, low = split_two(m_ref[block])
@@ -849,15 +834,20 @@
     for step in range(1, REPS):
         other = lax.rem(rep + step, REPS)
         right_copy(mine_ref, whole_ref.at[other], REPS, step, other).wait_recv()
-    for copy in scatter + spread:
+    for copy in scatter + spread + rows_out + shares_out + whole_out:
         copy.wait_send()
+    for block in range(blocks):
+        send_grad(block).wait_send()
+        save_matrix(block).wait()
+    rows_across.wait()
+    total_across.wait()
     for block in range(v_ref.shape[0]):
         load_moment(block).wait()
 
 
 def update_kernel(
     rates_ref,
-    m_ref,
+    m_hbm,
     v_ref,
     whole_ref,
     basis_cols,
@@ -872,23 +862,36 @@
     master_ref,
     moment_sem,
     master_sem,
+    matrix_sem,
     error_out,
     moment_out,
     master_out,
 ):
-    blocks = m_ref.shape[0]
-    early = v_ref.shape[0]
+    pieces = BLOCK // PIECE
+    blocks = m_hbm.shape[0] * pieces
+    early = v_ref.shape[0] * pieces
     slots = master_ref.shape[0]
     rate = rates_ref[0]
 
     def columns(block):
-        return pl.ds(pl.multiple_of(block * BLOCK, BLOCK), BLOCK)
+        return pl.ds(pl.multiple_of(block * PIECE, PIECE), PIECE)
 
     def load_master(block, slot):
         return pltpu.make_async_copy(
             master_hbm.at[:, columns(block)], master_ref.at[slot], master_sem.at[slot]
         )
 
+    def load_matrix(block, slot):
+        return pltpu.make_async_copy(
+            m_hbm.at[
+                lax.div(block, pieces),
+                :,
+                pl.ds(pl.multiple_of(lax.rem(block, pieces) * PIECE, PIECE), PIECE),
+            ],
+            error_ref.at[slot],
+            matrix_sem.at[slot],
+        )
+
     def load_moment(block, slot):
         return pltpu.make_async_copy(
             moment_hbm.at[:, columns(block)], moment_ref.at[slot], moment_sem.at[slot]
@@ -911,9 +914,12 @@
 
     ahead = slots - 2
     for block in range(ahead):
+        load_matrix(block, block).start()
         load_master(block, block).start()
 
-    def update_block(block, carry):
+    def update_piece(whole, piece):
+        block = whole * pieces + piece
+        span = slice(piece * PIECE, (piece + 1) * PIECE)
         slot = lax.rem(block, slots)
         next_slot = lax.rem(block + ahead, slots)
 
@@ -925,21 +931,25 @@
 
         @pl.when(block + ahead < blocks)
         def _():
+            load_matrix(block + ahead, next_slot).start()
             load_master(block + ahead, next_slot).start()
 
             @pl.when(block + ahead >= early)
             def _():
                 load_moment(block + ahead, next_slot).start()
 
-        right = whole_ref[block]
+        right = whole_ref[whole, :, span]
         right_ref[:, columns(block)] = right.astype(jnp.float32)
         approx = multiply(basis_cols[:, 0 : 2 * RANK], jnp.concatenate([right, right], axis=0))
-        error_ref[slot] = m_ref[block] - approx * (1.0 / REPS)
+        load_matrix(block, slot).wait()
+        error_ref[slot] = error_ref[slot] - approx * (1.0 / REPS)
         out_error(block, slot).start()
 
         @pl.when(block < early)
         def _():
-            moment_ref[slot] = momentum_decay * v_ref[jnp.minimum(block, early - 1)] + approx
+            moment_ref[slot] = (
+                momentum_decay * v_ref[jnp.minimum(whole, v_ref.shape[0] - 1), :, span] + approx
+            )
 
         @pl.when(block >= early)
         def _():
@@ -950,33 +960,41 @@
         load_master(block, slot).wait()
         master_ref[slot] = master_ref[slot] - rate * moment_ref[slot]
         out_master(block, slot).start()
+
+    def update_block(whole, carry):
+        for piece in range(pieces):
+            update_piece(whole, piece)
         return carry
 
-    lax.fori_loop(0, blocks, update_block, 0)
+    lax.fori_loop(0, m_hbm.shape[0], update_block, 0)
     for block in range(blocks - 2, blocks):
         out_error(block, block % slots).wait()
         out_moment(block, block % slots).wait()
         out_master(block, block % slots).wait()
 
 
-def compress(rates, own, received, error, factor_rows, moment, master):
-    rows, cols = own.shape
+def compress(rates, grads, error, factor_rows, moment, master, sums, lines):
+    rows, cols = master.shape
     blocks = cols // BLOCK
     depth = 3
-    slots = 4
-    hbm = pl.BlockSpec(memory_space=pl.ANY)
+    slots = 6
+    hbm = pl.BlockSpec(memory_space=pltpu.HBM)
     vmem = pl.BlockSpec(memory_space=pltpu.VMEM)
-    matrices, moments, whole, basis = pl.pallas_call(
+    moments, whole, basis, total, gathered, unused, matrices = pl.pallas_call(
         tail_kernel,
         out_shape=(
-            pltpu.VMEM((blocks, rows, BLOCK), jnp.float32),
-            pltpu.VMEM((4, rows, BLOCK), jnp.float32),
+            pltpu.VMEM((EARLY, rows, BLOCK), jnp.float32),
             pltpu.VMEM((blocks, RANK, BLOCK), half_type),
             pltpu.VMEM((rows, LANES), half_type),
+            sds((2, REPS) + sums.shape[2:]),
+            sds((2, REPS) + lines.shape),
+            pltpu.HBM((rows, cols), half_type),
+            pltpu.HBM((blocks, rows, BLOCK), jnp.float32),
         ),
-        in_specs=[hbm, hbm, hbm, vmem, hbm],
-        out_specs=[vmem] * 4,
+        in_specs=[hbm, hbm, vmem, hbm, vmem, vmem],
+        out_specs=[vmem] * 5 + [pl.BlockSpec(memory_space=pltpu.HBM)] * 2,
         scratch_shapes=[
+            pltpu.VMEM((blocks, rows, BLOCK), jnp.float32),
             pltpu.VMEM((depth, rows, BLOCK), half_type),
             pltpu.VMEM((depth, rows, BLOCK), half_type),
             pltpu.VMEM((LANES, cols), half_type),
@@ -988,6 +1006,9 @@
             pltpu.VMEM((blocks, RANK, BLOCK), half_type),
             pltpu.VMEM((blocks, RANK, BLOCK), half_type),
             pltpu.VMEM((RANK, BLOCK), half_type),
+            pltpu.VMEM(sums.shape[1:], jnp.float32),
+            pltpu.VMEM(sums.shape[1:], jnp.float32),
+            pltpu.VMEM(sums.shape[2:], jnp.float32),
             pltpu.SemaphoreType.DMA((blocks,)),
             pltpu.SemaphoreType.DMA((depth,)),
             pltpu.SemaphoreType.DMA((depth,)),
@@ -996,13 +1017,18 @@
             pltpu.SemaphoreType.DMA((8,)),
             pltpu.SemaphoreType.DMA((2 * REPS,)),
             pltpu.SemaphoreType.DMA((2 * REPS,)),
+            pltpu.SemaphoreType.DMA((blocks,)),
+            pltpu.SemaphoreType.DMA((blocks,)),
+            pltpu.SemaphoreType.DMA((51,)),
+            pltpu.SemaphoreType.DMA((51,)),
+            pltpu.SemaphoreType.DMA((blocks,)),
         ],
         compiler_params=pltpu.CompilerParams(
-            collective_id=2, has_side_effects=True, vmem_limit_bytes=14_000_000
+            collective_id=2, has_side_effects=True, vmem_limit_bytes=EXCHANGE_BYTES
         ),
         name="compress",
-    )(own, received, error, factor_rows, moment)
-    return pl.pallas_call(
+    )(grads, error, factor_rows, moment, sums, lines)
+    updated = pl.pallas_call(
         update_kernel,
         out_shape=(
             sds(master.shape),
@@ -1010,21 +1036,77 @@
             sds(error.shape),
             sds((RANK, cols)),
         ),
-        in_specs=[pl.BlockSpec(memory_space=pltpu.SMEM), vmem, vmem, vmem, vmem, hbm, hbm],
+        in_specs=[pl.BlockSpec(memory_space=pltpu.SMEM), hbm, vmem, vmem, vmem, hbm, hbm],
         out_specs=[hbm, hbm, hbm, vmem],
         scratch_shapes=[
-            pltpu.VMEM((slots, rows, BLOCK), jnp.float32),
-            pltpu.VMEM((slots, rows, BLOCK), jnp.float32),
-            pltpu.VMEM((slots, rows, BLOCK), jnp.float32),
+            pltpu.VMEM((slots, rows, PIECE), jnp.float32),
+            pltpu.VMEM((slots, rows, PIECE), jnp.float32),
+            pltpu.VMEM((slots, rows, PIECE), jnp.float32),
+            pltpu.SemaphoreType.DMA((slots,)),
             pltpu.SemaphoreType.DMA((slots,)),
             pltpu.SemaphoreType.DMA((slots,)),
             pltpu.SemaphoreType.DMA((slots,)),
             pltpu.SemaphoreType.DMA((slots,)),
             pltpu.SemaphoreType.DMA((slots,)),
         ],
-        compiler_params=pltpu.CompilerParams(vmem_limit_bytes=24500000),
+        compiler_params=pltpu.CompilerParams(vmem_limit_bytes=KERNEL_BYTES),
         name="update",
     )(rates, matrices, moments, whole, basis, moment, master)
+    return lax.optimization_barrier((tuple(updated), total, gathered))
+
+
+def small_kernel(
+    rates_ref, sums_ref, lines_ref, moment_ref, master_ref, new_moment_ref, new_master_ref
+):
+    step = pl.program_id(0)
+    height = moment_ref.shape[0]
+    images = lines_ref.shape[0] * lines_ref.shape[1] * 8
+    strips = D // LANES
+
+    def piece(place):
+        return lines_ref[:, :, place * 8 : (place + 1) * 8, :].reshape(images, LANES)
+
+    labels = piece(strips)[:, 0:1]
+    place = lax.broadcasted_iota(jnp.int32, (images, height), 1) + (step * height - P_DIM)
+    chosen = (place.astype(jnp.float32) == labels).astype(half_type)
+    for strip in range(strips):
+        span = slice(strip * LANES, (strip + 1) * LANES)
+        high, low = split_two(piece(strip))
+        new_moment_ref[:, span] = (
+            momentum_decay * moment_ref[:, span] + outer_sum(chosen, high) + outer_sum(chosen, low)
+        )
+
+    def add(first, base):
+        for strip in range(strips):
+            span = slice(strip * LANES, (strip + 1) * LANES)
+            new_moment_ref[first : first + P_DIM, span] += sums_ref[
+                base + strip * P_DIM : base + (strip + 1) * P_DIM, :
+            ]
+
+    @pl.when(step == 0)
+    def _():
+        add(0, 0)
+
+    @pl.when(step == pl.num_programs(0) - 1)
+    def _():
+        add(height - P_DIM, strips * P_DIM)
+
+    new_master_ref[...] = master_ref[...] - rates_ref[1] * new_moment_ref[...]
+
+
+def update_small(rates, total, gathered, moment, master):
+    rows = moment.shape[0]
+    steps = 3
+    vmem = pl.BlockSpec(memory_space=pltpu.VMEM)
+    block = pl.BlockSpec((rows // steps, D), lambda step: (step, 0))
+    return pl.pallas_call(
+        small_kernel,
+        grid=(steps,),
+        out_shape=(sds(moment.shape), sds(master.shape)),
+        in_specs=[pl.BlockSpec(memory_space=pltpu.SMEM), vmem, vmem, block, block],
+        out_specs=[block, block],
+        name="update_small",
+    )(rates, total.reshape(-1, LANES), gathered, moment, master)
 
 
 GROUP = 2 * HEAD_DIM
@@ -1460,74 +1542,56 @@
     grad_big, grad_patch, grad_head, grad_condition, grad_bias, loss_part = train_gradients(
         gathered, master_small, biases, noisy_patches, targets, timesteps, labels, entries
     )
-    shard = lax.axis_index("shard")
-    cols = master_big.shape[1]
-    low_grad = grad_big.astype(half_type)
-    own = lax.dynamic_slice_in_dim(low_grad, shard * cols, cols, axis=1)
-    received = lax.ppermute(
-        lax.dynamic_slice_in_dim(low_grad, (1 - shard) * cols, cols, axis=1),
-        "shard",
-        [(0, 1), (1, 0)],
-    )
     images = labels.shape[0]
+    strips = D // LANES
+
+    def lines_of(matrix):
+        return matrix.reshape(-1, strips, LANES).transpose(1, 0, 2)
+
     flat = jnp.concatenate(
         [
-            grad_patch.reshape(-1),
-            grad_head.reshape(-1),
+            lines_of(grad_patch).reshape(-1),
+            lines_of(grad_head).reshape(-1),
             grad_bias,
             loss_part[None],
         ]
     )
     width = shards * replicas * 16 * LANES
     sums = jnp.pad(flat, (0, width - flat.shape[0])).reshape(shards, replicas, 16, LANES)
-    lines = images * D // LANES
-    rows = jnp.concatenate(
+    label_lines = jnp.broadcast_to(labels.astype(jnp.float32)[None, :, None], (1, images, LANES))
+    lines = jnp.concatenate(
         [
-            grad_condition.reshape(lines, LANES),
-            jnp.pad(labels.astype(jnp.float32)[None], ((0, 7), (0, LANES - images))),
+            jnp.pad(lines_of(grad_condition), ((0, 0), (0, 8 - images), (0, 0))),
+            jnp.pad(label_lines, ((0, 0), (0, 8 - images), (0, 0)), constant_values=-100000.0),
         ]
-    )
-    total, all_rows = small_sums(sums, rows)
+    ).reshape(-1, LANES)
+    (new_master, new_moment, new_error, right_rows), total, gathered_lines = compress(
+        step_rates,
+        grad_big.astype(half_type),
+        error_big,
+        factor_right.T,
+        moment_big,
+        master_big,
+        sums,
+        lines,
+    )
+    new_moment_small, new_master_small = update_small(
+        step_rates, total, gathered_lines, moment_small.T, master_small.T
+    )
     total = total.reshape(-1)
-    all_labels = all_rows[:, :, lines, :images].reshape(-1).astype(jnp.int32)
-    conditions = all_rows[:, :, :lines, :].reshape(-1, D)
-    chosen = (jnp.arange(NCLASS, dtype=jnp.int32)[:, None] == all_labels[None, :]).astype(
-        jnp.float32
-    )
-    table_rows = jnp.dot(chosen, conditions, precision=highest, preferred_element_type=jnp.float32)
-    strip = P_DIM * D
-    small_sum = jnp.concatenate(
-        [total[:strip].reshape(P_DIM, D), table_rows, total[strip : 2 * strip].reshape(P_DIM, D)]
-    ).T
     bias_count = biases.shape[0]
-    bias_sum = total[2 * strip : 2 * strip + bias_count]
-    total_loss = total[2 * strip + bias_count]
-    new_moment_small = momentum_decay * moment_small + small_sum
-    new_master_small = master_small - step_rates[1] * new_moment_small
-    new_moment_bias = momentum_decay * moment_bias + bias_sum
+    base = 2 * P_DIM * D
+    total_loss = total[base + bias_count]
+    new_moment_bias = momentum_decay * moment_bias + total[base : base + bias_count]
     new_biases = biases - step_rates[1] * new_moment_bias
-    factor_rows, *small = lax.optimization_barrier(
-        (
-            factor_right.T,
-            total_loss,
-            new_master_small,
-            new_moment_small,
-            new_biases,
-            new_moment_bias,
-        )
-    )
-    total_loss, new_master_small, new_moment_small, new_biases, new_moment_bias = small
-    new_master, new_moment, new_error, right_rows = compress(
-        step_rates, own, received, error_big, factor_rows, moment_big, master_big
-    )
     return (
         total_loss,
         new_master,
         new_moment,
         new_error,
         right_rows.T,
-        new_master_small,
-        new_moment_small,
+        new_master_small.T,
+        new_moment_small.T,
         new_biases,
         new_moment_bias,
     )

time: 389 us -> 343 us (0.88)
  local copies, waits for them, and re-layouts: 50.5 us -> 21 us
  matrix products: 52.6 us -> 43 us
  other arithmetic: 28.7 us -> 23.1 us
    dynamic_slice x1 -> x0, local copies, waits for them, and re-layouts: 17.4 us -> none  [on_pair(): lax.dynamic_slice_in_dim(low_grad, (1 - shard) * cols, cols, axis=1)]
    unnamed x52 -> x42, local copies, waits for them, and re-layouts: 18.6 us -> 10.4 us
    dot_general x7, matrix products: 32.7 us -> 26.1 us  [outer_sum(): lax.dot_general(left_side, right_side, (((0,), (0,)), ((), ())), preferre...]
    sub x1 -> x0, other arithmetic: 6.14 us -> none  [on_pair(): new_master_small = master_small - step_rates[1] * new_moment_small]
    pallas_call x2, Pallas kernels: 72.7 us -> 68 us  [the longest x1 59.8 us: compress(): pl.pallas_call(tail_kernel, out_shape=(pltpu.VMEM((EARLY, rows, BLOCK), j...]
    pallas_call x1, Pallas kernels: 41.1 us -> 45.6 us  [compress(): pl.pallas_call(update_kernel, out_shape=(sds(master.shape), sds(moment.sh...]
  transfers between devices with their start and end apart: 2 -> 1, of which waited for: 1 -> 1; matrix products, arithmetic and copies ran while one was open for 8% -> 4% of each run, Pallas kernels for 8% -> 0%
where the time goes in v3:
time: 343 us; the launch traced here: 338 us
  Pallas kernels  205 us (60%)
  matrix products  43 us (13%)
  waiting for transfers between devices  30.4 us (9%)
  other arithmetic  23.1 us (7%)
  local copies, waits for them, and re-layouts  21 us (6%)
  between operations  15.6 us (5%)
    pallas_call x1, Pallas kernels, run_images(): pl.pallas_call(functools.partial(image_kernel, entries), grid=(images,),...  91 us
    pallas_call x1, Pallas kernels, compress(): pl.pallas_call(tail_kernel, out_shape=(pltpu.VMEM((EARLY, rows, BLOCK), j...  59.8 us
    pallas_call x1, Pallas kernels, compress(): pl.pallas_call(update_kernel, out_shape=(sds(master.shape), sds(moment.sh...  45.6 us
    all_gather x1, waiting for transfers between devices, on_pair(): lax.all_gather(master_big.astype(half_type), 'shard', axis=1, tiled=True)  30.4 us
    dot_general x7, matrix products, outer_sum(): lax.dot_general(left_side, right_side, (((0,), (0,)), ((), ())), preferre...  26.1 us
    convert_element_type x1, other arithmetic, on_pair(): master_big.astype(half_type)  13.1 us
    unnamed x42, local copies, waits for them, and re-layouts  10.4 us
    dot_general x3, matrix products, multiply_trans(): lax.dot_general(left_side, right_side, (((1,), (1,)), ((), ())), preferre...  9.17 us
  transfers between devices with their start and end apart: 1, of which 1 were waited for; matrix products, arithmetic and copies ran while one was open for 4% of the time, Pallas kernels for 0%

profile of v3, /device:TPU:0, one launch (start us, length us, event | category | flops | bytes accessed | tf_op | source)
XLA Modules:
  0.0 337.8 jit_solution(15933353782398204116)
XLA Ops:
  7.2 0.0 all-gather.2.cloned.1.call-start
  7.2 13.1 %convert_element_type.70 = bf16[768,8192]{1,0:T(8,128)(2,1)} convert(f32[768,8192]{1,0:T(8,128)} %master_hbm.1) | non-fusion elementwise | flops 6291456 | bytes 37748736 | tf_op jit(solution)/shard_map/convert_element_type | solution.py:1540
  20.4 0.0 copy-start.9
  20.4 0.0 copy-start.11
  20.4 0.0 copy-start.3
  20.4 0.0 all-gather.2.cloned.1.call-update
  20.4 0.8 copy-done.6
  21.2 0.6 slice.76
  21.8 0.6 broadcast_in_dim.17.qkv_bias_ref
  22.4 0.6 broadcast_in_dim.18.output_bias_ref
  23.0 0.6 broadcast_in_dim.20.down_bias_ref
  23.6 0.6 broadcast_in_dim.21.patch_bias_ref
  24.2 1.3 convert.33
  25.5 0.0 copy-done.7
  25.5 1.0 reshape.101.targets_ref
  26.5 0.0 copy-done.9
  26.5 0.9 reshape.100.patches_ref
  27.5 0.6 slice.83
  28.1 1.9 multiply_sine_fusion.1
  30.0 1.1 pad_maximum_fusion.place_ref
  31.1 0.1 fusion.33
  31.2 0.5 slice_bitcast_fusion.2.head_bias_ref
  31.8 1.4 slice_bitcast_fusion
  33.2 30.4 %all-gather.2.cloned.1.call-done.weights_hbm = bf16[768,16384]{1,0:T(8,128)(2,1)} async-done(((bf16[768,8192]{1,0:T(8,128)(2,1)}), bf16[768,16384]{1,0:T(8,128)(2,1)}) %all-gather.2.cloned.1.call-update) | async-done | bytes 25165840 | tf_op jit(solution)/shard_map/all_gather | solution.py:1540
  63.6 1.2 convolution_add_fusion
  64.8 1.6 convolution_add_fusion.1
  66.4 1.1 fusion.16
  67.5 5.0 %fusion.5 = f32[4,6144]{1,0:T(4,128)S(1)} fusion(bf16[768,16384]{1,0:T(8,128)(2,1)} %all-gather.2.cloned.1.call-done.weights_hbm, f32[6144]{0:T(1024)S(1)} %slice-done, f32[4,768]{1,0:T(4,128)S(1)} %fusion.16), kind=kOutput, calls=%fused_computation.6 | convolution fusion | flops 37788672 | bytes 9572352 | tf_op jit(solution)/shard_map/dot_general | solution.py:30
  72.5 0.7 copy.39
  73.2 91.0 %images.1 = (bf16[1024,768]{1,0:T(8,128)(2,1)}, bf16[1024,768]{1,0:T(8,128)(2,1)}, bf16[1024,768]{1,0:T(8,128)(2,1)}, bf16[1024,3072]{1,0:T(8,128)(2,1)}, bf16[1...) custom-call(bf16[1024,16]{1,0:T(8,128)(2,1)} %reshape.100.patches_re, ...), custom_call_target="tpu_custom_call" | custom-call | tf_op jit(solution)/shard_map/images/pallas_call | solution.py:1391
  164.2 0.0 copy-start.10
  164.2 0.0 copy-start.12
  164.2 0.9 convert_reduce_fusion
  165.2 0.7 slice_reduce_fusion
  165.9 0.8 reshape.103
  166.7 0.8 reshape.105
  167.5 0.7 reduce.3
  168.2 0.6 reduce.4
  168.9 0.7 reduce.5
  169.6 1.2 reduce_sum.42
  170.8 6.2 %convert_reduce_fusion.2 = (f32[768]{0:T(1024)S(1)}, f32[4,768]{1,0:T(4,128)S(1)}) fusion(f32[4,768]{1,0:T(4,128)S(1)} %fusion.16, bf16[4,6144]{1,0:T(4,128)(2,1)S(1)} %bitcast.55, bf16[768,16384]{1,0:T(8,128)(2,1)} %all-gather.2.cloned.1.call-done.weights_hbm), kind=kOutput, calls=%fused_computation.53 | convolution fusion | flops 37784832 | bytes 9513984 | tf_op jit(solution)/shard_map/dot_general | solution.py:34
  177.7 1.7 convert_reduce_fusion.1
  179.5 0.1 concatenate.28
  179.6 0.0 copy-start.15
  179.6 6.8 %fusion.10 = bf16[768,16384]{1,0:T(8,128)(2,1)S(1)} fusion(bf16[1024,768]{1,0:T(8,128)(2,1)} %get-tuple-element.45, bf16[1024,2304]{1,0:T(8,128)(2,1)} %get-tuple-element.46), kind=kOutput, calls=%fused_computation.12 | convolution fusion | flops 3625648128 | bytes 9830400 | tf_op jit(solution)/shard_map/dot_general | solution.py:40
  186.5 0.0 slice-start.1
  186.5 1.5 fusion.13
  188.0 0.0 slice-start.2
  188.0 8.4 %fusion.9 = bf16[768,16384]{1,0:T(8,128)(2,1)S(1)} fusion(bf16[768,16384]{1,0:T(8,128)(2,1)S(1)} %fusion.13, bf16[1024,768]{1,0:T(8,128)(2,1)S(1)} %copy-done.14, bf16[1024,3072]{1,0:T(8,128)(2,1)} %get-tuple-element.50), kind=kOutput, calls=%fused_computation.10 | convolution fusion | flops 4834197504 | bytes 12582912 | tf_op jit(solution)/shard_map/dot_general | solution.py:40
  196.3 0.0 slice-done.1
  196.4 5.7 %fusion.8 = bf16[768,16384]{1,0:T(8,128)(2,1)S(1)} fusion(bf16[768,16384]{1,0:T(8,128)(2,1)S(1)} %fusion.9, bf16[1024,768]{1,0:T(8,128)(2,1)S(1)} %copy-done.13, bf16[1024,3072]{1,0:T(8,128)(2,1)S(1)} %bitcast.68), kind=kOutput, calls=%fused_computation.8 | convolution fusion | flops 4834197504 | bytes 12582912 | tf_op jit(solution)/shard_map/dot_general | solution.py:40
  202.1 0.0 copy-start.2
  202.1 2.9 fusion
  205.0 0.5 fusion.14
  205.6 0.1 pad.17
  205.7 0.3 fusion.15.grad_hbm
  206.0 0.0 copy-start.5
  206.0 8.9 %copy-done.5 = bf16[768,16384]{1,0:T(8,128)(2,1)} copy-done((bf16[768,16384]{1,0:T(8,128)(2,1)}, bf16[768,16384]{1,0:T(8,128)(2,1)S(1)}, u32[]{:S(2)}) %copy-start.5) | copy-done | bytes 25165848
  214.9 59.8 %compress.1 = (f32[10,768,512]{2,1,0:T(8,128)S(1)}, bf16[16,8,512]{2,1,0:T(8,128)(2,1)S(1)}, bf16[768,128]{1,0:T(8,128)(2,1)S(1)}, f32[2,16,16,128]{3,2,1,0:T(8,...) custom-call(bf16[768,16384]{1,0:T(8,128)(2,1)} %copy-done.5, ...), custom_call_target="tpu_custom_call" | custom-call | tf_op jit(solution)/shard_map/compress/pallas_call | solution.py:983
  274.8 0.0 copy-start.8
  274.8 45.6 %update.1 = (f32[768,8192]{1,0:T(8,128)}, f32[768,8192]{1,0:T(8,128)}, f32[1,768,8192]{2,1,0:T(8,128)}, f32[8,8192]{1,0:T(8,128)}) custom-call(f32[2]{0:T(128)S(1)} %copy-done.3, f32[16,768,512]{2,1,0:T(8,128)} %get-tuple-element.63.m_hbm, f32[10,768,512]{2,1,0:T(8,128)S(1)} %get-tuple-element.64.v_ref, bf16[16,8,512]{2,1,0:T(8,128)(2,1)S(1)} %get-tuple-element.65.whole_ref, ...), custom_call_target="tpu_custom_call" | custom-call | tf_op jit(solution)/shard_map/update/pallas_call | solution.py:1031
  320.5 0.6 slice.90
  321.0 1.3 multiply_subtract_fusion
  322.3 8.2 %update_small.1 = (f32[1032,768]{1,0:T(8,128)}, f32[1032,768]{1,0:T(8,128)}) custom-call(f32[2]{0:T(128)} %rates_ref.3, f32[512,128]{1,0:T(8,128)} %bitcast.50, f32[2,16,56,128]{3,2,1,0:T(8,128)} %copy-done, f32[1032,768]{1,0:T(8,128)} %bitcast.54, f32[1032,768]{1,0:T(8,128)} %bitcast.53), custom_call_target="tpu_custom_call" | custom-call | tf_op jit(solution)/shard_map/update_small/pallas_call | solution.py:1102
  (44 shorter events, 0.2 us)
Async XLA Ops:
  7.2 56.4 %all-gather.2.cloned.1.call-start = ((), (), s32[]{:S(2)}) async-start(), calls=%async_computation | async-start | bytes 37748736 | tf_op jit(solution)/shard_map/all_gather | solution.py:1540
  20.4 0.8 copy-start.6
  20.4 1.4 copy-start.17
  20.4 3.9 %copy-start.4 = (f32[768,1032]{0,1:T(8,128)S(1)}, f32[768,1032]{0,1:T(8,128)}, u32[]{:S(2)}) copy-start(f32[768,1032]{0,1:T(8,128)} %param.21) | copy-start | bytes 9510916
  20.4 5.2 %copy-start.7 = (f32[4,4096]{1,0:T(4,128)S(1)}, f32[4,4096]{1,0:T(4,128)}, u32[]{:S(2)}) copy-start(f32[4,4096]{1,0:T(4,128)} %param.14) | copy-start | bytes 196612
  20.4 6.2 %copy-start.9 = (bf16[4,4096]{1,0:T(4,128)(2,1)S(1)}, bf16[4,4096]{1,0:T(4,128)(2,1)}, u32[]{:S(2)}) copy-start(bf16[4,4096]{1,0:T(4,128)(2,1)} %param.13) | copy-start | bytes 98308
  20.4 7.1 %copy-start.11 = (s32[4]{0:T(128)S(1)}, s32[4]{0:T(128)}, u32[]{:S(2)}) copy-start(s32[4]{0:T(128)} %param.16) | copy-start | bytes 52
  20.4 7.1 %copy-start.3 = (f32[2]{0:T(128)S(1)}, f32[2]{0:T(128)}, u32[]{:S(2)}) copy-start(f32[2]{0:T(128)} %rates_ref.3) | copy-start | bytes 28
  24.2 43.3 %slice-start = ((f32[14608]{0:T(1024)}), f32[6144]{0:T(1024)S(1)}, s32[]{:S(2)}) async-start(f32[14608]{0:T(1024)} %param.23), calls=%async_computation.1 | async-start | bytes 49152 | tf_op jit(solution)/shard_map/concatenate | solution.py:1454
  164.2 15.2 %copy-start.10 = (f32[1,3072]{1,0:T(1,128)S(1)}, f32[1,3072]{1,0:T(1,128)}, u32[]{:S(2)}) copy-start(f32[1,3072]{1,0:T(1,128)} %get-tuple-element.58) | copy-start | bytes 36868
  164.2 15.2 %copy-start.12 = (f32[1,16]{1,0:T(1,128)S(1)}, f32[1,16]{1,0:T(1,128)}, u32[]{:S(2)}) copy-start(f32[1,16]{1,0:T(1,128)} %get-tuple-element.61) | copy-start | bytes 196
  179.6 6.9 %copy-start.15 = (bf16[1024,768]{1,0:T(8,128)(2,1)S(1)}, bf16[1024,768]{1,0:T(8,128)(2,1)}, u32[]{:S(2)}) copy-start(bf16[1024,768]{1,0:T(8,128)(2,1)} %get-tuple-element.47) | copy-start | bytes 4718596
  179.6 6.9 %copy-start.16 = (bf16[1024,768]{1,0:T(8,128)(2,1)S(1)}, bf16[1024,768]{1,0:T(8,128)(2,1)}, u32[]{:S(2)}) copy-start(bf16[1024,768]{1,0:T(8,128)(2,1)} %get-tuple-element.48) | copy-start | bytes 4718596
  186.4 1.5 copy-start.14
  186.5 9.9 %slice-start.1 = ((s8[6291456]{0:T(1024)(128)(4,1)}), s8[4194304]{0:T(1024)(128)(4,1)S(1)}, s32[]{:S(2)}) async-start(s8[6291456]{0:T(1024)(128)(4,1)} %bitcast.67), calls=%async_computation.2 | async-start | bytes 8388608
  188.0 8.4 %slice-start.2 = ((s8[6291456]{0:T(1024)(128)(4,1)}), s8[2097152]{0:T(1024)(128)(4,1)S(1)}, s32[]{:S(2)}) async-start(s8[6291456]{0:T(1024)(128)(4,1)} %bitcast.67), calls=%async_computation.3 | async-start | bytes 4194304
  188.0 8.4 %copy-start.13 = (bf16[1024,768]{1,0:T(8,128)(2,1)S(1)}, bf16[1024,768]{1,0:T(8,128)(2,1)}, u32[]{:S(2)}) copy-start(bf16[1024,768]{1,0:T(8,128)(2,1)} %get-tuple-element.51) | copy-start | bytes 4718596
  202.1 12.8 %copy-start.2 = (f32[8192,8]{0,1:T(8,128)S(1)}, f32[8192,8]{0,1:T(8,128)}, u32[]{:S(2)}) copy-start(f32[8192,8]{0,1:T(8,128)} %param.20) | copy-start | bytes 786436
  206.0 8.9 %copy-start.5 = (bf16[768,16384]{1,0:T(8,128)(2,1)}, bf16[768,16384]{1,0:T(8,128)(2,1)S(1)}, u32[]{:S(2)}) copy-start(bf16[768,16384]{1,0:T(8,128)(2,1)S(1)} %fusion.15.grad_hbm) | copy-start | bytes 75497472
  274.8 45.7 %copy-start = (f32[2,16,56,128]{3,2,1,0:T(8,128)}, f32[2,16,56,128]{3,2,1,0:T(8,128)S(1)}, u32[]{:S(2)}) copy-start(f32[2,16,56,128]{3,2,1,0:T(8,128)S(1)} %get-tuple-element.78.lines_ref) | copy-start | bytes 2752516
  274.8 46.3 %copy-start.1 = (f32[2,16,16,128]{3,2,1,0:T(8,128)}, f32[2,16,16,128]{3,2,1,0:T(8,128)S(1)}, u32[]{:S(2)}) copy-start(f32[2,16,16,128]{3,2,1,0:T(8,128)S(1)} %get-tuple-element.73) | copy-start | bytes 786436
  274.8 46.3 %copy-start.8 = (f32[14608]{0:T(1024)S(1)}, f32[14608]{0:T(1024)}, u32[]{:S(2)}) copy-start(f32[14608]{0:T(1024)} %param.24) | copy-start | bytes 175300
Sparse Core Ops, SparseCore 0:
  20.6 42.9 all-gather.1

commit v4 on v3

--- a/solution.py
+++ b/solution.py
@@ -490,9 +490,9 @@
 MESH = pl.DeviceIdType.MESH
 BLOCK = 512
 PIECE = 256
-EARLY = 10
-KERNEL_BYTES = 18_000_000
-EXCHANGE_BYTES = 36_000_000
+EARLY = 5
+KERNEL_BYTES = 34_000_000
+EXCHANGE_BYTES = 50_000_000
 RANK = 8
 LANES = 128
 REPS = 16
@@ -516,7 +516,16 @@
 
 
 def tail_kernel(
-    grad_hbm,
+    attn_in_hbm,
+    mixed_hbm,
+    mlp_in_hbm,
+    grad_mlp_hbm,
+    grad_qkv_hbm,
+    grad_attn_hbm,
+    grad_pre_hbm,
+    hidden_hbm,
+    tail_left_ref,
+    tail_right_ref,
     error_hbm,
     factor_ref,
     moment_hbm,
@@ -530,8 +539,12 @@
     recv_hbm,
     m_hbm,
     m_ref,
-    own_ref,
+    error_ref,
     recv_ref,
+    left_stage,
+    turned_ref,
+    right_ref,
+    ring_ref,
     stack_ref,
     left_acc,
     left_ref,
@@ -545,7 +558,8 @@
     share_ref,
     small_ref,
     load_sem,
-    own_sem,
+    stage_sem,
+    right_sem,
     recv_sem,
     moment_sem,
     left_send,
@@ -559,25 +573,26 @@
     m_sem,
 ):
     blocks = m_ref.shape[0]
-    cols = recv_hbm.shape[1]
     shard = lax.axis_index("shard")
     rep = lax.axis_index("rep")
     partner = (1 - shard, rep)
+    shared = blocks - 14 * shard
+    shared_there = 2 + 14 * shard
     peers = [(shard, lax.rem(rep + step, REPS)) for step in range(1, REPS)]
     barrier, count = greet([partner] + peers)
 
     def columns(block):
         return pl.ds(pl.multiple_of(block * BLOCK, BLOCK), BLOCK)
 
-    def part_columns(part, block):
-        return pl.ds(pl.multiple_of(part * cols + block * BLOCK, BLOCK), BLOCK)
-
-    def send_grad(block):
+    ring = ring_ref.shape[0]
+
+    def send_piece(local):
+        slot = lax.rem(local, ring)
         return pltpu.make_async_remote_copy(
-            src_ref=grad_hbm.at[:, part_columns(1 - shard, block)],
-            dst_ref=recv_hbm.at[:, columns(block)],
-            send_sem=grad_send.at[block],
-            recv_sem=grad_recv.at[block],
+            src_ref=ring_ref.at[slot],
+            dst_ref=recv_hbm.at[:, pl.ds(pl.multiple_of(local * PIECE, PIECE), PIECE)],
+            send_sem=grad_send.at[slot],
+            recv_sem=grad_recv.at[local],
             device_id=partner,
             device_id_type=MESH,
         )
@@ -599,15 +614,23 @@
                 slots.at[other], slots.at[other], base, base + other, peers[step - 1]
             ).wait_recv()
 
-    def load_error(block):
+    def load_error(block, slot):
         return pltpu.make_async_copy(
-            error_hbm.at[0, :, columns(block)], m_ref.at[block], load_sem.at[block]
-        )
-
-    def load_own(block, slot):
-        return pltpu.make_async_copy(
-            grad_hbm.at[:, part_columns(shard, block)], own_ref.at[slot], own_sem.at[slot]
-        )
+            error_hbm.at[0, :, columns(block)], error_ref.at[slot], load_sem.at[slot]
+        )
+
+    def block_of(step):
+        return lax.rem(step + 2 * shard, blocks)
+
+    def start_loads(step):
+        block, slot = block_of(step), lax.rem(step, depth)
+        load_error(block, slot).start()
+
+        @pl.when(block < shared)
+        def _():
+            send_piece(2 * block).wait_recv()
+            send_piece(2 * block + 1).wait_recv()
+            load_recv(block, slot).start()
 
     def load_recv(block, slot):
         return pltpu.make_async_copy(
@@ -622,16 +645,29 @@
             moment_hbm.at[:, columns(block)], v_ref.at[block], moment_sem.at[block]
         )
 
-    depth = own_ref.shape[0]
-
-    for block in range(depth):
-        load_error(block).start()
-        load_own(block, block).start()
+    depth = error_ref.shape[0]
+    lefts = [attn_in_hbm, mixed_hbm, mlp_in_hbm, grad_mlp_hbm]
+    rights = [grad_qkv_hbm, grad_attn_hbm, grad_pre_hbm, hidden_hbm]
+    window = right_ref.shape[0]
+    halves = 2 * blocks
+
+    def load_left(part):
+        return pltpu.make_async_copy(lefts[part], left_stage, stage_sem.at[0])
+
+    def load_right(part, index):
+        slot = lax.rem(index, window)
+        return pltpu.make_async_copy(
+            rights[part].at[:, pl.ds(pl.multiple_of(index * PIECE, PIECE), PIECE)],
+            right_ref.at[slot],
+            right_sem.at[slot],
+        )
+
+    load_left(0).start()
+    for index in range(window):
+        load_right(0, index).start()
     pl.semaphore_wait(barrier, count)
     own_half = small_copy(sums_ref.at[1 - shard], half_ref, 16, 16, partner)
     own_half.start()
-    for block in range(blocks):
-        send_grad(block).start()
     rows_out = [
         small_copy(rows_ref, gathered_ref.at[shard, rep], step, rep, peers[step - 1])
         for step in range(1, REPS)
@@ -645,34 +681,77 @@
     stack_ref[0:RANK] = high
     stack_ref[RANK : 2 * RANK] = low
     left_acc[...] = jnp.zeros_like(left_acc)
-    for block in range(depth):
-        send_grad(block).wait_recv()
-        load_recv(block, block).start()
-
-    def gather_block(block, carry):
-        slot = lax.rem(block, depth)
-        load_error(block).wait()
-        load_own(block, slot).wait()
-        load_recv(block, slot).wait()
-        matrix = (
-            own_ref[slot].astype(jnp.float32) + recv_ref[slot].astype(jnp.float32) + m_ref[block]
-        )
-        m_ref[block] = matrix
+    edge = 0
+    for part in range(4):
+        number = rights[part].shape[1] // PIECE
+        load_left(part).wait()
+        turned_ref[...] = left_stage[...].T
+        if part < 3:
+            load_left(part + 1).start()
+
+        def grad_piece(index, carry):
+            load_right(part, index).wait()
+            grad = multiply(turned_ref[...], right_ref[lax.rem(index, window)])
+
+            @pl.when(index + window < number)
+            def _():
+                load_right(part, index + window).start()
+
+            place = edge + index
+            low_half = place < halves
+            local = lax.rem(place, halves)
+            mine = jnp.logical_xor(low_half, shard == 1)
+
+            @pl.when(mine)
+            def _():
+                span = pl.ds(pl.multiple_of(lax.rem(local, 2) * PIECE, PIECE), PIECE)
+                m_ref[lax.div(local, 2), :, span] = grad
+
+            @pl.when(jnp.logical_not(mine))
+            def _():
+                @pl.when(local >= ring)
+                def _():
+                    send_piece(local - ring).wait_send()
+
+                ring_ref[lax.rem(local, ring)] = grad.astype(half_type)
+                send_piece(local).start()
+
+            return carry
+
+        lax.fori_loop(0, number, grad_piece, 0)
+        edge += number
+        if part < 3:
+            for index in range(min(window, rights[part + 1].shape[1] // PIECE)):
+                load_right(part + 1, index).start()
+    for step in range(depth):
+        start_loads(step)
+
+    def gather_block(step, carry):
+        block, slot = block_of(step), lax.rem(step, depth)
+        load_error(block, slot).wait()
+
+        @pl.when(block < shared)
+        def _():
+            load_recv(block, slot).wait()
+            m_ref[block] = m_ref[block] + recv_ref[slot].astype(jnp.float32) + error_ref[slot]
+
+        @pl.when(block >= shared)
+        def _():
+            m_ref[block] = error_ref[slot] + multiply(
+                tail_left_ref[...], tail_right_ref[:, columns(block - shared)]
+            )
+
         save_matrix(block).start()
-        high, low = split_two(matrix)
+        high, low = split_two(m_ref[block])
         factor = stack_ref[:, columns(block)]
         left_acc[...] += multiply_trans(high, factor) + multiply_trans(low, factor)
 
-        @pl.when(block + depth < blocks)
+        @pl.when(step + depth < blocks)
         def _():
-            load_error(block + depth).start()
-            load_own(block + depth, slot).start()
-            send_grad(block + depth).wait_recv()
-            load_recv(block + depth, slot).start()
+            start_loads(step + depth)
 
         return carry
 
-    lax.fori_loop(0, blocks // 2, gather_block, 0)
     own_half.wait()
     half_ref[...] = half_ref[...] + sums_ref[shard]
     shares_out = [
@@ -688,7 +767,7 @@
     for copy in shares_out:
         copy.start()
     share_ref[rep] = half_ref[rep]
-    lax.fori_loop(blocks // 2, blocks, gather_block, 0)
+    lax.fori_loop(0, blocks, gather_block, 0)
     for block in range(v_ref.shape[0]):
         load_moment(block).start()
 
@@ -836,8 +915,14 @@
         right_copy(mine_ref, whole_ref.at[other], REPS, step, other).wait_recv()
     for copy in scatter + spread + rows_out + shares_out + whole_out:
         copy.wait_send()
+
+    def sent_piece(local, carry):
+        send_piece(local).wait_send()
+        return carry
+
+    sent = 2 * shared_there
+    lax.fori_loop((halves - ring) * shard, sent, sent_piece, 0)
     for block in range(blocks):
-        send_grad(block).wait_send()
         save_matrix(block).wait()
     rows_across.wait()
     total_across.wait()
@@ -973,11 +1058,11 @@
         out_master(block, block % slots).wait()
 
 
-def compress(rates, grads, error, factor_rows, moment, master, sums, lines):
+def compress(rates, sides, tail_left, tail_right, error, factor_rows, moment, master, sums, lines):
     rows, cols = master.shape
     blocks = cols // BLOCK
     depth = 3
-    slots = 6
+    slots = 8
     hbm = pl.BlockSpec(memory_space=pltpu.HBM)
     vmem = pl.BlockSpec(memory_space=pltpu.VMEM)
     moments, whole, basis, total, gathered, unused, matrices = pl.pallas_call(
@@ -991,12 +1076,16 @@
             pltpu.HBM((rows, cols), half_type),
             pltpu.HBM((blocks, rows, BLOCK), jnp.float32),
         ),
-        in_specs=[hbm, hbm, vmem, hbm, vmem, vmem],
+        in_specs=[hbm] * 8 + [vmem, vmem, hbm, vmem, hbm, vmem, vmem],
         out_specs=[vmem] * 5 + [pl.BlockSpec(memory_space=pltpu.HBM)] * 2,
         scratch_shapes=[
             pltpu.VMEM((blocks, rows, BLOCK), jnp.float32),
+            pltpu.VMEM((depth, rows, BLOCK), jnp.float32),
             pltpu.VMEM((depth, rows, BLOCK), half_type),
-            pltpu.VMEM((depth, rows, BLOCK), half_type),
+            pltpu.VMEM(sides[0].shape, half_type),
+            pltpu.VMEM(sides[0].shape[::-1], half_type),
+            pltpu.VMEM((4, sides[0].shape[0], PIECE), half_type),
+            pltpu.VMEM((4, rows, PIECE), half_type),
             pltpu.VMEM((LANES, cols), half_type),
             pltpu.VMEM((rows, LANES), jnp.float32),
             pltpu.VMEM((RANK, rows), jnp.float32),
@@ -1009,16 +1098,17 @@
             pltpu.VMEM(sums.shape[1:], jnp.float32),
             pltpu.VMEM(sums.shape[1:], jnp.float32),
             pltpu.VMEM(sums.shape[2:], jnp.float32),
-            pltpu.SemaphoreType.DMA((blocks,)),
             pltpu.SemaphoreType.DMA((depth,)),
+            pltpu.SemaphoreType.DMA((1,)),
+            pltpu.SemaphoreType.DMA((4,)),
             pltpu.SemaphoreType.DMA((depth,)),
             pltpu.SemaphoreType.DMA((blocks,)),
             pltpu.SemaphoreType.DMA((8,)),
             pltpu.SemaphoreType.DMA((8,)),
             pltpu.SemaphoreType.DMA((2 * REPS,)),
             pltpu.SemaphoreType.DMA((2 * REPS,)),
-            pltpu.SemaphoreType.DMA((blocks,)),
-            pltpu.SemaphoreType.DMA((blocks,)),
+            pltpu.SemaphoreType.DMA((4,)),
+            pltpu.SemaphoreType.DMA((2 * blocks,)),
             pltpu.SemaphoreType.DMA((51,)),
             pltpu.SemaphoreType.DMA((51,)),
             pltpu.SemaphoreType.DMA((blocks,)),
@@ -1027,7 +1117,7 @@
             collective_id=2, has_side_effects=True, vmem_limit_bytes=EXCHANGE_BYTES
         ),
         name="compress",
-    )(grads, error, factor_rows, moment, sums, lines)
+    )(*sides, tail_left, tail_right, error, factor_rows, moment, sums, lines)
     updated = pl.pallas_call(
         update_kernel,
         out_shape=(
@@ -1060,11 +1150,11 @@
 ):
     step = pl.program_id(0)
     height = moment_ref.shape[0]
-    images = lines_ref.shape[0] * lines_ref.shape[1] * 8
+    images = lines_ref.shape[1] * 8
     strips = D // LANES
 
     def piece(place):
-        return lines_ref[:, :, place * 8 : (place + 1) * 8, :].reshape(images, LANES)
+        return lines_ref[1, :, place * 8 : (place + 1) * 8, :].reshape(images, LANES)
 
     labels = piece(strips)[:, 0:1]
     place = lax.broadcasted_iota(jnp.int32, (images, height), 1) + (step * height - P_DIM)
@@ -1144,7 +1234,7 @@
     entries,
     patches_ref,
     targets_ref,
-    mods_ref,
+    both_mods_ref,
     place_ref,
     patch_weight_ref,
     head_weight_ref,
@@ -1154,7 +1244,7 @@
     down_bias_ref,
     patch_bias_ref,
     head_bias_ref,
-    weights_hbm,
+    master_hbm,
     attn_in_ref,
     mixed_ref,
     mlp_in_ref,
@@ -1163,7 +1253,7 @@
     grad_attn_ref,
     grad_pre_ref,
     grad_mlp_ref,
-    mod_grad_ref,
+    both_grads_ref,
     grad_patch_ref,
     grad_head_ref,
     bias_qkv_ref,
@@ -1184,14 +1274,60 @@
     mlp_out_ref,
     grad_mixed_ref,
     total_ref,
-    sem,
+    stage_ref,
+    mods_ref,
+    got_mods_ref,
+    mod_grad_ref,
+    got_grads_ref,
+    stage_sem,
+    weight_send,
+    weight_recv,
+    mod_send,
+    mod_recv,
 ):
     image = pl.program_id(0)
+    last = pl.num_programs(0) - 1
+    images = mods_ref.shape[0]
     edges = [0, 3 * D, 4 * D, 4 * D + FF, 4 * D + 2 * FF]
-
-    def load(part):
-        span = slice(edges[part], edges[part + 1])
-        return pltpu.make_async_copy(weights_hbm.at[:, span], weight_ref.at[:, span], sem.at[part])
+    shard = lax.axis_index("shard")
+    partner = (1 - shard, lax.axis_index("rep"))
+    cols = master_hbm.shape[1]
+    first_count = cols // BLOCK
+    all_count = edges[4] // BLOCK
+    count = first_count - (2 * first_count - all_count) * shard
+    depth = stage_ref.shape[0]
+
+    def load(block):
+        slot = lax.rem(block, depth)
+        return pltpu.make_async_copy(
+            master_hbm.at[:, pl.ds(pl.multiple_of(block * BLOCK, BLOCK), BLOCK)],
+            stage_ref.at[slot],
+            stage_sem.at[slot],
+        )
+
+    def weight_copy(block):
+        span = pl.ds(pl.multiple_of(block * BLOCK, BLOCK), BLOCK)
+        return pltpu.make_async_remote_copy(
+            src_ref=weight_ref.at[:, span],
+            dst_ref=weight_ref.at[:, span],
+            send_sem=weight_send.at[block],
+            recv_sem=weight_recv.at[block],
+            device_id=partner,
+            device_id_type=MESH,
+        )
+
+    def mod_copy(source, target, place):
+        return pltpu.make_async_remote_copy(
+            src_ref=source,
+            dst_ref=target,
+            send_sem=mod_send.at[place],
+            recv_sem=mod_recv.at[place],
+            device_id=partner,
+            device_id_type=MESH,
+        )
+
+    mods_across = mod_copy(both_mods_ref.at[pl.ds(images, images)], got_mods_ref, 0)
+    grads_across = mod_copy(mod_grad_ref, got_grads_ref, 1)
 
     sums = [
         grad_patch_ref,
@@ -1207,18 +1343,48 @@
 
     @pl.when(image == 0)
     def _():
-        for part in range(4):
-            load(part).start()
+        for block in range(2):
+            load(block).start()
+        barrier, greeted = greet([partner])
+        pl.semaphore_wait(barrier, greeted)
+        mods_across.start()
         for total in sums:
             total[...] = jnp.zeros_like(total)
 
+        def cast(block, carry):
+            @pl.when(block + 2 < count)
+            def _():
+                load(block + 2).start()
+
+            load(block).wait()
+            place = shard * first_count + block
+            weight_ref[:, pl.ds(pl.multiple_of(place * BLOCK, BLOCK), BLOCK)] = stage_ref[
+                lax.rem(block, depth)
+            ].astype(half_type)
+            weight_copy(place).start()
+            return carry
+
+        lax.fori_loop(0, count, cast, 0)
+        mods_across.wait_recv()
+        mods_ref[...] = jnp.where(shard == 1, both_mods_ref[0:images], got_mods_ref[...])
+
+    stops = [-(-edge // BLOCK) for edge in edges]
+
     def arrived(part):
-        @pl.when(image == 0)
+        @pl.when(jnp.logical_and(image == 0, shard == 1))
         def _():
-            load(part).wait()
+            for block in range(stops[part], min(stops[part + 1], first_count)):
+                weight_copy(block).wait_recv()
+
+        if stops[part + 1] > first_count:
+
+            @pl.when(jnp.logical_and(image == 0, shard == 0))
+            def _():
+                for block in range(first_count, all_count):
+                    weight_copy(block).wait_recv()
 
     def modulation(place):
-        return mods_ref[0, place : place + 1, :]
+        return mods_ref[image, place : place + 1, :]
 
     def weight(first, width):
         return weight_ref[:, pl.ds(first, width)]
@@ -1300,11 +1466,11 @@
     grad_head_ref[...] += outer_sum(grad_out, final_in)
 
     grad_final = multiply(grad_out, head_weight_ref[...])
-    mod_grad_ref[0, 6:7] = token_sum(grad_final)
-    mod_grad_ref[0, 7:8] = token_sum(grad_final * unit)
+    mod_grad_ref[image, 6:7] = token_sum(grad_final)
+    mod_grad_ref[image, 7:8] = token_sum(grad_final * unit)
     grad_stream = unit_back(unit, inverse_end, grad_final * (1.0 + modulation(7)))
     stream_ref[...] = grad_stream
-    mod_grad_ref[0, 5:6] = token_sum(grad_stream * mlp_out_ref[...])
+    mod_grad_ref[image, 5:6] = token_sum(grad_stream * mlp_out_ref[...])
     grad_mlp = (grad_stream * modulation(5)).astype(half_type)
     grad_mlp_ref[...] = grad_mlp
     bias_down_ref[...] += token_sum(grad_mlp.astype(jnp.float32))
@@ -1319,11 +1485,11 @@
         total_ref[...] += multiply_trans(grad_pre, weight(edges[2] + part * CHUNK, CHUNK))
     grad_in = total_ref[...]
     unit = unit_mid_ref[...]
-    mod_grad_ref[0, 3:4] = token_sum(grad_in)
-    mod_grad_ref[0, 4:5] = token_sum(grad_in * unit)
+    mod_grad_ref[image, 3:4] = token_sum(grad_in)
+    mod_grad_ref[image, 4:5] = token_sum(grad_in * unit)
     grad_stream = stream_ref[...] + unit_back(unit, inverse_mid, grad_in * (1.0 + modulation(4)))
     stream_ref[...] = grad_stream
-    mod_grad_ref[0, 2:3] = token_sum(grad_stream * attended_ref[...])
+    mod_grad_ref[image, 2:3] = token_sum(grad_stream * attended_ref[...])
     grad_attn = (grad_stream * modulation(2)).astype(half_type)
     grad_attn_ref[...] = grad_attn
     bias_output_ref[...] += token_sum(grad_attn.astype(jnp.float32))
@@ -1362,19 +1528,33 @@
     bias_qkv_ref[...] += token_sum(grad_qkv_ref[...].astype(jnp.float32))
     grad_in = multiply_trans(grad_qkv_ref[...], weight_ref[:, : edges[1]])
     unit = unit_start_ref[...]
-    mod_grad_ref[0, 0:1] = token_sum(grad_in)
-    mod_grad_ref[0, 1:2] = token_sum(grad_in * unit)
+    mod_grad_ref[image, 0:1] = token_sum(grad_in)
+    mod_grad_ref[image, 1:2] = token_sum(grad_in * unit)
     grad_start = (
         stream_ref[...] + unit_back(unit, inverse_start, grad_in * (1.0 + modulation(1)))
     ).astype(half_type)
     bias_patch_ref[...] += token_sum(grad_start.astype(jnp.float32))
     grad_patch_ref[...] += outer_sum(patches, grad_start)
 
+    @pl.when(image == last)
+    def _():
+        grads_across.start()
+
+        def sent(block, carry):
+            weight_copy(shard * first_count + block).wait_send()
+            return carry
+
+        lax.fori_loop(0, count, sent, 0)
+        mods_across.wait_send()
+        both_grads_ref[0:images] = mod_grad_ref[...]
+        grads_across.wait()
+        both_grads_ref[images : 2 * images] = got_grads_ref[...]
+
 
 def run_images(
-    patches, targets, mods, places, patch_weight, head_weight, biases, gathered, entries
+    patches, targets, mods, places, patch_weight, head_weight, biases, master, entries
 ):
-    images = mods.shape[0]
+    images = mods.shape[0] // 2
     tokens = images * SEQ
     wide = 4 * D + 2 * FF
 
@@ -1387,18 +1567,17 @@
     vector = [(P_DIM, D), (P_DIM, D), (1, 3 * D), (1, D), (1, FF), (1, D), (1, D), (1, P_DIM)]
     vector = [sds(shape) for shape in vector + [(1, P_DIM)]]
     saved = [D, D, D, FF, 3 * D, D, FF, D]
-    per_image = pl.BlockSpec((1, 8, D), lambda image: (image, 0, 0))
     return pl.pallas_call(
         functools.partial(image_kernel, entries),
         grid=(images,),
         out_shape=[sds((tokens, width), half_type) for width in saved]
-        + [sds((images, 8, D))]
+        + [sds(mods.shape)]
         + vector,
-        in_specs=[rows(P_DIM), rows(P_DIM), per_image, fixed(places)]
+        in_specs=[rows(P_DIM), rows(P_DIM), fixed(mods), fixed(places)]
         + [fixed(patch_weight), fixed(head_weight)]
         + [fixed(bias) for bias in biases]
-        + [pl.BlockSpec(memory_space=pl.ANY)],
-        out_specs=[rows(width) for width in saved] + [per_image] + [fixed(item) for item in vector],
+        + [pl.BlockSpec(memory_space=pltpu.HBM)],
+        out_specs=[rows(width) for width in saved] + [fixed(mods)] + [fixed(item) for item in vector],
         scratch_shapes=[
             pltpu.VMEM((D, wide), half_type),
             pltpu.VMEM((SEQ, 3 * D), half_type),
@@ -1411,17 +1590,31 @@
             pltpu.VMEM((SEQ, D), jnp.float32),
             pltpu.VMEM((SEQ, D), half_type),
             pltpu.VMEM((SEQ, D), jnp.float32),
-            pltpu.SemaphoreType.DMA((4,)),
+            pltpu.VMEM((3, D, BLOCK), jnp.float32),
+            pltpu.VMEM((images, 8, D), jnp.float32),
+            pltpu.VMEM((images, 8, D), jnp.float32),
+            pltpu.VMEM((images, 8, D), jnp.float32),
+            pltpu.VMEM((images, 8, D), jnp.float32),
+            pltpu.SemaphoreType.DMA((3,)),
+            pltpu.SemaphoreType.DMA((wide // BLOCK,)),
+            pltpu.SemaphoreType.DMA((wide // BLOCK,)),
+            pltpu.SemaphoreType.DMA((2,)),
+            pltpu.SemaphoreType.DMA((2,)),
         ],
-        compiler_params=pltpu.CompilerParams(vmem_limit_bytes=60_000_000),
+        compiler_params=pltpu.CompilerParams(
+            collective_id=1, has_side_effects=True, vmem_limit_bytes=60_000_000
+        ),
         name="images",
-    )(patches, targets, mods, places, patch_weight, head_weight, *biases, gathered)
-
-
-def train_gradients(gathered, master_small, biases, noisy_patches, targets, timesteps, labels, entries):
-    edges = [0, 3 * D, 4 * D, 4 * D + FF, 4 * D + 2 * FF]
-    pieces = split_big(gathered)
-    modulate_weight, final_weight, embed_second, embed_first = pieces[4:]
+    )(patches, targets, mods, places, patch_weight, head_weight, *biases, master)
+
+
+def train_gradients(master, master_small, biases, noisy_patches, targets, timesteps, labels, entries):
+    owner = lax.axis_index("shard") == 1
+    last = master.shape[1]
+    first_edge = last - 9 * D - FREQ
+    both_weight, embed_second, embed_first = split_at(
+        master, [first_edge, last - D - FREQ, last - FREQ, last]
+    )
     patch_weight, class_table, head_weight = split_small(master_small)
     (
         query_bias,
@@ -1438,9 +1631,9 @@
     ) = split_bias(biases)
     images = noisy_patches.shape[0]
     frequency = timestep_features(timesteps).astype(half_type)
-    embed_pre = multiply_trans(frequency, embed_first) + first_bias
+    embed_pre = multiply_trans(frequency.astype(jnp.float32), embed_first) + first_bias
     embed_hidden = jax.nn.silu(embed_pre).astype(half_type)
-    time_embed = multiply(embed_hidden, embed_second) + second_bias
+    time_embed = multiply(embed_hidden.astype(jnp.float32), embed_second) + second_bias
     chosen = (labels[:, None] == jnp.arange(NCLASS, dtype=jnp.int32)[None, :]).astype(jnp.float32)
     condition = time_embed + lax.dot_general(
         chosen,
@@ -1450,8 +1643,7 @@
         preferred_element_type=jnp.float32,
     )
     active = jax.nn.silu(condition).astype(half_type)
-    both_weight = gathered[:, edges[4] : edges[4] + 8 * D]
-    mods = multiply(active, both_weight) + jnp.concatenate([modulate_bias, final_bias])
+    mods = multiply(active.astype(jnp.float32), both_weight) + jnp.concatenate([modulate_bias, final_bias])
     qkv_bias = jnp.concatenate([query_bias, jnp.zeros_like(query_bias), value_bias])
     (
         attn_in,
@@ -1475,33 +1667,32 @@
     ) = run_images(
         noisy_patches.reshape(-1, P_DIM),
         targets.reshape(-1, P_DIM),
-        mods.reshape(images, 8, D),
+        mods.reshape(-1, 8, D),
         position_table(),
         patch_weight.T.astype(half_type),
         head_weight.T.astype(half_type),
         [item[None] for item in (qkv_bias, output_bias, up_bias, down_bias, patch_bias, head_bias)],
-        gathered,
+        master,
         entries,
     )
-    grad_mods = mod_grads.reshape(images, 8 * D).astype(half_type)
+    grad_mods = mod_grads.reshape(-1, 8 * D).astype(half_type)
     bias_mods = column_sums(grad_mods)
-    grad_active = multiply_trans(grad_mods, both_weight)
+    grad_active = multiply_trans(grad_mods.astype(jnp.float32), both_weight)
     grad_condition = slope(jax.nn.silu, condition, grad_active)
     grad_embed = grad_condition.astype(half_type)
-    grad_embed_hidden = multiply_trans(grad_embed, embed_second)
+    grad_embed_hidden = multiply_trans(grad_embed.astype(jnp.float32), embed_second)
     grad_embed_pre = slope(jax.nn.silu, embed_pre, grad_embed_hidden).astype(half_type)
-    grad_big = jnp.concatenate(
+    tail_left = jnp.pad(
+        jnp.concatenate([active, embed_hidden, grad_embed_pre]), ((0, 8), (0, 0))
+    ).T
+    tail_right = jnp.concatenate(
         [
-            outer_sum(attn_in, grad_qkv),
-            outer_sum(mixed, grad_attn),
-            outer_sum(mlp_in, grad_pre),
-            outer_sum(grad_mlp, hidden),
-            outer_sum(active, grad_mods),
-            outer_sum(embed_hidden, grad_embed),
-            outer_sum(grad_embed_pre, frequency),
-        ],
-        axis=1,
-    )
+            jnp.pad(grad_mods, ((0, 0), (0, D + FREQ))),
+            jnp.pad(grad_embed, ((0, 0), (8 * D, FREQ))),
+            jnp.pad(frequency, ((0, 16 - frequency.shape[0]), (9 * D, 0))),
+        ]
+    )
+    sides = (attn_in, mixed, mlp_in, grad_mlp, grad_qkv, grad_attn, grad_pre, hidden)
     grad_bias = jnp.concatenate(
         [
             bias_qkv[0, :D],
@@ -1509,15 +1700,17 @@
             bias_output[0],
             bias_up[0],
             bias_down[0],
-            bias_mods,
-            column_sums(grad_embed),
-            column_sums(grad_embed_pre),
+            jnp.where(
+                owner,
+                jnp.concatenate([bias_mods, column_sums(grad_embed), column_sums(grad_embed_pre)]),
+                0.0,
+            ),
             bias_patch[0],
             bias_head[0],
         ]
     )
     loss_part = jnp.sum(losses) / entries
-    return grad_big, grad_patch, grad_head, grad_condition, grad_bias, loss_part
+    return sides, tail_left, tail_right, grad_patch, grad_head, grad_condition, grad_bias, loss_part
 
 
 def on_pair(
@@ -1537,10 +1730,15 @@
 ):
     shards = lax.axis_size("shard")
     replicas = lax.axis_size("rep")
-    gathered = lax.all_gather(master_big.astype(half_type), "shard", axis=1, tiled=True)
     entries = noisy_patches.shape[0] * shards * replicas * SEQ * P_DIM
-    grad_big, grad_patch, grad_head, grad_condition, grad_bias, loss_part = train_gradients(
-        gathered, master_small, biases, noisy_patches, targets, timesteps, labels, entries
+    own = jnp.stack([timesteps, labels])
+    timesteps, labels = jnp.concatenate(
+        [own, lax.ppermute(own, "shard", [(0, 1), (1, 0)])], axis=1
+    )
+    sides, tail_left, tail_right, grad_patch, grad_head, grad_condition, grad_bias, loss_part = (
+        train_gradients(
+            master_big, master_small, biases, noisy_patches, targets, timesteps, labels, entries
+        )
     )
     images = labels.shape[0]
     strips = D // LANES
@@ -1561,13 +1759,15 @@
     label_lines = jnp.broadcast_to(labels.astype(jnp.float32)[None, :, None], (1, images, LANES))
     lines = jnp.concatenate(
         [
-            jnp.pad(lines_of(grad_condition), ((0, 0), (0, 8 - images), (0, 0))),
-            jnp.pad(label_lines, ((0, 0), (0, 8 - images), (0, 0)), constant_values=-100000.0),
+            lines_of(grad_condition),
+            label_lines,
         ]
     ).reshape(-1, LANES)
     (new_master, new_moment, new_error, right_rows), total, gathered_lines = compress(
         step_rates,
-        grad_big.astype(half_type),
+        sides,
+        tail_left,
+        tail_right,
         error_big,
         factor_right.T,
         moment_big,

time: 343 us -> 302 us (0.88); the launches traced: 338 us -> 301 us
  Pallas kernels: 205 us -> 245 us
  waiting for transfers between devices: 30.4 us -> 0.01 us
  matrix products: 43 us -> 23.2 us
  between operations: 15.6 us -> 1.52 us
  other arithmetic: 23.1 us -> 13.8 us
  local copies, waits for them, and re-layouts: 21 us -> 17.2 us
    all_gather x1 -> x0, waiting for transfers between devices: 30.4 us -> none  [on_pair(): lax.all_gather(master_big.astype(half_type), 'shard', axis=1, tiled=True)]
    dot_general x7 -> x0, matrix products: 26.1 us -> none  [outer_sum(): lax.dot_general(left_side, right_side, (((0,), (0,)), ((), ())), preferre...]
    pallas_call x1, Pallas kernels: 59.8 us -> 83.6 us  [compress(): pl.pallas_call(tail_kernel, out_shape=(pltpu.VMEM((EARLY, rows, BLOCK), j...]
    pallas_call x1, Pallas kernels: 91 us -> 105 us  [run_images(): pl.pallas_call(functools.partial(image_kernel, entries), grid=(images,),...]
    convert_element_type x2 -> x0, other arithmetic: 13.1 us -> none  [the longest x1 13.1 us: on_pair(): master_big.astype(half_type)]
    unnamed x42 -> x18, local copies, waits for them, and re-layouts: 10.4 us -> 0.8 us
  transfers between devices with their start and end apart: 1 -> 1, of which waited for: 1 -> 0; matrix products, arithmetic and copies ran while one was open for 4% -> 5% of each run, Pallas kernels for 0% -> 0%
where the time goes in v4:
time: 302 us; the launch traced here: 301 us
  Pallas kernels  245 us (81%)
  matrix products  23.2 us (8%)
  local copies, waits for them, and re-layouts  17.2 us (6%)
  other arithmetic  13.8 us (5%)
    pallas_call x1, Pallas kernels, run_images(): pl.pallas_call(functools.partial(image_kernel, entries), grid=(images,),...  105 us
    pallas_call x1, Pallas kernels, compress(): pl.pallas_call(tail_kernel, out_shape=(pltpu.VMEM((EARLY, rows, BLOCK), j...  83.6 us
    pallas_call x1, Pallas kernels, compress(): pl.pallas_call(update_kernel, out_shape=(sds(master.shape), sds(moment.sh...  48.6 us
    dot_general x3, matrix products, multiply_trans(): lax.dot_general(left_side, right_side, (((1,), (1,)), ((), ())), preferre...  12.4 us
    dot_general x2, matrix products, multiply(): return jnp.dot(left_side, right_side, preferred_element_type=jnp.float32)  9.65 us
    pallas_call x1, Pallas kernels, update_small(): pl.pallas_call(small_kernel, grid=(steps,), out_shape=(sds(moment.shape),...  7.6 us
  transfers between devices with their start and end apart: 1, of which 0 were waited for; matrix products, arithmetic and copies ran while one was open for 5% of the time, Pallas kernels for 0%

profile of v4, /device:TPU:0, one launch (start us, length us, event | category | flops | bytes accessed | tf_op | source)
XLA Modules:
  0.0 300.9 jit_solution(4514722210489262146)
XLA Ops:
  0.6 0.0 copy-start.6
  0.7 0.0 copy-start.5
  0.7 0.0 slice-start
  0.7 0.0 copy-start.1
  0.7 0.8 pad_add_fusion
  1.5 0.5 collective-permute-start
  2.0 0.8 fusion.48
  2.8 1.3 slice.76
  4.2 1.2 slice_bitcast_fusion.2.head_bias_ref
  5.4 0.6 broadcast_in_dim.23.qkv_bias_ref
  6.0 0.6 broadcast_in_dim.46.output_bias_ref
  6.6 0.6 broadcast_in_dim.48.down_bias_ref
  7.2 0.6 broadcast_in_dim.49.patch_bias_ref
  7.8 2.1 convert.12
  9.8 0.6 slice_bitcast_fusion
  10.4 1.8 reshape.110.targets_ref
  12.3 1.7 reshape.109.patches_ref
  14.0 1.2 slice.83
  15.2 1.9 multiply_sine_fusion.1
  17.1 1.1 pad_maximum_fusion.place_ref
  18.2 0.0 collective-permute-done
  18.2 0.0 copy-done.6
  18.2 0.0 copy-done.5
  18.2 0.1 pad_add_fusion.1
  18.3 0.1 fusion.42
  18.4 1.4 multiply_convert_fusion.1
  19.8 1.9 fusion.16
  21.7 0.0 copy-done.1
  21.7 1.2 multiply_convert_fusion
  22.9 0.0 slice-done
  22.9 7.7 %fusion.4 = f32[8,6144]{1,0:T(8,128)S(1)} fusion(bf16[8,768]{1,0:T(8,128)(2,1)S(1)} %get-tuple-element.111, f32[768,8192]{1,0:T(8,128)} %master_hbm.3, f32[6144]{0:T(1024)S(1)} %slice-done), kind=kOutput, calls=%fused_computation.4 | convolution fusion | flops 75546624 | bytes 9670656 | tf_op jit(solution)/shard_map/dot_general | solution.py:30
  30.6 0.7 copy.29
  31.4 104.8 %images.1 = (bf16[1024,768]{1,0:T(8,128)(2,1)}, bf16[1024,768]{1,0:T(8,128)(2,1)}, bf16[1024,768]{1,0:T(8,128)(2,1)}, bf16[1024,3072]{1,0:T(8,128)(2,1)}, bf16[1...) custom-call(bf16[1024,16]{1,0:T(8,128)(2,1)} %reshape.109.patches_re, ...), custom_call_target="tpu_custom_call" | custom-call | tf_op jit(solution)/shard_map/images/pallas_call | solution.py:1570
  136.2 0.9 convert_reduce_fusion
  137.2 0.7 slice_reduce_fusion
  137.9 0.8 reshape.112
  138.7 0.8 reshape.114
  139.5 0.7 reduce.3
  140.2 0.7 reduce.4
  140.9 0.7 reduce.5
  141.6 1.2 reduce_sum.42
  142.8 0.0 copy-start.4
  142.8 0.0 copy-start.7
  142.8 8.9 %convert_reduce_fusion.2 = (f32[768]{0:T(1024)S(1)}, bf16[8,768]{1,0:T(8,128)(2,1)S(1)}, f32[8,768]{1,0:T(8,128)S(1)}) fusion(f32[8,768]{1,0:T(8,128)S(1)} %get-tuple-element.112, bf16[8,6144]{1,0:T(8,128)(2,1)S(1)} %bitcast.54, f32[768,8192]{1,0:T(8,128)} %master_hbm.3), kind=kOutput, calls=%fused_computation.55 | convolution fusion | flops 75570432 | bytes 9600000 | tf_op jit(solution)/shard_map/dot_general | solution.py:34
  151.8 2.1 convert_reduce_fusion.1
  154.6 0.0 copy-done.4
  154.6 0.0 copy-done.7
  154.6 0.1 concatenate.39
  154.7 0.7 pad.24
  155.4 0.8 fusion.25.tail_right_ref
  156.2 0.8 copy.25.tail_left_ref
  157.0 0.1 broadcast_in_dim.53
  157.1 0.6 maximum_bitcast_fusion.rows_ref
  157.7 0.0 copy-start
  157.7 83.6 %compress.1 = (f32[5,768,512]{2,1,0:T(8,128)S(1)}, bf16[16,8,512]{2,1,0:T(8,128)(2,1)S(1)}, bf16[768,128]{1,0:T(8,128)(2,1)S(1)}, f32[2,16,16,128]{3,2,1,0:T(8,1...) custom-call(bf16[1024,768]{1,0:T(8,128)(2,1)} %get-tuple-element.45.attn_in_hbm, ...), custom_call_target="tpu_custom_call" | custom-call | tf_op jit(solution)/shard_map/compress/pallas_call | solution.py:1068
  241.3 0.0 copy-done
  241.4 0.0 copy-start.2
  241.4 0.0 copy-start.3
  241.4 48.6 %update.1 = (f32[768,8192]{1,0:T(8,128)}, f32[768,8192]{1,0:T(8,128)}, f32[1,768,8192]{2,1,0:T(8,128)}, f32[8,8192]{1,0:T(8,128)}) custom-call(f32[2]{0:T(128)S(1)} %copy-done, f32[16,768,512]{2,1,0:T(8,128)} %get-tuple-element.63.m_hbm, f32[5,768,512]{2,1,0:T(8,128)S(1)} %get-tuple-element.64.v_ref, bf16[16,8,512]{2,1,0:T(8,128)(2,1)S(1)} %get-tuple-element.65.whole_ref, ...), custom_call_target="tpu_custom_call" | custom-call | tf_op jit(solution)/shard_map/update/pallas_call | solution.py:1121
  290.0 1.3 slice.87
  291.3 0.0 copy-done.2
  291.3 0.0 copy-done.3
  291.3 2.0 multiply_subtract_fusion
  293.3 7.6 %update_small.1 = (f32[1032,768]{1,0:T(8,128)}, f32[1032,768]{1,0:T(8,128)}) custom-call(f32[2]{0:T(128)} %rates_ref.3, f32[512,128]{1,0:T(8,128)} %bitcast.60, f32[2,16,56,128]{3,2,1,0:T(8,128)} %get-tuple-element.78.lines_ref, f32[1032,768]{1,0:T(8,128)} %bitcast.52, f32[1032,768]{1,0:T(8,128)} %bitcast.51), custom_call_target="tpu_custom_call" | custom-call | tf_op jit(solution)/shard_map/update_small/pallas_call | solution.py:1192
  (13 shorter events, 0.1 us)
Async XLA Ops:
  0.6 17.5 %copy-start.6 = (s32[4]{0:T(128)S(1)}, s32[4]{0:T(128)}, u32[]{:S(2)}) copy-start(s32[4]{0:T(128)} %param.15) | copy-start | bytes 52
  0.7 17.5 %copy-start.5 = (s32[4]{0:T(128)S(1)}, s32[4]{0:T(128)}, u32[]{:S(2)}) copy-start(s32[4]{0:T(128)} %param.16) | copy-start | bytes 52
  0.7 22.2 %slice-start = ((f32[14608]{0:T(1024)}), f32[6144]{0:T(1024)S(1)}, s32[]{:S(2)}) async-start(f32[14608]{0:T(1024)} %param.23), calls=%async_computation | async-start | bytes 49152 | tf_op jit(solution)/shard_map/concatenate | solution.py:1646
  0.7 21.1 %copy-start.1 = (f32[768,1032]{0,1:T(8,128)S(1)}, f32[768,1032]{0,1:T(8,128)}, u32[]{:S(2)}) copy-start(f32[768,1032]{0,1:T(8,128)} %param.21) | copy-start | bytes 9510916
  1.5 16.7 %collective-permute-start = (s32[2,4]{1,0:T(2,128)S(1)}, s32[2,4]{1,0:T(2,128)S(1)}, u32[]{:S(2)}, u32[]{:S(2)}) collective-permute-start(s32[2,4]{1,0:T(2,128)S(1)} %pad_add_fusion), channel_id=1, source_target_pairs={{0,16},{16,0},{1,17},{17,1},{2,18},{18,2},{3,19},{19,3},{4,20},{20... | collective-permute-start | bytes 104 | tf_op jit(solution)/shard_map/ppermute | solution.py:1736
  142.8 11.7 %copy-start.4 = (f32[1,3072]{1,0:T(1,128)S(1)}, f32[1,3072]{1,0:T(1,128)}, u32[]{:S(2)}) copy-start(f32[1,3072]{1,0:T(1,128)} %get-tuple-element.58) | copy-start | bytes 36868
  142.8 11.8 %copy-start.7 = (f32[1,16]{1,0:T(1,128)S(1)}, f32[1,16]{1,0:T(1,128)}, u32[]{:S(2)}) copy-start(f32[1,16]{1,0:T(1,128)} %get-tuple-element.61) | copy-start | bytes 196
  157.7 83.7 %copy-start = (f32[2]{0:T(128)S(1)}, f32[2]{0:T(128)}, u32[]{:S(2)}) copy-start(f32[2]{0:T(128)} %rates_ref.3) | copy-start | bytes 28
  241.4 49.9 %copy-start.2 = (f32[14608]{0:T(1024)S(1)}, f32[14608]{0:T(1024)}, u32[]{:S(2)}) copy-start(f32[14608]{0:T(1024)} %param.23) | copy-start | bytes 175300
  241.4 49.9 %copy-start.3 = (f32[14608]{0:T(1024)S(1)}, f32[14608]{0:T(1024)}, u32[]{:S(2)}) copy-start(f32[14608]{0:T(1024)} %param.24) | copy-start | bytes 175300

commit v5 on v4

--- a/solution.py
+++ b/solution.py
@@ -3,6 +3,7 @@
 
 import jax
 import jax.numpy as jnp
+import numpy as np
 from jax import lax
 from jax.experimental import pallas as pl
 from jax.experimental.pallas import tpu as pltpu
@@ -82,6 +83,17 @@
     return jnp.concatenate(
         [jnp.sin(across), jnp.cos(across), jnp.sin(downward), jnp.cos(downward)], axis=1
     )
+
+
+def position_constant():
+    quarter = D // 4
+    omega = 1.0 / 10000.0 ** (np.arange(quarter, dtype=np.float32) / np.float32(quarter))
+    cells = np.arange(SEQ)
+    across = (cells % GRID).astype(np.float32)[:, None] * omega[None, :].astype(np.float32)
+    downward = (cells // GRID).astype(np.float32)[:, None] * omega[None, :].astype(np.float32)
+    return np.concatenate(
+        [np.sin(across), np.cos(across), np.sin(downward), np.cos(downward)], axis=1
+    ).astype(np.float32)
 
 
 def split_at(matrix, edges):
@@ -874,10 +886,7 @@
     total_across.start()
 
     def right_block(block, carry):
-        high, low = split_two(m_ref[block])
-        first = multiply(basis_rows[...], high)
-        second = multiply(basis_rows[...], low)
-        both = first + second
+        both = multiply(basis_rows[...], m_ref[block].astype(half_type))
         send_ref[block] = (both[0:RANK] + both[RANK : 2 * RANK]).astype(half_type)
         return carry
 
@@ -1201,6 +1210,7 @@
 
 GROUP = 2 * HEAD_DIM
 CHUNK = 768
+UNROLL = 6
 
 
 def unit_rows(values):
@@ -1234,7 +1244,8 @@
     entries,
     patches_ref,
     targets_ref,
-    both_mods_ref,
+    active_ref,
+    mod_bias_ref,
     place_ref,
     patch_weight_ref,
     head_weight_ref,
@@ -1275,6 +1286,7 @@
     grad_mixed_ref,
     total_ref,
     stage_ref,
+    flat_mods_ref,
     mods_ref,
     got_mods_ref,
     mod_grad_ref,
@@ -1296,6 +1308,7 @@
     all_count = edges[4] // BLOCK
     count = first_count - (2 * first_count - all_count) * shard
     depth = stage_ref.shape[0]
+    loads = first_count - 2 * shard
 
     def load(block):
         slot = lax.rem(block, depth)
@@ -1326,7 +1339,7 @@
             device_id_type=MESH,
         )
 
-    mods_across = mod_copy(both_mods_ref.at[pl.ds(images, images)], got_mods_ref, 0)
+    mods_across = mod_copy(flat_mods_ref, got_mods_ref, 0)
     grads_across = mod_copy(mod_grad_ref, got_grads_ref, 1)
 
     sums = [
@@ -1347,26 +1360,46 @@
             load(block).start()
         barrier, greeted = greet([partner])
         pl.semaphore_wait(barrier, greeted)
-        mods_across.start()
         for total in sums:
             total[...] = jnp.zeros_like(total)
 
         def cast(block, carry):
-            @pl.when(block + 2 < count)
+            @pl.when(block + 2 < loads)
             def _():
                 load(block + 2).start()
 
             load(block).wait()
-            place = shard * first_count + block
-            weight_ref[:, pl.ds(pl.multiple_of(place * BLOCK, BLOCK), BLOCK)] = stage_ref[
-                lax.rem(block, depth)
-            ].astype(half_type)
-            weight_copy(place).start()
+            low_weight = stage_ref[lax.rem(block, depth)].astype(half_type)
+
+            @pl.when(block < count)
+            def _():
+                place = shard * first_count + block
+                weight_ref[:, pl.ds(pl.multiple_of(place * BLOCK, BLOCK), BLOCK)] = low_weight
+                weight_copy(place).start()
+
+            @pl.when(block >= count)
+            def _():
+                span = pl.ds(pl.multiple_of((block - count) * BLOCK, BLOCK), BLOCK)
+                flat_mods_ref[:, span] = (
+                    multiply(active_ref[...], low_weight) + mod_bias_ref[:, span]
+                )
             return carry
 
-        lax.fori_loop(0, count, cast, 0)
-        mods_across.wait_recv()
-        mods_ref[...] = jnp.where(shard == 1, both_mods_ref[0:images], got_mods_ref[...])
+        lax.fori_loop(0, loads, cast, 0)
+
+        @pl.when(shard == 1)
+        def _():
+            mods_across.start()
+            for place in range(8):
+                mods_ref[:, place, :] = flat_mods_ref[0:images, place * D : (place + 1) * D]
+
+        @pl.when(shard == 0)
+        def _():
+            mods_across.wait_recv()
+            for place in range(8):
+                mods_ref[:, place, :] = got_mods_ref[
+                    images : 2 * images, place * D : (place + 1) * D
+                ]
 
     stops = [-(-edge // BLOCK) for edge in edges]
 
@@ -1432,7 +1465,7 @@
         )
         return carry
 
-    lax.fori_loop(0, HEADS // 2, attend, 0)
+    lax.fori_loop(0, HEADS // 2, attend, 0, unroll=UNROLL)
     arrived(1)
     attended = multiply(mixed_ref[...], weight_ref[:, edges[1] : edges[2]]) + output_bias_ref[...]
     attended_ref[...] = attended
@@ -1524,7 +1557,7 @@
         put(2, jnp.where(first_half, value_grads[0], value_grads[1]))
         return carry
 
-    lax.fori_loop(0, HEADS // 2, attend_back, 0)
+    lax.fori_loop(0, HEADS // 2, attend_back, 0, unroll=UNROLL)
     bias_qkv_ref[...] += token_sum(grad_qkv_ref[...].astype(jnp.float32))
     grad_in = multiply_trans(grad_qkv_ref[...], weight_ref[:, : edges[1]])
     unit = unit_start_ref[...]
@@ -1545,16 +1578,19 @@
             return carry
 
         lax.fori_loop(0, count, sent, 0)
-        mods_across.wait_send()
+        @pl.when(shard == 1)
+        def _():
+            mods_across.wait_send()
+
         both_grads_ref[0:images] = mod_grad_ref[...]
         grads_across.wait()
         both_grads_ref[images : 2 * images] = got_grads_ref[...]
 
 
 def run_images(
-    patches, targets, mods, places, patch_weight, head_weight, biases, master, entries
+    patches, targets, active, mod_bias, places, patch_weight, head_weight, biases, master, entries
 ):
-    images = mods.shape[0] // 2
+    images = active.shape[0] // 2
     tokens = images * SEQ
     wide = 4 * D + 2 * FF
 
@@ -1571,13 +1607,13 @@
         functools.partial(image_kernel, entries),
         grid=(images,),
         out_shape=[sds((tokens, width), half_type) for width in saved]
-        + [sds(mods.shape)]
+        + [sds((2 * images, 8, D))]
         + vector,
-        in_specs=[rows(P_DIM), rows(P_DIM), fixed(mods), fixed(places)]
+        in_specs=[rows(P_DIM), rows(P_DIM), fixed(active), fixed(mod_bias), fixed(places)]
         + [fixed(patch_weight), fixed(head_weight)]
         + [fixed(bias) for bias in biases]
         + [pl.BlockSpec(memory_space=pltpu.HBM)],
-        out_specs=[rows(width) for width in saved] + [fixed(mods)] + [fixed(item) for item in vector],
+        out_specs=[rows(width) for width in saved] + [fixed(sds((2 * images, 8, D)))] + [fixed(item) for item in vector],
         scratch_shapes=[
             pltpu.VMEM((D, wide), half_type),
             pltpu.VMEM((SEQ, 3 * D), half_type),
@@ -1591,8 +1627,9 @@
             pltpu.VMEM((SEQ, D), half_type),
             pltpu.VMEM((SEQ, D), jnp.float32),
             pltpu.VMEM((3, D, BLOCK), jnp.float32),
+            pltpu.VMEM((2 * images, 8 * D), jnp.float32),
             pltpu.VMEM((images, 8, D), jnp.float32),
-            pltpu.VMEM((images, 8, D), jnp.float32),
+            pltpu.VMEM((2 * images, 8 * D), jnp.float32),
             pltpu.VMEM((images, 8, D), jnp.float32),
             pltpu.VMEM((images, 8, D), jnp.float32),
             pltpu.SemaphoreType.DMA((3,)),
@@ -1605,7 +1642,7 @@
             collective_id=1, has_side_effects=True, vmem_limit_bytes=60_000_000
         ),
         name="images",
-    )(patches, targets, mods, places, patch_weight, head_weight, *biases, master)
+    )(patches, targets, active, mod_bias, places, patch_weight, head_weight, *biases, master)
 
 
 def train_gradients(master, master_small, biases, noisy_patches, targets, timesteps, labels, entries):
@@ -1643,7 +1680,7 @@
         preferred_element_type=jnp.float32,
     )
     active = jax.nn.silu(condition).astype(half_type)
-    mods = multiply(active.astype(jnp.float32), both_weight) + jnp.concatenate([modulate_bias, final_bias])
+    mod_bias = jnp.concatenate([modulate_bias, final_bias]).reshape(1, 8 * D)
     qkv_bias = jnp.concatenate([query_bias, jnp.zeros_like(query_bias), value_bias])
     (
         attn_in,
@@ -1667,8 +1704,9 @@
     ) = run_images(
         noisy_patches.reshape(-1, P_DIM),
         targets.reshape(-1, P_DIM),
-        mods.reshape(-1, 8, D),
-        position_table(),
+        active,
+        mod_bias,
+        jnp.asarray(position_constant()),
         patch_weight.T.astype(half_type),
         head_weight.T.astype(half_type),
         [item[None] for item in (qkv_bias, output_bias, up_bias, down_bias, patch_bias, head_bias)],

time: 302 us -> 285 us (0.944)
  Pallas kernels: 245 us -> 236 us
  matrix products: 23.2 us -> 16.2 us
    dot_general x2 -> x1, matrix products: 9.65 us -> 1.95 us  [multiply(): return jnp.dot(left_side, right_side, preferred_element_type=jnp.float32)]
    pallas_call x1, Pallas kernels: 105 us -> 98.9 us  [run_images(): pl.pallas_call(functools.partial(image_kernel, entries), grid=(images,),...]
where the time goes in v5:
time: 285 us; the launch traced here: 284 us
  Pallas kernels  236 us (83%)
  local copies, waits for them, and re-layouts  17.8 us (6%)
  matrix products  16.2 us (6%)
  other arithmetic  11.5 us (4%)
    pallas_call x1, Pallas kernels, run_images(): pl.pallas_call(functools.partial(image_kernel, entries), grid=(images,),...  98.9 us
    pallas_call x1, Pallas kernels, compress(): pl.pallas_call(tail_kernel, out_shape=(pltpu.VMEM((EARLY, rows, BLOCK), j...  81.2 us
    pallas_call x1, Pallas kernels, compress(): pl.pallas_call(update_kernel, out_shape=(sds(master.shape), sds(moment.sh...  48.6 us
    dot_general x3, matrix products, multiply_trans(): lax.dot_general(left_side, right_side, (((1,), (1,)), ((), ())), preferre...  12.5 us
    pallas_call x1, Pallas kernels, update_small(): pl.pallas_call(small_kernel, grid=(steps,), out_shape=(sds(moment.shape),...  7.61 us
  transfers between devices with their start and end apart: 1, of which 0 were waited for; matrix products, arithmetic and copies ran while one was open for 5% of the time, Pallas kernels for 0%

profile of v5, /device:TPU:0, one launch (start us, length us, event | category | flops | bytes accessed | tf_op | source)
XLA Modules:
  0.0 283.8 jit_solution(1652545686921038083)
XLA Ops:
  0.6 0.0 copy-start.1
  0.7 0.8 pad_add_fusion
  1.5 0.5 collective-permute-start
  2.0 0.8 fusion.40
  2.8 1.3 concatenate.30
  4.1 1.3 slice.75
  5.5 1.2 slice_bitcast_fusion.2.head_bias_ref
  6.7 0.6 broadcast_in_dim.40.qkv_bias_ref
  7.3 0.6 broadcast_in_dim.41.output_bias_ref
  7.9 0.6 broadcast_in_dim.43.down_bias_ref
  8.5 0.6 broadcast_in_dim.44.patch_bias_ref
  9.1 2.1 convert.12
  11.1 0.6 slice_bitcast_fusion
  11.7 1.8 reshape.79.targets_ref
  13.6 1.7 reshape.78.patches_ref
  15.3 1.2 slice.83
  16.5 0.0 collective-permute-done
  16.5 0.7 pad_add_fusion.1
  17.2 0.1 fusion.37
  17.4 1.4 multiply_convert_fusion.1
  18.8 2.0 fusion.11
  20.7 0.0 copy-done.1
  20.7 1.8 multiply_convert_fusion
  22.5 98.9 %images.1 = (bf16[1024,768]{1,0:T(8,128)(2,1)}, bf16[1024,768]{1,0:T(8,128)(2,1)}, bf16[1024,768]{1,0:T(8,128)(2,1)}, bf16[1024,3072]{1,0:T(8,128)(2,1)}, bf16[1...) custom-call(bf16[1024,16]{1,0:T(8,128)(2,1)} %reshape.78.patches_ref, ...), custom_call_target="tpu_custom_call" | custom-call | tf_op jit(solution)/shard_map/images/pallas_call | solution.py:1606
  121.4 0.9 convert_reduce_fusion
  122.3 0.7 slice_reduce_fusion
  123.1 0.8 reshape.81
  123.9 0.8 reshape.83
  124.7 0.7 reduce.3
  125.4 0.7 reduce.4
  126.1 0.7 reduce.5
  126.8 1.3 reduce_sum.42
  128.0 0.0 copy-start.5
  128.0 0.0 copy-start.6
  128.0 0.0 copy-start.3
  128.0 8.9 %convert_reduce_fusion.2 = (f32[768]{0:T(1024)S(1)}, bf16[8,768]{1,0:T(8,128)(2,1)S(1)}, f32[8,768]{1,0:T(8,128)S(1)}) fusion(f32[8,768]{1,0:T(8,128)S(1)} %get-tuple-element.106, bf16[8,6144]{1,0:T(8,128)(2,1)S(1)} %bitcast.50, f32[768,8192]{1,0:T(8,128)} %master_hbm.3), kind=kOutput, calls=%fused_computation.46 | convolution fusion | flops 75570432 | bytes 9600000 | tf_op jit(solution)/shard_map/dot_general | solution.py:35
  137.0 2.1 convert_reduce_fusion.1
  139.8 0.0 copy-done.5
  139.8 0.0 copy-done.6
  139.8 0.1 concatenate.35
  139.9 0.7 pad.24
  140.6 0.8 fusion.20.tail_right_ref
  141.4 0.0 copy-done.3
  141.4 0.8 copy.26.tail_left_ref
  142.3 0.1 broadcast_in_dim.48
  142.3 0.6 maximum_bitcast_fusion.rows_ref
  142.9 0.0 copy-start
  142.9 81.2 %compress.1 = (f32[5,768,512]{2,1,0:T(8,128)S(1)}, bf16[16,8,512]{2,1,0:T(8,128)(2,1)S(1)}, bf16[768,128]{1,0:T(8,128)(2,1)S(1)}, f32[2,16,16,128]{3,2,1,0:T(8,1...) custom-call(bf16[1024,768]{1,0:T(8,128)(2,1)} %get-tuple-element.45.attn_in_hbm, ...), custom_call_target="tpu_custom_call" | custom-call | tf_op jit(solution)/shard_map/compress/pallas_call | solution.py:1077
  224.2 0.0 copy-done
  224.2 0.0 copy-start.2
  224.2 0.0 copy-start.4
  224.2 48.6 %update.1 = (f32[768,8192]{1,0:T(8,128)}, f32[768,8192]{1,0:T(8,128)}, f32[1,768,8192]{2,1,0:T(8,128)}, f32[8,8192]{1,0:T(8,128)}) custom-call(f32[2]{0:T(128)S(1)} %copy-done, f32[16,768,512]{2,1,0:T(8,128)} %get-tuple-element.63.m_hbm, f32[5,768,512]{2,1,0:T(8,128)S(1)} %get-tuple-element.64.v_ref, bf16[16,8,512]{2,1,0:T(8,128)(2,1)S(1)} %get-tuple-element.65.whole_ref, ...), custom_call_target="tpu_custom_call" | custom-call | tf_op jit(solution)/shard_map/update/pallas_call | solution.py:1130
  272.8 1.3 slice.87
  274.1 0.0 copy-done.2
  274.1 0.0 copy-done.4
  274.1 2.0 multiply_subtract_fusion
  276.1 7.6 %update_small.1 = (f32[1032,768]{1,0:T(8,128)}, f32[1032,768]{1,0:T(8,128)}) custom-call(f32[2]{0:T(128)} %rates_ref.3, f32[512,128]{1,0:T(8,128)} %bitcast.54, f32[2,16,56,128]{3,2,1,0:T(8,128)} %get-tuple-element.78.lines_ref, f32[1032,768]{1,0:T(8,128)} %bitcast.48, f32[1032,768]{1,0:T(8,128)} %bitcast.47), custom_call_target="tpu_custom_call" | custom-call | tf_op jit(solution)/shard_map/update_small/pallas_call | solution.py:1201
  (11 shorter events, 0.1 us)
Async XLA Ops:
  0.6 20.1 %copy-start.1 = (f32[768,1032]{0,1:T(8,128)S(1)}, f32[768,1032]{0,1:T(8,128)}, u32[]{:S(2)}) copy-start(f32[768,1032]{0,1:T(8,128)} %param.22) | copy-start | bytes 9510916
  1.5 15.0 %collective-permute-start = (s32[2,4]{1,0:T(2,128)S(1)}, s32[2,4]{1,0:T(2,128)S(1)}, u32[]{:S(2)}, u32[]{:S(2)}) collective-permute-start(s32[2,4]{1,0:T(2,128)S(1)} %pad_add_fusion), channel_id=1, source_target_pairs={{0,16},{16,0},{1,17},{17,1},{2,18},{18,2},{3,19},{19,3},{4,20},{20... | collective-permute-start | bytes 104 | tf_op jit(solution)/shard_map/ppermute | solution.py:1774
  128.0 11.8 %copy-start.5 = (f32[1,3072]{1,0:T(1,128)S(1)}, f32[1,3072]{1,0:T(1,128)}, u32[]{:S(2)}) copy-start(f32[1,3072]{1,0:T(1,128)} %get-tuple-element.58) | copy-start | bytes 36868
  128.0 11.8 %copy-start.6 = (f32[1,16]{1,0:T(1,128)S(1)}, f32[1,16]{1,0:T(1,128)}, u32[]{:S(2)}) copy-start(f32[1,16]{1,0:T(1,128)} %get-tuple-element.61) | copy-start | bytes 196
  128.0 13.4 %copy-start.3 = (bf16[8,768]{1,0:T(8,128)(2,1)S(1)}, bf16[8,768]{1,0:T(8,128)(2,1)}, u32[]{:S(2)}) copy-start(bf16[8,768]{1,0:T(8,128)(2,1)} %get-tuple-element.105.active_ref) | copy-start | bytes 36868
  142.9 81.2 %copy-start = (f32[2]{0:T(128)S(1)}, f32[2]{0:T(128)}, u32[]{:S(2)}) copy-start(f32[2]{0:T(128)} %rates_ref.3) | copy-start | bytes 28
  224.2 49.9 %copy-start.2 = (f32[14608]{0:T(1024)S(1)}, f32[14608]{0:T(1024)}, u32[]{:S(2)}) copy-start(f32[14608]{0:T(1024)} %param.24) | copy-start | bytes 175300
  224.2 49.9 %copy-start.4 = (f32[14608]{0:T(1024)S(1)}, f32[14608]{0:T(1024)}, u32[]{:S(2)}) copy-start(f32[14608]{0:T(1024)} %param.25) | copy-start | bytes 175300

commit v6 on v5

--- a/solution.py
+++ b/solution.py
@@ -502,7 +502,7 @@
 MESH = pl.DeviceIdType.MESH
 BLOCK = 512
 PIECE = 256
-EARLY = 5
+EARLY = 7
 KERNEL_BYTES = 34_000_000
 EXCHANGE_BYTES = 50_000_000
 RANK = 8
@@ -1265,6 +1265,7 @@
     grad_pre_ref,
     grad_mlp_ref,
     both_grads_ref,
+    grad_active_ref,
     grad_patch_ref,
     grad_head_ref,
     bias_qkv_ref,
@@ -1286,6 +1287,7 @@
     grad_mixed_ref,
     total_ref,
     stage_ref,
+    mod_weight_ref,
     flat_mods_ref,
     mods_ref,
     got_mods_ref,
@@ -1380,6 +1382,7 @@
             @pl.when(block >= count)
             def _():
                 span = pl.ds(pl.multiple_of((block - count) * BLOCK, BLOCK), BLOCK)
+                mod_weight_ref[:, span] = low_weight
                 flat_mods_ref[:, span] = (
                     multiply(active_ref[...], low_weight) + mod_bias_ref[:, span]
                 )
@@ -1585,6 +1588,17 @@
         both_grads_ref[0:images] = mod_grad_ref[...]
         grads_across.wait()
         both_grads_ref[images : 2 * images] = got_grads_ref[...]
+        grad_active_ref[...] = jnp.zeros_like(grad_active_ref)
+
+        @pl.when(shard == 1)
+        def _():
+            for place in range(8):
+                part = jnp.concatenate(
+                    [mod_grad_ref[:, place, :], got_grads_ref[:, place, :]], axis=0
+                ).astype(half_type)
+                grad_active_ref[...] += multiply_trans(
+                    part, mod_weight_ref[:, place * D : (place + 1) * D]
+                )
 
 
 def run_images(
@@ -1607,13 +1621,13 @@
         functools.partial(image_kernel, entries),
         grid=(images,),
         out_shape=[sds((tokens, width), half_type) for width in saved]
-        + [sds((2 * images, 8, D))]
+        + [sds((2 * images, 8, D)), sds((2 * images, D))]
         + vector,
         in_specs=[rows(P_DIM), rows(P_DIM), fixed(active), fixed(mod_bias), fixed(places)]
         + [fixed(patch_weight), fixed(head_weight)]
         + [fixed(bias) for bias in biases]
         + [pl.BlockSpec(memory_space=pltpu.HBM)],
-        out_specs=[rows(width) for width in saved] + [fixed(sds((2 * images, 8, D)))] + [fixed(item) for item in vector],
+        out_specs=[rows(width) for width in saved] + [fixed(sds((2 * images, 8, D))), fixed(sds((2 * images, D)))] + [fixed(item) for item in vector],
         scratch_shapes=[
             pltpu.VMEM((D, wide), half_type),
             pltpu.VMEM((SEQ, 3 * D), half_type),
@@ -1627,6 +1641,7 @@
             pltpu.VMEM((SEQ, D), half_type),
             pltpu.VMEM((SEQ, D), jnp.float32),
             pltpu.VMEM((3, D, BLOCK), jnp.float32),
+            pltpu.VMEM((D, 8 * D), half_type),
             pltpu.VMEM((2 * images, 8 * D), jnp.float32),
             pltpu.VMEM((images, 8, D), jnp.float32),
             pltpu.VMEM((2 * images, 8 * D), jnp.float32),
@@ -1639,7 +1654,7 @@
             pltpu.SemaphoreType.DMA((2,)),
         ],
         compiler_params=pltpu.CompilerParams(
-            collective_id=1, has_side_effects=True, vmem_limit_bytes=60_000_000
+            collective_id=1, has_side_effects=True, vmem_limit_bytes=64_000_000
         ),
         name="images",
     )(patches, targets, active, mod_bias, places, patch_weight, head_weight, *biases, master)
@@ -1648,9 +1663,8 @@
 def train_gradients(master, master_small, biases, noisy_patches, targets, timesteps, labels, entries):
     owner = lax.axis_index("shard") == 1
     last = master.shape[1]
-    first_edge = last - 9 * D - FREQ
-    both_weight, embed_second, embed_first = split_at(
-        master, [first_edge, last - D - FREQ, last - FREQ, last]
+    embed_second, embed_first = split_at(
+        master, [last - D - FREQ, last - FREQ, last]
     )
     patch_weight, class_table, head_weight = split_small(master_small)
     (
@@ -1692,6 +1706,7 @@
         grad_pre,
         grad_mlp,
         mod_grads,
+        grad_active,
         grad_patch,
         grad_head,
         bias_qkv,
@@ -1715,7 +1730,6 @@
     )
     grad_mods = mod_grads.reshape(-1, 8 * D).astype(half_type)
     bias_mods = column_sums(grad_mods)
-    grad_active = multiply_trans(grad_mods.astype(jnp.float32), both_weight)
     grad_condition = slope(jax.nn.silu, condition, grad_active)
     grad_embed = grad_condition.astype(half_type)
     grad_embed_hidden = multiply_trans(grad_embed.astype(jnp.float32), embed_second)

time: 285 us -> 273 us (0.958)
  matrix products: 16.2 us -> 7.23 us
    dot_general x3 -> x2, matrix products: 12.5 us -> 3.51 us  [multiply_trans(): lax.dot_general(left_side, right_side, (((1,), (1,)), ((), ())), preferre...]
where the time goes in v6:
time: 273 us; the launch traced here: 272 us
  Pallas kernels  235 us (86%)
  local copies, waits for them, and re-layouts  15.6 us (6%)
  other arithmetic  11.7 us (4%)
  matrix products  7.23 us (3%)
    pallas_call x1, Pallas kernels, run_images(): pl.pallas_call(functools.partial(image_kernel, entries), grid=(images,),...  99.1 us
    pallas_call x1, Pallas kernels, compress(): pl.pallas_call(tail_kernel, out_shape=(pltpu.VMEM((EARLY, rows, BLOCK), j...  81.4 us
    pallas_call x1, Pallas kernels, compress(): pl.pallas_call(update_kernel, out_shape=(sds(master.shape), sds(moment.sh...  47.2 us
    pallas_call x1, Pallas kernels, update_small(): pl.pallas_call(small_kernel, grid=(steps,), out_shape=(sds(moment.shape),...  7.6 us
  transfers between devices with their start and end apart: 1, of which 0 were waited for; matrix products, arithmetic and copies ran while one was open for 5% of the time, Pallas kernels for 0%

profile of v6, /device:TPU:0, one launch (start us, length us, event | category | flops | bytes accessed | tf_op | source)
XLA Modules:
  0.0 271.8 jit_solution(14115477208234474572)
XLA Ops:
  0.6 0.0 copy-start.9
  0.7 0.0 copy-start.8
  0.7 0.0 copy-start.4
  0.7 0.0 copy-start.6
  0.7 0.0 copy-start
  0.7 0.7 pad_add_fusion
  1.4 0.5 collective-permute-start
  1.9 0.8 fusion.39
  2.7 1.3 concatenate.30
  4.1 1.3 slice.72
  5.4 1.2 slice_bitcast_fusion.2.head_bias_ref
  6.6 0.6 broadcast_in_dim.40.qkv_bias_ref
  7.2 0.6 broadcast_in_dim.41.output_bias_ref
  7.8 0.6 broadcast_in_dim.43.down_bias_ref
  8.4 0.6 broadcast_in_dim.44.patch_bias_ref
  9.0 2.1 convert.12
  11.0 0.0 copy-start.1
  11.0 0.6 slice_bitcast_fusion
  11.7 0.0 copy-done.4
  11.7 1.0 reshape.79.targets_ref
  12.7 0.0 copy-done.6
  12.7 0.9 reshape.78.patches_ref
  13.6 0.0 copy-done
  13.6 0.7 slice.79
  14.3 0.0 collective-permute-done
  14.3 0.0 copy-done.9
  14.3 0.0 copy-done.8
  14.3 0.1 pad_add_fusion.1
  14.3 0.1 fusion.33
  14.5 1.4 multiply_convert_fusion.1
  15.9 2.0 fusion.9
  17.8 0.0 copy-done.1
  17.8 1.8 multiply_convert_fusion
  19.6 99.1 %images.1 = (bf16[1024,768]{1,0:T(8,128)(2,1)}, bf16[1024,768]{1,0:T(8,128)(2,1)}, bf16[1024,768]{1,0:T(8,128)(2,1)}, bf16[1024,3072]{1,0:T(8,128)(2,1)}, bf16[1...) custom-call(bf16[1024,16]{1,0:T(8,128)(2,1)} %reshape.78.patches_ref, ...), custom_call_target="tpu_custom_call" | custom-call | tf_op jit(solution)/shard_map/images/pallas_call | solution.py:1620
  118.7 0.0 copy-start.7
  118.7 0.0 copy-start.10
  118.7 0.0 copy-start.3
  118.8 1.0 convert_reduce_fusion
  119.7 0.7 slice_reduce_fusion
  120.4 0.8 reshape.81
  121.3 0.8 reshape.83
  122.1 0.7 reduce.3
  122.8 0.7 reduce.4
  123.5 0.7 reduce.5
  124.2 1.3 reduce_sum.42
  125.5 0.8 convert_reduce_fusion.2
  126.2 2.1 convert_reduce_fusion.1
  129.0 0.0 copy-done.7
  129.1 0.0 copy-done.10
  129.1 0.1 concatenate.35
  129.2 0.7 pad.24
  129.9 0.0 copy-done.3
  129.9 0.8 copy.26.tail_left_ref
  130.7 0.8 fusion.18.tail_right_ref
  131.5 0.1 broadcast_in_dim.48
  131.6 0.6 maximum_bitcast_fusion.rows_ref
  132.2 81.4 %compress.1 = (f32[7,768,512]{2,1,0:T(8,128)S(1)}, bf16[16,8,512]{2,1,0:T(8,128)(2,1)S(1)}, bf16[768,128]{1,0:T(8,128)(2,1)S(1)}, f32[2,16,16,128]{3,2,1,0:T(8,1...) custom-call(bf16[1024,768]{1,0:T(8,128)(2,1)} %get-tuple-element.46.attn_in_hbm, ...), custom_call_target="tpu_custom_call" | custom-call | tf_op jit(solution)/shard_map/compress/pallas_call | solution.py:1077
  213.6 0.0 copy-start.2
  213.6 0.0 copy-start.5
  213.6 47.2 %update.1 = (f32[768,8192]{1,0:T(8,128)}, f32[768,8192]{1,0:T(8,128)}, f32[1,768,8192]{2,1,0:T(8,128)}, f32[8,8192]{1,0:T(8,128)}) custom-call(f32[2]{0:T(128)S(1)} %copy-done, f32[16,768,512]{2,1,0:T(8,128)} %get-tuple-element.65.m_hbm, f32[7,768,512]{2,1,0:T(8,128)S(1)} %get-tuple-element.66.v_ref, bf16[16,8,512]{2,1,0:T(8,128)(2,1)S(1)} %get-tuple-element.67.whole_ref, ...), custom_call_target="tpu_custom_call" | custom-call | tf_op jit(solution)/shard_map/update/pallas_call | solution.py:1130
  260.8 1.3 slice.83
  262.1 0.0 copy-done.2
  262.1 2.2 multiply_subtract_fusion
  264.2 7.6 %update_small.1 = (f32[1032,768]{1,0:T(8,128)}, f32[1032,768]{1,0:T(8,128)}) custom-call(f32[2]{0:T(128)} %rates_ref.3, f32[512,128]{1,0:T(8,128)} %bitcast.52, f32[2,16,56,128]{3,2,1,0:T(8,128)} %get-tuple-element.80.lines_ref, f32[1032,768]{1,0:T(8,128)} %bitcast.48, f32[1032,768]{1,0:T(8,128)} %bitcast.47), custom_call_target="tpu_custom_call" | custom-call | tf_op jit(solution)/shard_map/update_small/pallas_call | solution.py:1201
  (12 shorter events, 0.1 us)
Async XLA Ops:
  0.6 13.6 %copy-start.9 = (s32[4]{0:T(128)S(1)}, s32[4]{0:T(128)}, u32[]{:S(2)}) copy-start(s32[4]{0:T(128)} %param.16) | copy-start | bytes 52
  0.7 13.6 %copy-start.8 = (s32[4]{0:T(128)S(1)}, s32[4]{0:T(128)}, u32[]{:S(2)}) copy-start(s32[4]{0:T(128)} %param.17) | copy-start | bytes 52
  0.7 11.0 %copy-start.4 = (f32[4,4096]{1,0:T(4,128)S(1)}, f32[4,4096]{1,0:T(4,128)}, u32[]{:S(2)}) copy-start(f32[4,4096]{1,0:T(4,128)} %param.15) | copy-start | bytes 196612
  0.7 12.0 %copy-start.6 = (bf16[4,4096]{1,0:T(4,128)(2,1)S(1)}, bf16[4,4096]{1,0:T(4,128)(2,1)}, u32[]{:S(2)}) copy-start(bf16[4,4096]{1,0:T(4,128)(2,1)} %param.14) | copy-start | bytes 98308
  0.7 12.9 %copy-start = (f32[2]{0:T(128)S(1)}, f32[2]{0:T(128)}, u32[]{:S(2)}) copy-start(f32[2]{0:T(128)} %rates_ref.3) | copy-start | bytes 28
  1.4 12.8 %collective-permute-start = (s32[2,4]{1,0:T(2,128)S(1)}, s32[2,4]{1,0:T(2,128)S(1)}, u32[]{:S(2)}, u32[]{:S(2)}) collective-permute-start(s32[2,4]{1,0:T(2,128)S(1)} %pad_add_fusion), channel_id=1, source_target_pairs={{0,16},{16,0},{1,17},{17,1},{2,18},{18,2},{3,19},{19,3},{4,20},{20... | collective-permute-start | bytes 104 | tf_op jit(solution)/shard_map/ppermute | solution.py:1788
  11.0 6.8 %copy-start.1 = (f32[768,1032]{0,1:T(8,128)S(1)}, f32[768,1032]{0,1:T(8,128)}, u32[]{:S(2)}) copy-start(f32[768,1032]{0,1:T(8,128)} %param.22) | copy-start | bytes 9510916
  118.7 10.3 %copy-start.7 = (f32[1,3072]{1,0:T(1,128)S(1)}, f32[1,3072]{1,0:T(1,128)}, u32[]{:S(2)}) copy-start(f32[1,3072]{1,0:T(1,128)} %get-tuple-element.60) | copy-start | bytes 36868
  118.7 10.3 %copy-start.10 = (f32[1,16]{1,0:T(1,128)S(1)}, f32[1,16]{1,0:T(1,128)}, u32[]{:S(2)}) copy-start(f32[1,16]{1,0:T(1,128)} %get-tuple-element.63) | copy-start | bytes 196
  118.7 11.2 %copy-start.3 = (bf16[8,768]{1,0:T(8,128)(2,1)S(1)}, bf16[8,768]{1,0:T(8,128)(2,1)}, u32[]{:S(2)}) copy-start(bf16[8,768]{1,0:T(8,128)(2,1)} %get-tuple-element.108.active_ref) | copy-start | bytes 36868
  213.6 48.5 %copy-start.2 = (f32[14608]{0:T(1024)S(1)}, f32[14608]{0:T(1024)}, u32[]{:S(2)}) copy-start(f32[14608]{0:T(1024)} %param.24) | copy-start | bytes 175300
  213.6 48.5 %copy-start.5 = (f32[14608]{0:T(1024)S(1)}, f32[14608]{0:T(1024)}, u32[]{:S(2)}) copy-start(f32[14608]{0:T(1024)} %param.25) | copy-start | bytes 175300

commit v7 on v6

--- a/solution.py
+++ b/solution.py
@@ -1168,12 +1168,10 @@
     labels = piece(strips)[:, 0:1]
     place = lax.broadcasted_iota(jnp.int32, (images, height), 1) + (step * height - P_DIM)
     chosen = (place.astype(jnp.float32) == labels).astype(half_type)
-    for strip in range(strips):
-        span = slice(strip * LANES, (strip + 1) * LANES)
-        high, low = split_two(piece(strip))
-        new_moment_ref[:, span] = (
-            momentum_decay * moment_ref[:, span] + outer_sum(chosen, high) + outer_sum(chosen, low)
-        )
+    high, low = split_two(jnp.concatenate([piece(strip) for strip in range(strips)], axis=1))
+    new_moment_ref[...] = momentum_decay * moment_ref[...] + outer_sum(
+        jnp.concatenate([chosen, chosen], axis=0), jnp.concatenate([high, low], axis=0)
+    )
 
     def add(first, base):
         for strip in range(strips):

time: 273 us -> 273 us (level)
  no operation moved by 1% of the time
where the time goes in v7:
time: 273 us; the launch traced here: 272 us
  Pallas kernels  235 us (86%)
  local copies, waits for them, and re-layouts  15.6 us (6%)
  other arithmetic  11.7 us (4%)
  matrix products  7.23 us (3%)
    pallas_call x1, Pallas kernels, run_images(): pl.pallas_call(functools.partial(image_kernel, entries), grid=(images,),...  99.1 us
    pallas_call x1, Pallas kernels, compress(): pl.pallas_call(tail_kernel, out_shape=(pltpu.VMEM((EARLY, rows, BLOCK), j...  81.4 us
    pallas_call x1, Pallas kernels, compress(): pl.pallas_call(update_kernel, out_shape=(sds(master.shape), sds(moment.sh...  47.2 us
    pallas_call x1, Pallas kernels, update_small(): pl.pallas_call(small_kernel, grid=(steps,), out_shape=(sds(moment.shape),...  7.35 us
  transfers between devices with their start and end apart: 1, of which 0 were waited for; matrix products, arithmetic and copies ran while one was open for 5% of the time, Pallas kernels for 0%

profile of v7, /device:TPU:0, one launch (start us, length us, event | category | flops | bytes accessed | tf_op | source)
XLA Modules:
  0.0 271.6 jit_solution(4131034142339693283)
XLA Ops:
  0.6 0.0 copy-start.9
  0.7 0.0 copy-start.8
  0.7 0.0 copy-start.4
  0.7 0.0 copy-start.6
  0.7 0.0 copy-start
  0.7 0.7 pad_add_fusion
  1.4 0.5 collective-permute-start
  1.9 0.8 fusion.39
  2.7 1.3 concatenate.30
  4.1 1.3 slice.72
  5.4 1.2 slice_bitcast_fusion.2.head_bias_ref
  6.6 0.6 broadcast_in_dim.40.qkv_bias_ref
  7.2 0.6 broadcast_in_dim.41.output_bias_ref
  7.8 0.6 broadcast_in_dim.43.down_bias_ref
  8.4 0.6 broadcast_in_dim.44.patch_bias_ref
  9.0 2.1 convert.12
  11.0 0.0 copy-start.1
  11.0 0.6 slice_bitcast_fusion
  11.7 0.0 copy-done.4
  11.7 1.0 reshape.79.targets_ref
  12.7 0.0 copy-done.6
  12.7 0.9 reshape.78.patches_ref
  13.6 0.0 copy-done
  13.6 0.7 slice.79
  14.3 0.0 collective-permute-done
  14.3 0.0 copy-done.9
  14.3 0.0 copy-done.8
  14.3 0.1 pad_add_fusion.1
  14.3 0.1 fusion.33
  14.5 1.4 multiply_convert_fusion.1
  15.9 2.0 fusion.9
  17.8 0.0 copy-done.1
  17.8 1.8 multiply_convert_fusion
  19.6 99.1 %images.1 = (bf16[1024,768]{1,0:T(8,128)(2,1)}, bf16[1024,768]{1,0:T(8,128)(2,1)}, bf16[1024,768]{1,0:T(8,128)(2,1)}, bf16[1024,3072]{1,0:T(8,128)(2,1)}, bf16[1...) custom-call(bf16[1024,16]{1,0:T(8,128)(2,1)} %reshape.78.patches_ref, ...), custom_call_target="tpu_custom_call" | custom-call | tf_op jit(solution)/shard_map/images/pallas_call | solution.py:1618
  118.7 0.0 copy-start.7
  118.7 0.0 copy-start.10
  118.7 0.0 copy-start.3
  118.8 1.0 convert_reduce_fusion
  119.7 0.7 slice_reduce_fusion
  120.4 0.8 reshape.81
  121.3 0.8 reshape.83
  122.1 0.7 reduce.3
  122.8 0.7 reduce.4
  123.5 0.7 reduce.5
  124.2 1.3 reduce_sum.42
  125.5 0.8 convert_reduce_fusion.2
  126.2 2.1 convert_reduce_fusion.1
  129.0 0.0 copy-done.7
  129.1 0.0 copy-done.10
  129.1 0.1 concatenate.35
  129.2 0.7 pad.24
  129.9 0.0 copy-done.3
  129.9 0.8 copy.26.tail_left_ref
  130.7 0.8 fusion.18.tail_right_ref
  131.5 0.1 broadcast_in_dim.48
  131.6 0.6 maximum_bitcast_fusion.rows_ref
  132.2 81.4 %compress.1 = (f32[7,768,512]{2,1,0:T(8,128)S(1)}, bf16[16,8,512]{2,1,0:T(8,128)(2,1)S(1)}, bf16[768,128]{1,0:T(8,128)(2,1)S(1)}, f32[2,16,16,128]{3,2,1,0:T(8,1...) custom-call(bf16[1024,768]{1,0:T(8,128)(2,1)} %get-tuple-element.46.attn_in_hbm, ...), custom_call_target="tpu_custom_call" | custom-call | tf_op jit(solution)/shard_map/compress/pallas_call | solution.py:1077
  213.6 0.0 copy-start.2
  213.6 0.0 copy-start.5
  213.6 47.2 %update.1 = (f32[768,8192]{1,0:T(8,128)}, f32[768,8192]{1,0:T(8,128)}, f32[1,768,8192]{2,1,0:T(8,128)}, f32[8,8192]{1,0:T(8,128)}) custom-call(f32[2]{0:T(128)S(1)} %copy-done, f32[16,768,512]{2,1,0:T(8,128)} %get-tuple-element.65.m_hbm, f32[7,768,512]{2,1,0:T(8,128)S(1)} %get-tuple-element.66.v_ref, bf16[16,8,512]{2,1,0:T(8,128)(2,1)S(1)} %get-tuple-element.67.whole_ref, ...), custom_call_target="tpu_custom_call" | custom-call | tf_op jit(solution)/shard_map/update/pallas_call | solution.py:1130
  260.8 1.3 slice.83
  262.1 0.0 copy-done.5
  262.1 2.2 multiply_subtract_fusion
  264.2 7.4 %update_small.1 = (f32[1032,768]{1,0:T(8,128)}, f32[1032,768]{1,0:T(8,128)}) custom-call(f32[2]{0:T(128)} %rates_ref.3, f32[512,128]{1,0:T(8,128)} %bitcast.52, f32[2,16,56,128]{3,2,1,0:T(8,128)} %get-tuple-element.80.lines_ref, f32[1032,768]{1,0:T(8,128)} %bitcast.48, f32[1032,768]{1,0:T(8,128)} %bitcast.47), custom_call_target="tpu_custom_call" | custom-call | tf_op jit(solution)/shard_map/update_small/pallas_call | solution.py:1199
  (12 shorter events, 0.1 us)
Async XLA Ops:
  0.6 13.6 %copy-start.9 = (s32[4]{0:T(128)S(1)}, s32[4]{0:T(128)}, u32[]{:S(2)}) copy-start(s32[4]{0:T(128)} %param.16) | copy-start | bytes 52
  0.7 13.6 %copy-start.8 = (s32[4]{0:T(128)S(1)}, s32[4]{0:T(128)}, u32[]{:S(2)}) copy-start(s32[4]{0:T(128)} %param.17) | copy-start | bytes 52
  0.7 11.0 %copy-start.4 = (f32[4,4096]{1,0:T(4,128)S(1)}, f32[4,4096]{1,0:T(4,128)}, u32[]{:S(2)}) copy-start(f32[4,4096]{1,0:T(4,128)} %param.15) | copy-start | bytes 196612
  0.7 12.0 %copy-start.6 = (bf16[4,4096]{1,0:T(4,128)(2,1)S(1)}, bf16[4,4096]{1,0:T(4,128)(2,1)}, u32[]{:S(2)}) copy-start(bf16[4,4096]{1,0:T(4,128)(2,1)} %param.14) | copy-start | bytes 98308
  0.7 12.9 %copy-start = (f32[2]{0:T(128)S(1)}, f32[2]{0:T(128)}, u32[]{:S(2)}) copy-start(f32[2]{0:T(128)} %rates_ref.3) | copy-start | bytes 28
  1.4 12.8 %collective-permute-start = (s32[2,4]{1,0:T(2,128)S(1)}, s32[2,4]{1,0:T(2,128)S(1)}, u32[]{:S(2)}, u32[]{:S(2)}) collective-permute-start(s32[2,4]{1,0:T(2,128)S(1)} %pad_add_fusion), channel_id=1, source_target_pairs={{0,16},{16,0},{1,17},{17,1},{2,18},{18,2},{3,19},{19,3},{4,20},{20... | collective-permute-start | bytes 104 | tf_op jit(solution)/shard_map/ppermute | solution.py:1786
  11.0 6.8 %copy-start.1 = (f32[768,1032]{0,1:T(8,128)S(1)}, f32[768,1032]{0,1:T(8,128)}, u32[]{:S(2)}) copy-start(f32[768,1032]{0,1:T(8,128)} %param.22) | copy-start | bytes 9510916
  118.7 10.3 %copy-start.7 = (f32[1,3072]{1,0:T(1,128)S(1)}, f32[1,3072]{1,0:T(1,128)}, u32[]{:S(2)}) copy-start(f32[1,3072]{1,0:T(1,128)} %get-tuple-element.60) | copy-start | bytes 36868
  118.7 10.3 %copy-start.10 = (f32[1,16]{1,0:T(1,128)S(1)}, f32[1,16]{1,0:T(1,128)}, u32[]{:S(2)}) copy-start(f32[1,16]{1,0:T(1,128)} %get-tuple-element.63) | copy-start | bytes 196
  118.7 11.2 %copy-start.3 = (bf16[8,768]{1,0:T(8,128)(2,1)S(1)}, bf16[8,768]{1,0:T(8,128)(2,1)}, u32[]{:S(2)}) copy-start(bf16[8,768]{1,0:T(8,128)(2,1)} %get-tuple-element.108.active_ref) | copy-start | bytes 36868
  213.6 48.5 %copy-start.2 = (f32[14608]{0:T(1024)S(1)}, f32[14608]{0:T(1024)}, u32[]{:S(2)}) copy-start(f32[14608]{0:T(1024)} %param.24) | copy-start | bytes 175300
  213.6 48.5 %copy-start.5 = (f32[14608]{0:T(1024)S(1)}, f32[14608]{0:T(1024)}, u32[]{:S(2)}) copy-start(f32[14608]{0:T(1024)} %param.25) | copy-start | bytes 175300
